TPU v7x, 32 devices: a whole 2x2x4 slice. The times are simulated.
32 devices in a mesh: aux: 8 (over z, x), pair: 4 (over y, core).
Axes of the slice: x: 2, y: 2, z: 4, core: 2. Of those that a mesh axis runs over, the one named last changes fastest.
Arguments:
- three_center: float32 [8192, 4, 384], P('aux', 'pair'), may hold values from -0.875 to 0.875
- occ_energy: float32 [4], P('pair'), may hold values from -1.5 to -0.3
- vir_energy: float32 [384], replicated, may hold values from 0.2 to 3
- pair_mask: int32 [4, 4], replicated, may hold values from 0 to 1, as said below
Outputs:
- gamma_aux: float32 [8192, 4, 384], P('aux', 'pair')
Inputs may be any that keep to these rules, and one draw needn't show every extreme that they name: pair_mask is symmetric and holds 1 on its diagonal.
All inputs are finite; a program needn't handle non-finite values.
Results may differ from a plain program's by a relative error of at most 0.000071.
Values sent between devices are 32-bit elements; how exact they have to be, the bound alone decides.
No kernel may reach another device: no remote copies, remote signals or barrier semaphores. Data moves between devices by JAX's collectives and lax.ppermute only.
A program may use at most 64 MiB of HBM per device.

v0:
```python
import functools

import jax
import jax.numpy as jnp
from jax import lax
from jax.experimental import pallas as pl
from jax.experimental.pallas import tpu as pltpu
from jax.sharding import PartitionSpec as P

AXES = ("aux", "pair")
precision = lax.Precision.HIGH


def across(value, aux_flip, pair_flip):
    aux_count, pair_count = lax.axis_size("aux"), lax.axis_size("pair")
    moves = [
        (a * pair_count + p, (a ^ aux_flip) * pair_count + (p ^ pair_flip))
        for a in range(aux_count)
        for p in range(pair_count)
    ]
    return lax.ppermute(value, AXES, moves)


def pick(pieces, index):
    return lax.dynamic_index_in_dim(pieces, index, 0, keepdims=False)


def tn(left, right):
    return lax.dot_general(
        left, right, (((0,), (0,)), ((), ())), precision=precision,
        preferred_element_type=jnp.float32)


def nt(left, right):
    return lax.dot_general(
        left, right, (((1,), (1,)), ((), ())), precision=precision,
        preferred_element_type=jnp.float32)


def scatter_sum(value, flips, index):
    members = len(flips)
    pieces = value.reshape((members, value.shape[0] // members) + value.shape[1:])
    total = pick(pieces, index)
    for step in range(1, members):
        total = total + across(pick(pieces, index ^ step), *flips[step])
    return total


def gather(piece, flips, index):
    members = len(flips)
    whole = jnp.zeros((members,) + piece.shape, piece.dtype)
    whole = lax.dynamic_update_index_in_dim(whole, piece, index, 0)
    for step in range(1, members):
        whole = lax.dynamic_update_index_in_dim(
            whole, across(piece, *flips[step]), index ^ step, 0)
    return whole.reshape((members * piece.shape[0],) + piece.shape[1:])


def aux_groups(aux_count):
    bits = aux_count.bit_length() - 1
    low, groups = 1, []
    while low < bits:
        width = min(2, bits - low)
        groups.append((low, width))
        low += width
    return groups


def general_path(three_center, occ_energy, vir_energy, pair_mask):
    rows, occ_count, virt = three_center.shape
    aux_count = lax.axis_size("aux")
    aux, pair = lax.axis_index("aux"), lax.axis_index("pair")
    side, lane = pair // 2, pair % 2
    half = rows // 2
    own = three_center.reshape(rows, virt)
    pieces = own.reshape(2, half, virt)
    occ_side = jnp.stack([occ_energy[0], across(occ_energy, 0, 1)[0]])
    occ_side = jnp.where(lane == 0, occ_side, occ_side[::-1])
    occ_other = across(occ_side, 0, 2)
    occ_low = jnp.where(side == 0, occ_side, occ_other)
    occ_high = jnp.where(side == 0, occ_other, occ_side)
    mask = pair_mask.astype(jnp.float32)

    facing_near = across(pick(pieces, side ^ 1), 0, 2)
    twin = across(own, 0, 1)
    facing_far = across(pick(pieces, side), 0, 2)

    z_groups = aux_groups(aux_count)

    def z_scatter(value):
        start = jnp.int32(0)
        for low, width in z_groups:
            members = 1 << width
            index = (aux >> low) & (members - 1)
            value = scatter_sum(value, [(s << low, 0) for s in range(members)], index)
            start = start + index * value.shape[0]
        return value, start

    def z_gather(value):
        for low, width in reversed(z_groups):
            members = 1 << width
            index = (aux >> low) & (members - 1)
            value = gather(value, [(s << low, 0) for s in range(members)], index)
        return value

    first = jnp.where(lane == 0, own, twin)
    second = jnp.where(lane == 0, twin, own)
    near = virt // 2
    left = lax.dynamic_slice_in_dim(first, lane * near, near, 1)
    side_ints = jnp.concatenate([tn(own, own), tn(left, second)], 0)
    x_flips = [(0, 0), (1, 0)]
    x_index = aux & 1
    part = scatter_sum(side_ints, x_flips, x_index)
    start = x_index * part.shape[0]
    part, more = z_scatter(part)
    start = start + more
    row = start + jnp.arange(part.shape[0])
    in_own = row < virt
    a_index = jnp.where(in_own, row, row - virt + lane * near)
    occ_i = jnp.where(in_own, pick(occ_side, lane), occ_side[0])
    occ_j = jnp.where(in_own, pick(occ_side, lane), occ_side[1])
    weight = jnp.where(
        in_own, mask[pair, pair], mask[2 * side, 2 * side + 1])
    row_term = jnp.take(vir_energy, a_index) - occ_i - occ_j
    part = weight[:, None] * part / (row_term[:, None] + vir_energy[None, :])
    side_amps = gather(z_gather(part), x_flips, x_index)
    own_amps = side_amps[:virt]
    mixed = side_amps[virt:]
    mixed_twin = across(mixed, 0, 1)
    mixed_amps = jnp.concatenate(
        [jnp.where(lane == 0, mixed, mixed_twin), jnp.where(lane == 0, mixed_twin, mixed)], 0)

    here = pick(pieces, side)
    twin_here = pick(twin.reshape(2, half, virt), side)
    facing_twin = across(facing_near, 0, 1)
    low = jnp.where(side == 0, here, facing_near)
    high = jnp.where(side == 0, facing_near, here)
    high_twin = jnp.where(side == 0, facing_twin, twin_here)
    high_first = jnp.where(lane == 0, high, high_twin)
    high_second = jnp.where(lane == 0, high_twin, high)
    cross_ints = jnp.concatenate([tn(low, high_first), tn(low, high_second)], 0)
    q_flips = [(0, 0), (1, 0), (0, 2), (1, 2)]
    q_index = (aux & 1) + 2 * side
    part = scatter_sum(cross_ints, q_flips, q_index)
    start = q_index * part.shape[0]
    part, more = z_scatter(part)
    start = start + more
    row = start + jnp.arange(part.shape[0])
    block = row // virt
    a_index = row % virt
    weight = jnp.where(block == 0, mask[lane, 2], mask[lane, 3])
    row_term = jnp.take(vir_energy, a_index) - pick(occ_low, lane) - jnp.where(
        block == 0, occ_high[0], occ_high[1])
    part = weight[:, None] * part / (row_term[:, None] + vir_energy[None, :])
    cross_amps = gather(z_gather(part), q_flips, q_index)

    cross_blocks = cross_amps.reshape(2, virt, virt)
    swapped = across(pick(cross_blocks, lane ^ 1), 0, 1)
    kept = pick(cross_blocks, lane)
    facing_far_twin = across(facing_far, 0, 1)
    zero_near = jnp.where(side == 0, facing_near, facing_far)
    zero_far = jnp.where(side == 0, facing_far, facing_near)
    facing = jnp.concatenate([zero_near, zero_far], 0)
    twin_near = jnp.where(side == 0, facing_twin, facing_far_twin)
    twin_far = jnp.where(side == 0, facing_far_twin, facing_twin)
    facing_t = jnp.concatenate([twin_near, twin_far], 0)
    f_first = jnp.where(lane == 0, facing, facing_t)
    f_second = jnp.where(lane == 0, facing_t, facing)
    low_amps = jnp.where(lane == 0, kept, swapped)
    high_amps = jnp.where(lane == 0, swapped, kept)
    m0 = jnp.where(side == 0, cross_blocks[0], low_amps.T)
    m1 = jnp.where(side == 0, cross_blocks[1], high_amps.T)
    mixed_use = jnp.where(lane == 0, mixed_amps, mixed_amps.T)
    gamma = nt(own, own_amps) + nt(twin, mixed_use) + nt(f_first, m0) + nt(f_second, m1)
    return gamma.reshape(rows, occ_count, virt)


LANES = 128
IN_VMEM = pl.BlockSpec(memory_space=pltpu.VMEM)
IN_SMEM = pl.BlockSpec(memory_space=pltpu.SMEM)
SLOTS = (1, 2, 4)
WHOLE_SLOTS = 2
STEP = 512


def dot_tn(left, right):
    return lax.dot_general(
        left, right, (((0,), (0,)), ((), ())), preferred_element_type=jnp.float32)


def dot_nn(left, right):
    return jnp.dot(left, right, preferred_element_type=jnp.float32)


def halves(value):
    top = value.astype(jnp.bfloat16)
    return top, (value - top.astype(jnp.float32)).astype(jnp.bfloat16)


def spots():
    aux, pair = lax.axis_index("aux"), lax.axis_index("pair")
    return aux & 1, aux >> 1, pair >> 1, pair & 1, pair


def call(kernel, outs, args, in_smem=(), scratch=(), flops=0):
    outs = [jax.ShapeDtypeStruct(o[:2], o[2] if len(o) > 2 else jnp.float32) for o in outs]
    moved = sum(a.size * a.dtype.itemsize for a in (*args, *outs))
    return pl.pallas_call(
        kernel,
        out_shape=outs,
        in_specs=[IN_SMEM if i in in_smem else IN_VMEM for i in range(len(args))],
        out_specs=[IN_VMEM for _ in outs],
        scratch_shapes=list(scratch),
        cost_estimate=pl.CostEstimate(flops=flops, bytes_accessed=moved, transcendentals=0),
    )(*args)


def unpack(ref, rows, chunks, top_ref, low_ref):
    step = min(256, rows)

    @pl.loop(0, rows // step)
    def _(block):
        for c in range(chunks):
            top, low = halves(ref[pl.ds(block * step * chunks + c, step, stride=chunks), :])
            where = pl.ds(pl.multiple_of(block * step, step), step)
            top_ref[where, c * LANES:(c + 1) * LANES] = top
            low_ref[where, c * LANES:(c + 1) * LANES] = low


def half_rows(left, right, lane, chunks, spare, store):
    full = chunks // 2

    def product(chunk):
        where = pl.ds(pl.multiple_of(chunk * LANES, LANES), LANES)
        lt, ll = left[0][:, where], left[1][:, where]
        rt, rl = right[0][...], right[1][...]
        return dot_tn(lt, rt) + (dot_tn(lt, rl) + dot_tn(ll, rt))

    for t in range(full):
        store(t * LANES, LANES, product(lane * (chunks - full) + t))
    if chunks % 2:
        spare[...] = product(full)
        part = LANES // 2
        store(full * LANES, part, spare[pl.ds(pl.multiple_of(lane * part, part), part), :])


def row_origin(row, lane, chunks):
    full = chunks // 2
    whole = full * LANES
    return jnp.where(
        row < whole, lane * (chunks - full) * LANES + row,
        full * LANES + lane * (LANES // 2) + row - whole)


def own_kernel(rows, chunks, own, keep, send, top, low, acc, cross):
    x, _, _, _, _ = spots()
    unpack(own, rows, chunks, top, low)
    cross[...] = dot_tn(top[...], low[...])
    acc[...] = dot_tn(top[...], top[...]) + (cross[...] + cross[...].T)
    size = keep.shape[0]
    keep[...] = acc[pl.ds(pl.multiple_of(x * size, 8), size), :]
    send[...] = acc[pl.ds(pl.multiple_of((1 - x) * size, 8), size), :]


def twin_kernel(rows, chunks, own_top, own_low, twin, keep, send, top, low, acc, spare):
    x, _, _, lane, _ = spots()
    unpack(twin, rows, chunks, top, low)

    def store(first, count, value):
        acc[first:first + count, :] = value

    own, other = (own_top, own_low), (top, low)
    for here, left, right in ((0, own, other), (1, other, own)):

        @pl.when(lane == here)
        def _(here=here, left=left, right=right):
            half_rows(left, right, here, chunks, spare, store)

    size = keep.shape[0]
    keep[...] = acc[pl.ds(pl.multiple_of(x * size, 8), size), :]
    send[...] = acc[pl.ds(pl.multiple_of((1 - x) * size, 8), size), :]


def side_pair(mask, slot, slots):
    if slots == 4:
        return slot // 2, 2 + slot % 2, mask[slot // 2, 2 + slot % 2]
    count, found, weight = jnp.int32(0), jnp.int32(0), jnp.int32(0)
    for k in range(4):
        live = mask[k // 2, 2 + k % 2]
        hit = (live > 0) & (count == slot)
        found = jnp.where(hit, k, found)
        weight = jnp.where(hit, live, weight)
        count = count + (live > 0).astype(jnp.int32)
    return found // 2, 2 + found % 2, weight


def cross_kernel(half, chunks, mask, own_top, own_low, twin_top, twin_low, face, face_twin,
                 *rest):
    outs, (face_tops, face_lows), (top, low, acc, spare) = rest[:-6], rest[-6:-4], rest[-4:]
    x, _, side, lane, pair = spots()
    virt = chunks * LANES
    rows = pl.ds(pl.multiple_of(side * half, half), half)
    top[pair], low[pair] = own_top[rows, :], own_low[rows, :]
    top[pair ^ 1], low[pair ^ 1] = twin_top[rows, :], twin_low[rows, :]
    for ref, flip in ((face, 2), (face_twin, 3)):
        which = pair ^ flip
        unpack(ref, half, chunks, top.at[which], low.at[which])
        at = slice((flip - 2) * half, (flip - 1) * half)
        face_tops[at, :], face_lows[at, :] = top[which], low[which]
    live = jnp.int32(0)
    for k in range(4):
        live = live + (mask[k // 2, 2 + k % 2] > 0).astype(jnp.int32)
    square = x + 2 * side
    for number, slots in enumerate(SLOTS):
        fewer = SLOTS[number - 1] if number else 0

        @pl.when((live > fewer) & (live <= slots))
        def _(number=number, slots=slots):
            for slot in range(slots):
                first, second, _ = side_pair(mask, slot, slots)

                def store(start, count, value, slot=slot):
                    at = slot * virt // 2 + start
                    acc[at:at + count, :] = value

                half_rows((top.at[first], low.at[first]), (top.at[second], low.at[second]),
                          lane, chunks, spare, store)
            mine = outs[4 * number:4 * number + 4]
            size = mine[0].shape[0]
            for step in range(4):
                mine[step][...] = acc[
                    pl.ds(pl.multiple_of((square ^ step) * size, 8), size), :]


def add_kernel(members, sets, *refs):
    _, z, _, _, _ = spots()
    ins, outs = refs[:members * sets], refs[members * sets:]
    count = len(outs)
    at = 0
    for which in range(sets):
        mine = ins[which * members:(which + 1) * members]
        size = mine[0].shape[0] // count
        for step in range(count):
            where = pl.ds(pl.multiple_of((z ^ step) * size, 8), size)
            total = mine[0][where, :]
            for other in mine[1:]:
                total = total + other[where, :]
            outs[step][at:at + size, :] = total
        at += size


def sum_kernel(*refs):
    total = refs[0][...]
    for other in refs[1:-1]:
        total = total + other[...]
    refs[-1][...] = total


def join_kernel(sizes, *refs):
    _, z, _, _, _ = spots()
    out, ins = refs[-1], refs[:-1]
    inner = outer = 0
    for size in sizes:
        for step, piece in enumerate(ins):
            at = pl.multiple_of(outer + (z ^ step) * size, 8)
            out[pl.ds(at, size), :] = piece[inner:inner + size, :]
        inner += size
        outer += size * len(ins)


def scale_kernel(chunks, slots, members, cut, mask, occ, vir_row, vir_col, *refs):
    x, z, side, lane, pair = spots()
    ins, out = refs[:members], refs[members]
    virt = chunks * LANES
    size = out.shape[0]
    own_size = size * 2 // 3
    for group in range(size // 8):
        row = group * 8
        if slots == 0:
            mixed = row >= own_size
            if mixed:
                row = (x * members + z) * (size - own_size) + row - own_size
                first, second = 2 * side, 2 * side + 1
                origin = row_origin(row, lane, chunks)
            else:
                origin = (x * members + z) * own_size + row
                first = second = pair
            weight = mask[first, second]
        else:
            row = ((x + 2 * side) * (members if cut else 1) + (z if cut else 0)) * size + row
            first, second, weight = side_pair(mask, 0, slots)
            for slot in range(1, slots):
                f, s, w = side_pair(mask, slot, slots)
                here = row >= slot * virt // 2
                first = jnp.where(here, f, first)
                second = jnp.where(here, s, second)
                weight = jnp.where(here, w, weight)
            origin = row_origin(row % (virt // 2), lane, chunks)
        here = slice(group * 8, group * 8 + 8)
        total = ins[0][here, :]
        for other in ins[1:]:
            total = total + other[here, :]
        energy = vir_col[pl.ds(pl.multiple_of(origin, 8), 8), :] + vir_row[...]
        energy = energy - occ[first] - occ[second]
        out[here, :] = weight.astype(jnp.float32) * total / energy


def place_block(halves_ref, first, chunks, whole):
    full = chunks // 2
    part = LANES // 2
    for lane in range(2):
        at = lane * (chunks - full) * LANES
        whole[at:at + full * LANES, :] = halves_ref[lane, pl.ds(first, full * LANES), :]
        if chunks % 2:
            at = full * LANES + lane * part
            whole[at:at + part, :] = halves_ref[
                lane, pl.ds(first + full * LANES, part), :]


def wide(top, low):
    return jnp.concatenate([top, low, top], 1)


def stack(value, stacked):
    virt = value.shape[0]
    top, low = halves(value)
    stacked[0:virt, :] = top
    stacked[virt:2 * virt, :] = top
    stacked[2 * virt:3 * virt, :] = low


def near_gamma_kernel(rows, chunks, own_top, own_low, twin_top, twin_low,
                      keep, other, keep_t, other_t, out, parts, whole, stacked):
    x, _, _, lane, _ = spots()
    virt = chunks * LANES
    size = keep.shape[0]
    own_size = size * 2 // 3
    mixed = size - own_size
    for ref, slot, piece in ((keep, lane, x), (other, lane, 1 - x),
                             (keep_t, 1 - lane, x), (other_t, 1 - lane, 1 - x)):
        parts[slot, pl.ds(pl.multiple_of(piece * own_size, 8), own_size), :] = ref[:own_size, :]
        parts[slot, pl.ds(pl.multiple_of(virt + piece * mixed, 8), mixed), :] = ref[own_size:, :]
    stack(parts[lane, 0:virt, :], stacked.at[0])
    place_block(parts, virt, chunks, whole)

    @pl.when(lane == 0)
    def _():
        stack(whole[...].T, stacked.at[1])

    @pl.when(lane == 1)
    def _():
        stack(whole[...], stacked.at[1])

    step = min(STEP, rows)

    @pl.loop(0, rows // step)
    def _(block):
        at = pl.ds(pl.multiple_of(block * step, step), step)
        out[at, :] = dot_nn(wide(own_top[at, :], own_low[at, :]), stacked[0]) + dot_nn(
            wide(twin_top[at, :], twin_low[at, :]), stacked[1])


def far_gamma_kernel(rows, chunks, slots, mask, base, face_tops, face_lows, far, far_t, *rest):
    pieces, pieces_t = rest[0:4], rest[4:8]
    out, parts, whole, stacked, total = rest[8:]
    x, _, side, lane, pair = spots()
    virt = chunks * LANES
    half = rows // 2
    size = pieces[0].shape[0]
    square = x + 2 * side
    for step in range(4):
        where = pl.ds(pl.multiple_of((square ^ step) * size, 8), size)
        parts[lane, where, :] = pieces[step][...]
        parts[1 - lane, where, :] = pieces_t[step][...]
    step = min(STEP, half)
    total[...] = base[...]
    for flip in (0, 1):
        partner = pair ^ (2 + flip)
        first = jnp.minimum(pair, partner)
        second = jnp.maximum(pair, partner)
        live, at = jnp.int32(0), jnp.int32(0)
        for slot in range(slots):
            f, s, weight = side_pair(mask, slot, slots)
            hit = (f == first) & (s == second) & (weight > 0)
            live = jnp.where(hit, 1, live)
            at = jnp.where(hit, slot, at)

        @pl.when(live > 0)
        def _(flip=flip, at=at):
            place_block(parts, pl.multiple_of(at * (virt // 2), 8), chunks, whole)

            @pl.when(side == 0)
            def _():
                stack(whole[...].T, stacked)

            @pl.when(side == 1)
            def _():
                stack(whole[...], stacked)

            @pl.loop(0, half // step)
            def _(block):
                rows_in = pl.ds(pl.multiple_of(flip * half + block * step, step), step)
                rows_out = pl.ds(pl.multiple_of(side * half + block * step, step), step)
                total[rows_out, :] += dot_nn(
                    wide(face_tops[rows_in, :], face_lows[rows_in, :]), stacked[...])
                source = far_t if flip else far
                parts_in = [
                    halves(source[pl.ds(block * step * chunks + c, step, stride=chunks), :])
                    for c in range(chunks)]
                tops, lows = [p[0] for p in parts_in], [p[1] for p in parts_in]
                rows_out = pl.ds(pl.multiple_of((1 - side) * half + block * step, step), step)
                total[rows_out, :] += dot_nn(
                    jnp.concatenate(tops + lows + tops, 1), stacked[...])

    flat_kernel(rows, chunks, total, out)


def flat_kernel(rows, chunks, base, out):
    step = min(256, rows)

    @pl.loop(0, rows // step)
    def _(block):
        at = block * step
        for c in range(chunks):
            out[pl.ds(at * chunks + c, step, stride=chunks), :] = base[
                pl.ds(pl.multiple_of(at, step), step), c * LANES:(c + 1) * LANES]


def opening(three_center, occ_energy, pair_mask):
    rows, _, virt = three_center.shape
    chunks = virt // LANES
    half = rows // 2
    z_count = lax.axis_size("aux") // 2
    pair = lax.axis_index("pair")
    side, lane = pair // 2, pair % 2
    own = three_center.reshape(rows * chunks, LANES)
    bf16, f32 = jnp.bfloat16, jnp.float32
    block_flops = 6 * rows * virt * virt
    flat_pieces = own.reshape(2, half * chunks, LANES)
    near = across(pick(flat_pieces, 1 - side), 0, 2)
    twin = across(own, 0, 1)
    split = [(rows, virt, bf16)] * 2
    mixed_rows = virt // 2
    occ_side = jnp.concatenate([occ_energy, across(occ_energy, 0, 1)])
    occ_side = jnp.where(lane == 0, occ_side, occ_side[::-1])
    occ_other = across(occ_side, 0, 2)
    occ = jnp.where(side == 0, jnp.concatenate([occ_side, occ_other]),
                    jnp.concatenate([occ_other, occ_side]))
    keep_a, send_a, own_top, own_low = call(
        functools.partial(own_kernel, rows, chunks), [(virt // 2, virt)] * 2 + split, [own],
        scratch=[pltpu.VMEM((virt, virt), f32)] * 2, flops=block_flops)
    got_a = across(send_a, 1, 0)
    twin, send_a = lax.optimization_barrier((twin, send_a))
    keep_b, send_b, twin_top, twin_low = call(
        functools.partial(twin_kernel, rows, chunks), [(mixed_rows // 2, virt)] * 2 + split,
        [own_top, own_low, twin],
        scratch=[pltpu.VMEM((mixed_rows, virt), f32), pltpu.VMEM((LANES, virt), f32)],
        flops=block_flops)
    got_b = across(send_b, 1, 0)
    piece_rows = (virt + mixed_rows) // 2 // z_count
    pieces = call(functools.partial(add_kernel, 2, 2), [(piece_rows, virt)] * z_count,
                   [keep_a, got_a, keep_b, got_b])
    side_got = [across(pieces[s], s << 1, 0) for s in range(1, z_count)]
    near_t = across(near, 0, 1)
    most = SLOTS[-1] * mixed_rows
    cross = call(
        functools.partial(cross_kernel, half, chunks),
        [(n * mixed_rows // 4, virt) for n in SLOTS for _ in range(4)] + split,
        [pair_mask, own_top, own_low, twin_top, twin_low, near, near_t], in_smem=(0,),
        scratch=[pltpu.VMEM((4, half, virt), bf16)] * 2 + [
            pltpu.VMEM((most, virt), f32), pltpu.VMEM((LANES, virt), f32)],
        flops=block_flops)
    cross, faces = cross[:-2], cross[-2:]
    far_send = pick(flat_pieces, side)
    return lax.optimization_barrier((
        (own_top, own_low, twin_top, twin_low), faces, far_send, occ,
        [pieces[0], *side_got], cross))


def closing(slots, shape, opened, vir_row, vir_col, pair_mask):
    splits, faces, far_send, occ, side_parts, cross = opened
    rows, _, virt = shape
    chunks = virt // LANES
    z_count = lax.axis_size("aux") // 2
    bf16, f32 = jnp.bfloat16, jnp.float32
    block_flops = 6 * rows * virt * virt
    energies = [pair_mask, occ, vir_row, vir_col]
    piece_rows = side_parts[0].shape[0]
    own_size = piece_rows * 2 // 3
    total_rows = slots * virt // 2
    square_rows = total_rows // 4
    slab_rows = square_rows // z_count
    flips = [(0, 0), (1, 0), (0, 2), (1, 2)]

    def z_spread(slab):
        return [across(slab, s << 1, 0) for s in range(1, z_count)]

    if slots:
        at = 4 * SLOTS.index(slots)
        cross = cross[at:at + 4]
        cross_got = [across(cross[s], *flips[s]) for s in range(1, 4)]
    slab, = call(
        functools.partial(scale_kernel, chunks, 0, z_count, True),
        [(piece_rows, virt)], [*energies, *side_parts], in_smem=(0, 1))
    side_slabs = [slab] + z_spread(slab)
    joined, = call(
        functools.partial(join_kernel, (own_size, piece_rows - own_size)),
        [(piece_rows * z_count, virt)], side_slabs)
    other = across(joined, 1, 0)
    joined_t = across(joined, 0, 1)
    other_t = across(other, 0, 1)
    gamma, = call(
        functools.partial(near_gamma_kernel, rows, chunks), [(rows, virt)],
        [*splits, joined, other, joined_t, other_t],
        scratch=[pltpu.VMEM((2, virt + virt // 2, virt), f32), pltpu.VMEM((virt, virt), f32),
                 pltpu.VMEM((2, 3 * virt, virt), bf16)], flops=2 * block_flops)
    if not slots:
        gamma, = call(functools.partial(flat_kernel, rows, chunks), [(rows * chunks, LANES)],
                      [gamma])
        return gamma
    if slots <= WHOLE_SLOTS:
        summed, = call(sum_kernel, [(square_rows, virt)], [cross[0], *cross_got])
        z_got = z_spread(summed)
        joined_c, = call(
            functools.partial(scale_kernel, chunks, slots, z_count, False),
            [(square_rows, virt)], [*energies, summed, *z_got], in_smem=(0, 1))
    else:
        pieces_c = call(
            functools.partial(add_kernel, 4, 1), [(slab_rows, virt)] * z_count,
            [cross[0], *cross_got])
        summed = pieces_c[0]
        z_got = [across(pieces_c[s], s << 1, 0) for s in range(1, z_count)]
        cross_slab, = call(
            functools.partial(scale_kernel, chunks, slots, z_count, True),
            [(slab_rows, virt)], [*energies, pieces_c[0], *z_got], in_smem=(0, 1))
        joined_c, = call(
            functools.partial(join_kernel, (slab_rows,)), [(square_rows, virt)],
            [cross_slab] + z_spread(cross_slab))
    far_send, summed = lax.optimization_barrier((far_send, summed))
    far = across(far_send, 0, 2)
    far_t = across(far, 0, 1)
    whole = [across(joined_c, *flips[s]) for s in range(1, 4)]
    joined_ct = across(joined_c, 0, 1)
    whole_t = [across(piece, 0, 1) for piece in whole]
    gamma, = call(
        functools.partial(far_gamma_kernel, rows, chunks, slots),
        [(rows * chunks, LANES)],
        [pair_mask, gamma, *faces, far, far_t, joined_c, *whole, joined_ct, *whole_t],
        in_smem=(0,),
        scratch=[pltpu.VMEM((2, total_rows, virt), f32), pltpu.VMEM((virt, virt), f32),
                 pltpu.VMEM((3 * virt, virt), bf16), pltpu.VMEM((rows, virt), f32)],
        flops=2 * block_flops)
    return gamma


def on_device(three_center, occ_energy, vir_energy, pair_mask):
    rows, occ_count, virt = three_center.shape
    aux_count, pair_count = lax.axis_size("aux"), lax.axis_size("pair")
    z_count = aux_count // 2
    fits = (
        occ_count == 1 and pair_count == 4 and z_count in (2, 4) and aux_count == 2 * z_count
        and virt % LANES == 0 and rows % 16 == 0
        and virt % (8 * z_count * 8 // 2) == 0 and (virt + virt // 2) % (16 * z_count) == 0)
    args = (three_center, occ_energy, vir_energy, pair_mask)
    if not fits:
        return general_path(*args)
    live = jnp.sum((pair_mask[:2, 2:] > 0).astype(jnp.int32))
    branch = jnp.int32(0)
    for slots in (0, *SLOTS[:-1]):
        branch = branch + (live > slots).astype(jnp.int32)
    opened = opening(three_center, occ_energy, pair_mask)
    gamma = lax.switch(
        branch, [functools.partial(closing, n, three_center.shape)
                 for n in (0, *SLOTS)],
        opened, vir_energy.reshape(1, virt), vir_energy.reshape(virt, 1), pair_mask)
    return gamma.reshape(three_center.shape)


def solution(mesh):
    in_specs = (P("aux", "pair", None), P("pair"), P(), P())
    out_specs = P("aux", "pair", None)
    return jax.shard_map(
        on_device, mesh=mesh, in_specs=in_specs, out_specs=out_specs, check_vma=False
    )
```

profile of v0, /device:TPU:0, one launch (start us, length us, event | category | flops | bytes accessed | tf_op | source)
XLA Modules:
  0.0 127.8 jit_solution(17176957001330776313)
XLA Ops:
  0.0 0.5 collective-permute-start.72
  0.5 2.4 %dynamic-slice_bitcast_fusion = (f32[1536,128]{1,0:T(8,128)}, f32[1536,128]{1,0:T(8,128)S(1)}) fusion(f32[2,1536,128]{2,1,0:T(8,128)} %bitcast.11, s32[]{:T(128)S(6)} %select_n.36, s32[]{:T(128)S(6)} %select_n.35), kind=kLoop, calls=%fused_computation | loop fusion | bytes 3145736 | tf_op jit(solution)/shard_map/jit(dynamic_index_in_dim)/squeeze | solution.py:25
  2.9 2.5 %collective-permute-start.73 = (f32[1536,128]{1,0:T(8,128)S(1)}, f32[1536,128]{1,0:T(8,128)S(1)}, u32[]{:S(2)}, u32[]{:S(2)}) collective-permute-start(f32[1536,128]{1,0:T(8,128)S(1)} %get-tuple-element.399), channel_id=1, source_target_pairs={{0,2},{1,3},{2,0},{3,1},{4,6},{5,7},{6,4},{7,5},{8,10},{9,11},{10,... | collective-permute-start | bytes 2359304 | tf_op jit(solution)/shard_map/ppermute | solution.py:21
  5.4 18.2 %collective-permute-done.73.face = f32[1536,128]{1,0:T(8,128)S(1)} collective-permute-done((f32[1536,128]{1,0:T(8,128)S(1)}, f32[1536,128]{1,0:T(8,128)S(1)}, u32[]{:S(2)}, u32[]{:S(2)}) %collective-permute-start.73) | collective-permute-done | bytes 786464 | tf_op jit(solution)/shard_map/ppermute | solution.py:21
  23.6 0.5 collective-permute-start.75
  24.1 3.6 %shard_map.50 = (f32[192,384]{1,0:T(8,128)}, f32[192,384]{1,0:T(8,128)}, bf16[1024,384]{1,0:T(8,128)(2,1)S(1)}, bf16[1024,384]{1,0:T(8,128)(2,1)S(1)}) custom-call(f32[3072,128]{1,0:T(8,128)} %bitcast.12), custom_call_target="tpu_custom_call" | custom-call | flops 905969664 | bytes 3735552 | tf_op jit(solution)/shard_map/pallas_call | solution.py:208
  27.7 1.7 %collective-permute-start.77 = (f32[192,384]{1,0:T(8,128)}, f32[192,384]{1,0:T(8,128)S(1)}, u32[]{:S(2)}, u32[]{:S(2)}) collective-permute-start(f32[192,384]{1,0:T(8,128)} %get-tuple-element.278), channel_id=1, source_target_pairs={{0,4},{1,5},{2,6},{3,7},{4,0},{5,1},{6,2},{7,3},{8,12},{9,13},{10,... | collective-permute-start | bytes 884744 | tf_op jit(solution)/shard_map/ppermute | solution.py:21
  30.1 0.7 fusion
  32.8 0.6 pad_maximum_fusion
  33.4 0.1 rev.3
  33.5 4.0 %shard_map.51 = (f32[96,384]{1,0:T(8,128)}, f32[96,384]{1,0:T(8,128)}, bf16[1024,384]{1,0:T(8,128)(2,1)}, bf16[1024,384]{1,0:T(8,128)(2,1)}) custom-call(bf16[1024,384]{1,0:T(8,128)(2,1)S(1)} %get-tuple-element.308.own_top, bf16[1024,384]{1,0:T(8,128)(2,1)S(1)} %get-tuple-element.309.own_low, f32[3072,128]{1,0:T(8,128)} %collective-permute-done.72.twin), custom_call_target="tpu_custom_call" | custom-call | flops 905969664 | bytes 5013504 | tf_op jit(solution)/shard_map/pallas_call | solution.py:208
  37.5 0.3 collective-permute-start.78
  37.8 0.6 broadcast_select_fusion
  38.4 1.7 %collective-permute-start.76 = (f32[2]{0:T(128)S(1)}, f32[2]{0:T(128)S(1)}, u32[]{:S(2)}, u32[]{:S(2)}) collective-permute-start(f32[2]{0:T(128)S(1)} %broadcast_select_fusion), channel_id=1, source_target_pairs={{0,2},{1,3},{2,0},{3,1},{4,6},{5,7},{6,4},{7,5},{8,10},{9,11},{10,... | collective-permute-start | bytes 32 | tf_op jit(solution)/shard_map/ppermute | solution.py:21
  40.2 3.0 %collective-permute-done.78.refs_3_ = f32[96,384]{1,0:T(8,128)S(1)} collective-permute-done((f32[96,384]{1,0:T(8,128)}, f32[96,384]{1,0:T(8,128)S(1)}, u32[]{:S(2)}, u32[]{:S(2)}) %collective-permute-start.78) | collective-permute-done | bytes 147488 | tf_op jit(solution)/shard_map/ppermute | solution.py:21
  43.2 0.7 copy-done.18
  43.9 1.9 %shard_map.53 = (f32[72,384]{1,0:T(8,128)S(1)}, f32[72,384]{1,0:T(8,128)}, f32[72,384]{1,0:T(8,128)}, f32[72,384]{1,0:T(8,128)}) custom-call(f32[192,384]{1,0:T(8,128)} %get-tuple-element.284.refs_0_, f32[192,384]{1,0:T(8,128)} %copy-done.12, f32[96,384]{1,0:T(8,128)} %get-tuple-element.285.refs_2_, f32[96,384]{1,0:T(8,128)} %copy-done.18), custom_call_target="tpu_custom_call" | custom-call | bytes 1327104 | tf_op jit(solution)/shard_map/pallas_call | solution.py:208
  45.8 1.6 %collective-permute-start.79 = (f32[72,384]{1,0:T(8,128)}, f32[72,384]{1,0:T(8,128)S(1)}, u32[]{:S(2)}, u32[]{:S(2)}) collective-permute-start(f32[72,384]{1,0:T(8,128)} %get-tuple-element.288), channel_id=1, source_target_pairs={{0,8},{1,9},{2,10},{3,11},{4,12},{5,13},{6,14},{7,15},{8,0},{9,1},... | collective-permute-start | bytes 331784 | tf_op jit(solution)/shard_map/ppermute | solution.py:21
  47.4 2.6 %collective-permute-start.80 = (f32[72,384]{1,0:T(8,128)}, f32[72,384]{1,0:T(8,128)S(1)}, u32[]{:S(2)}, u32[]{:S(2)}) collective-permute-start(f32[72,384]{1,0:T(8,128)} %get-tuple-element.289), channel_id=1, source_target_pairs={{0,16},{1,17},{2,18},{3,19},{4,20},{5,21},{6,22},{7,23},{8,24},{9,... | collective-permute-start | bytes 331784 | tf_op jit(solution)/shard_map/ppermute | solution.py:21
  50.0 0.2 collective-permute-start.81
  50.2 0.1 broadcast_select_fusion.1
  50.3 4.4 %shard_map.52 = (f32[48,384]{1,0:T(8,128)S(1)}, f32[48,384]{1,0:T(8,128)S(1)}, f32[48,384]{1,0:T(8,128)S(1)}, f32[48,384]{1,0:T(8,128)}, f32[96,384]{1,0:T(8,128...) custom-call(s32[4,4]{1,0:T(4,128)S(1)} %copy-done.15, ...), custom_call_target="tpu_custom_call" | custom-call | flops 905969664 | bytes 8355904 | tf_op jit(solution)/shard_map/pallas_call | solution.py:208
  54.7 3.3 %collective-permute-done.80 = f32[72,384]{1,0:T(8,128)S(1)} collective-permute-done((f32[72,384]{1,0:T(8,128)}, f32[72,384]{1,0:T(8,128)S(1)}, u32[]{:S(2)}, u32[]{:S(2)}) %collective-permute-start.80) | collective-permute-done | bytes 110624 | tf_op jit(solution)/shard_map/ppermute | solution.py:21
  58.0 69.8 %conditional.1 = (f32[1024,1,384]{2,1,0:T(1,128)}) conditional(s32[]{:T(128)} %clamp.3, (s32[4,4]{1,0:T(4,128)S(1)}, f32[4]{0:T(128)S(1)}, f32[1,384]{1,0:T(1,128)S(1)}, f32[384,1]{0,1:T(1,128)S(1)}, f32[72,384]{1,0:T(8,128)S(1)}, /*index=5*/f32[72,384]{1,0:T(8,128)S(1)}, f32[72,384]{1,0:T(8,128)S(1)}, ...), branch_computations={%region_1.2_spmd, %region_2.3_spmd, %region_3.4_spmd, %region_4.5_... | conditional | flops 3623878656 | bytes 60504736 | solution.py:672
  58.0 1.5 %collective-permute-start.14 = (f32[48,384]{1,0:T(8,128)}, f32[48,384]{1,0:T(8,128)S(1)}, u32[]{:S(2)}, u32[]{:S(2)}) collective-permute-start(f32[48,384]{1,0:T(8,128)} %get-tuple-element.179), channel_id=1, source_target_pairs={{0,6},{1,7},{2,4},{3,5},{4,2},{5,3},{6,0},{7,1},{8,14},{9,15},{10,... | collective-permute-start | bytes 221192 | tf_op jit(solution)/shard_map/cond/branch_1_fun/ppermute | solution.py:21
  59.5 0.5 collective-permute-start.13
  60.1 1.4 %collective-permute-start.12 = (f32[48,384]{1,0:T(8,128)S(1)}, f32[48,384]{1,0:T(8,128)S(1)}, u32[]{:S(2)}, u32[]{:S(2)}) collective-permute-start(f32[48,384]{1,0:T(8,128)S(1)} %get-tuple-element.177), channel_id=1, source_target_pairs={{0,4},{1,5},{2,6},{3,7},{4,0},{5,1},{6,2},{7,3},{8,12},{9,13},{10,... | collective-permute-start | bytes 221192 | tf_op jit(solution)/shard_map/cond/branch_1_fun/ppermute | solution.py:21
  61.5 2.0 %collective-permute-done.14.refs_3_ = f32[48,384]{1,0:T(8,128)S(1)} collective-permute-done((f32[48,384]{1,0:T(8,128)}, f32[48,384]{1,0:T(8,128)S(1)}, u32[]{:S(2)}, u32[]{:S(2)}) %collective-permute-start.14) | collective-permute-done | bytes 73760 | tf_op jit(solution)/shard_map/cond/branch_1_fun/ppermute | solution.py:21
  63.5 0.7 collective-permute-done.13.refs_2_
  64.3 0.1 collective-permute-done.12.refs_1_
  64.4 0.5 copy-done.52
  64.9 0.1 copy-done.53
  65.0 1.6 %branch_1_fun.9.refs_0_ = f32[48,384]{1,0:T(8,128)} custom-call(f32[48,384]{1,0:T(8,128)S(1)} %get-tuple-element.176.refs_0_, f32[48,384]{1,0:T(8,128)} %copy-done.53, f32[48,384]{1,0:T(8,128)} %copy-done.52, f32[48,384]{1,0:T(8,128)} %copy-done.51), custom_call_target="tpu_custom_call" | custom-call | bytes 368640 | tf_op jit(solution)/shard_map/cond/branch_1_fun/pallas_call | solution.py:208
  66.7 1.5 %collective-permute-start.15 = (f32[1536,128]{1,0:T(8,128)}, f32[1536,128]{1,0:T(8,128)S(1)}, u32[]{:S(2)}, u32[]{:S(2)}) collective-permute-start(f32[1536,128]{1,0:T(8,128)} %get-tuple-element.180), channel_id=1, source_target_pairs={{0,2},{1,3},{2,0},{3,1},{4,6},{5,7},{6,4},{7,5},{8,10},{9,11},{10,... | collective-permute-start | bytes 2359304 | tf_op jit(solution)/shard_map/cond/branch_1_fun/ppermute | solution.py:21
  68.2 0.8 copy.11.vir_col
  69.0 1.7 %branch_1_fun.6.refs_0_ = f32[72,384]{1,0:T(8,128)} custom-call(s32[4,4]{1,0:T(4,128)S(1)} %get-tuple-element.161.mask, f32[4]{0:T(128)S(1)} %get-tuple-element.166.occ, f32[1,384]{1,0:T(1,128)S(1)} %get-tuple-element.167.vir_row, f32[384,1]{1,0:T(8,128)} %copy.11.vir_col, f32[72,384]{1,0:T(8,128)S(1)} %get-tuple-element.169.refs_0_, ...), custom_call_target="tpu_custom_call" | custom-call | bytes 556112 | tf_op jit(solution)/shard_map/cond/branch_1_fun/pallas_call | solution.py:208
  70.7 2.5 %collective-permute-start.8 = (f32[72,384]{1,0:T(8,128)}, f32[72,384]{1,0:T(8,128)S(1)}, u32[]{:S(2)}, u32[]{:S(2)}) collective-permute-start(f32[72,384]{1,0:T(8,128)} %branch_1_fun.6.refs_0_), channel_id=1, source_target_pairs={{0,24},{1,25},{2,26},{3,27},{4,28},{5,29},{6,30},{7,31},{8,16},{9,... | collective-permute-start | bytes 331784 | tf_op jit(solution)/shard_map/cond/branch_1_fun/ppermute | solution.py:21
  73.2 0.7 collective-permute-start.7
  73.9 1.2 collective-permute-start.6
  75.1 2.5 %collective-permute-done.8.refs_3_ = f32[72,384]{1,0:T(8,128)S(1)} collective-permute-done((f32[72,384]{1,0:T(8,128)}, f32[72,384]{1,0:T(8,128)S(1)}, u32[]{:S(2)}, u32[]{:S(2)}) %collective-permute-start.8) | collective-permute-done | bytes 110624 | tf_op jit(solution)/shard_map/cond/branch_1_fun/ppermute | solution.py:21
  77.5 2.8 %collective-permute-done.7.refs_2_ = f32[72,384]{1,0:T(8,128)S(1)} collective-permute-done((f32[72,384]{1,0:T(8,128)}, f32[72,384]{1,0:T(8,128)S(1)}, u32[]{:S(2)}, u32[]{:S(2)}) %collective-permute-start.7) | collective-permute-done | bytes 110624 | tf_op jit(solution)/shard_map/cond/branch_1_fun/ppermute | solution.py:21
  80.4 0.6 copy-done.35
  81.0 0.6 copy-done.39
  81.6 1.9 %branch_1_fun.7.keep = f32[288,384]{1,0:T(8,128)} custom-call(f32[72,384]{1,0:T(8,128)} %branch_1_fun.6.refs_0_, f32[72,384]{1,0:T(8,128)} %copy-done.39, f32[72,384]{1,0:T(8,128)} %copy-done.35, f32[72,384]{1,0:T(8,128)} %copy-done.31), custom_call_target="tpu_custom_call" | custom-call | bytes 884736 | tf_op jit(solution)/shard_map/cond/branch_1_fun/pallas_call | solution.py:208
  83.6 1.6 %collective-permute-start.9 = (f32[288,384]{1,0:T(8,128)}, f32[288,384]{1,0:T(8,128)S(1)}, u32[]{:S(2)}, u32[]{:S(2)}) collective-permute-start(f32[288,384]{1,0:T(8,128)} %branch_1_fun.7.keep), channel_id=1, source_target_pairs={{0,4},{1,5},{2,6},{3,7},{4,0},{5,1},{6,2},{7,3},{8,12},{9,13},{10,... | collective-permute-start | bytes 1327112 | tf_op jit(solution)/shard_map/cond/branch_1_fun/ppermute | solution.py:21
  85.1 0.5 collective-permute-start.10
  85.6 6.4 %collective-permute-done.9.other = f32[288,384]{1,0:T(8,128)S(1)} collective-permute-done((f32[288,384]{1,0:T(8,128)}, f32[288,384]{1,0:T(8,128)S(1)}, u32[]{:S(2)}, u32[]{:S(2)}) %collective-permute-start.9) | collective-permute-done | bytes 442400 | tf_op jit(solution)/shard_map/cond/branch_1_fun/ppermute | solution.py:21
  92.1 2.6 %collective-permute-start.19 = (f32[48,384]{1,0:T(8,128)S(1)}, f32[48,384]{1,0:T(8,128)S(1)}, u32[]{:S(2)}, u32[]{:S(2)}) collective-permute-start(f32[48,384]{1,0:T(8,128)S(1)} %copy-done.13), channel_id=1, source_target_pairs={{0,24},{1,25},{2,26},{3,27},{4,28},{5,29},{6,30},{7,31},{8,16},{9,... | collective-permute-start | bytes 221192 | tf_op jit(solution)/shard_map/cond/branch_1_fun/ppermute | solution.py:21
  94.6 4.5 %collective-permute-done.19.refs_3_ = f32[48,384]{1,0:T(8,128)S(1)} collective-permute-done((f32[48,384]{1,0:T(8,128)S(1)}, f32[48,384]{1,0:T(8,128)S(1)}, u32[]{:S(2)}, u32[]{:S(2)}) %collective-permute-start.19) | collective-permute-done | bytes 73760 | tf_op jit(solution)/shard_map/cond/branch_1_fun/ppermute | solution.py:21
  99.2 2.6 %collective-permute-done.18.refs_2_ = f32[48,384]{1,0:T(8,128)S(1)} collective-permute-done((f32[48,384]{1,0:T(8,128)S(1)}, f32[48,384]{1,0:T(8,128)S(1)}, u32[]{:S(2)}, u32[]{:S(2)}) %collective-permute-start.18) | collective-permute-done | bytes 73760 | tf_op jit(solution)/shard_map/cond/branch_1_fun/ppermute | solution.py:21
  101.8 1.7 %collective-permute-done.17.refs_1_ = f32[48,384]{1,0:T(8,128)S(1)} collective-permute-done((f32[48,384]{1,0:T(8,128)S(1)}, f32[48,384]{1,0:T(8,128)S(1)}, u32[]{:S(2)}, u32[]{:S(2)}) %collective-permute-start.17) | collective-permute-done | bytes 73760 | tf_op jit(solution)/shard_map/cond/branch_1_fun/ppermute | solution.py:21
  103.5 0.6 copy-done.49
  104.2 1.8 %branch_1_fun.10.rest_0_ = f32[48,384]{1,0:T(8,128)} custom-call(s32[4,4]{1,0:T(4,128)S(1)} %get-tuple-element.161.mask, f32[4]{0:T(128)S(1)} %get-tuple-element.166.occ, f32[1,384]{1,0:T(1,128)S(1)} %get-tuple-element.167.vir_row, f32[384,1]{1,0:T(8,128)} %copy.11.vir_col, f32[48,384]{1,0:T(8,128)} %branch_1_fun.9.refs_0_, f32[48,384]{1,0:T(8,128)} %copy-done.49, ...), custom_call_target="tpu_custom_call" | custom-call | bytes 371792 | tf_op jit(solution)/shard_map/cond/branch_1_fun/pallas_call | solution.py:208
  106.0 1.4 %collective-permute-start.22 = (f32[48,384]{1,0:T(8,128)}, f32[48,384]{1,0:T(8,128)S(1)}, u32[]{:S(2)}, u32[]{:S(2)}) collective-permute-start(f32[48,384]{1,0:T(8,128)} %branch_1_fun.10.rest_0_), channel_id=1, source_target_pairs={{0,6},{1,7},{2,4},{3,5},{4,2},{5,3},{6,0},{7,1},{8,14},{9,15},{10,... | collective-permute-start | bytes 221192 | tf_op jit(solution)/shard_map/cond/branch_1_fun/ppermute | solution.py:21
  107.4 1.6 %collective-permute-start.21 = (f32[48,384]{1,0:T(8,128)}, f32[48,384]{1,0:T(8,128)S(1)}, u32[]{:S(2)}, u32[]{:S(2)}) collective-permute-start(f32[48,384]{1,0:T(8,128)} %branch_1_fun.10.rest_0_), channel_id=1, source_target_pairs={{0,2},{1,3},{2,0},{3,1},{4,6},{5,7},{6,4},{7,5},{8,10},{9,11},{10,... | collective-permute-start | bytes 221192 | tf_op jit(solution)/shard_map/cond/branch_1_fun/ppermute | solution.py:21
  109.0 2.5 %collective-permute-done.22.rest_3_ = f32[48,384]{1,0:T(8,128)S(1)} collective-permute-done((f32[48,384]{1,0:T(8,128)}, f32[48,384]{1,0:T(8,128)S(1)}, u32[]{:S(2)}, u32[]{:S(2)}) %collective-permute-start.22) | collective-permute-done | bytes 73760 | tf_op jit(solution)/shard_map/cond/branch_1_fun/ppermute | solution.py:21
  111.5 1.6 %collective-permute-start.20 = (f32[48,384]{1,0:T(8,128)}, f32[48,384]{1,0:T(8,128)S(1)}, u32[]{:S(2)}, u32[]{:S(2)}) collective-permute-start(f32[48,384]{1,0:T(8,128)} %branch_1_fun.10.rest_0_), channel_id=1, source_target_pairs={{0,4},{1,5},{2,6},{3,7},{4,0},{5,1},{6,2},{7,3},{8,12},{9,13},{10,... | collective-permute-start | bytes 221192 | tf_op jit(solution)/shard_map/cond/branch_1_fun/ppermute | solution.py:21
  113.1 2.9 %collective-permute-done.20.rest_1_ = f32[48,384]{1,0:T(8,128)S(1)} collective-permute-done((f32[48,384]{1,0:T(8,128)}, f32[48,384]{1,0:T(8,128)S(1)}, u32[]{:S(2)}, u32[]{:S(2)}) %collective-permute-start.20) | collective-permute-done | bytes 73760 | tf_op jit(solution)/shard_map/cond/branch_1_fun/ppermute | solution.py:21
  116.1 0.5 collective-permute-start.25
  116.6 0.1 collective-permute-start.24
  116.6 6.9 %branch_1_fun.8.base = f32[1024,384]{1,0:T(8,128)} custom-call(bf16[1024,384]{1,0:T(8,128)(2,1)} %copy-done.2, bf16[1024,384]{1,0:T(8,128)(2,1)} %get-tuple-element.163.own_low, bf16[1024,384]{1,0:T(8,128)(2,1)} %get-tuple-element.164.twin_top, bf16[1024,384]{1,0:T(8,128)(2,1)} %get-tuple-element.165.twin_low, f32[288,384]{1,0:T(8,128)} %branch_1_fun.7.keep, ...), custom_call_target="tpu_custom_call" | custom-call | flops 1811939328 | bytes 6488064 | tf_op jit(solution)/shard_map/cond/branch_1_fun/pallas_call | solution.py:208
  123.7 0.6 copy-done.57
  124.2 0.0 copy-done.58
  124.3 3.4 %branch_1_fun.11 = f32[3072,128]{1,0:T(8,128)} custom-call(s32[4,4]{1,0:T(4,128)S(1)} %get-tuple-element.161.mask, f32[1024,384]{1,0:T(8,128)} %branch_1_fun.8.base, bf16[1024,384]{1,0:T(8,128)(2,1)S(1)} %get-tuple-element.173.face_tops, bf16[1024,384]{1,0:T(8,128)(2,1)S(1)} %get-tuple-element.174.face_lows, f32[1536,128]{1,0:T(8,128)} %copy-done.1, ...), custom_call_target="tpu_custom_call" | custom-call | flops 1811939328 | bytes 6881344 | tf_op jit(solution)/shard_map/cond/branch_1_fun/pallas_call | solution.py:208
  (70 shorter events, 0.2 us)
Async XLA Ops:
  0.0 33.5 %collective-permute-start.72 = (f32[3072,128]{1,0:T(8,128)}, f32[3072,128]{1,0:T(8,128)}, u32[]{:S(2)}, u32[]{:S(2)}) collective-permute-start(f32[3072,128]{1,0:T(8,128)} %bitcast.10), channel_id=1, source_target_pairs={{0,1},{1,0},{2,3},{3,2},{4,5},{5,4},{6,7},{7,6},{8,9},{9,8},{10,11... | collective-permute-start | bytes 4718600 | tf_op jit(solution)/shard_map/ppermute | solution.py:21
  2.8 27.2 %copy-start.15 = (s32[4,4]{1,0:T(4,128)S(1)}, s32[4,4]{1,0:T(4,128)}, u32[]{:S(2)}) copy-start(s32[4,4]{1,0:T(4,128)} %mask.1) | copy-start | bytes 196
  2.8 29.9 %copy-start.61 = (f32[384]{0:T(512)S(1)}, f32[384]{0:T(512)}, u32[]{:S(2)}) copy-start(f32[384]{0:T(512)} %param.10) | copy-start | bytes 4612
  2.9 20.7 %collective-permute-start.73 = (f32[1536,128]{1,0:T(8,128)S(1)}, f32[1536,128]{1,0:T(8,128)S(1)}, u32[]{:S(2)}, u32[]{:S(2)}) collective-permute-start(f32[1536,128]{1,0:T(8,128)S(1)} %get-tuple-element.399), channel_id=1, source_target_pairs={{0,2},{1,3},{2,0},{3,1},{4,6},{5,7},{6,4},{7,5},{8,10},{9,11},{10,... | collective-permute-start | bytes 2359304 | tf_op jit(solution)/shard_map/ppermute | solution.py:21
  23.6 4.1 %copy-start.7 = (f32[1536,128]{1,0:T(8,128)}, f32[1536,128]{1,0:T(8,128)S(1)}, u32[]{:S(2)}) copy-start(f32[1536,128]{1,0:T(8,128)S(1)} %collective-permute-done.73.face) | copy-start | bytes 2359300
  23.6 26.7 %collective-permute-start.74 = (f32[1536,128]{1,0:T(8,128)S(1)}, f32[1536,128]{1,0:T(8,128)}, u32[]{:S(2)}, u32[]{:S(2)}) collective-permute-start(f32[1536,128]{1,0:T(8,128)S(1)} %collective-permute-done.73.face), channel_id=1, source_target_pairs={{0,1},{1,0},{2,3},{3,2},{4,5},{5,4},{6,7},{7,6},{8,9},{9,8},{10,11... | collective-permute-start | bytes 2359304 | tf_op jit(solution)/shard_map/ppermute | solution.py:21
  23.6 9.2 %collective-permute-start.75 = (f32[1]{0:T(128)}, f32[1]{0:T(128)}, u32[]{:S(2)}, u32[]{:S(2)}) collective-permute-start(f32[1]{0:T(128)} %param.9), channel_id=1, source_target_pairs={{0,1},{1,0},{2,3},{3,2},{4,5},{5,4},{6,7},{7,6},{8,9},{9,8},{10,11... | collective-permute-start | bytes 20 | tf_op jit(solution)/shard_map/ppermute | solution.py:21
  27.7 9.8 %copy-start.4 = (bf16[1024,384]{1,0:T(8,128)(2,1)}, bf16[1024,384]{1,0:T(8,128)(2,1)S(1)}, u32[]{:S(2)}) copy-start(bf16[1024,384]{1,0:T(8,128)(2,1)S(1)} %get-tuple-element.309.own_low) | copy-start | bytes 2359300
  27.7 12.5 %collective-permute-start.77 = (f32[192,384]{1,0:T(8,128)}, f32[192,384]{1,0:T(8,128)S(1)}, u32[]{:S(2)}, u32[]{:S(2)}) collective-permute-start(f32[192,384]{1,0:T(8,128)} %get-tuple-element.278), channel_id=1, source_target_pairs={{0,4},{1,5},{2,6},{3,7},{4,0},{5,1},{6,2},{7,3},{8,12},{9,13},{10,... | collective-permute-start | bytes 884744 | tf_op jit(solution)/shard_map/ppermute | solution.py:21
  37.5 5.7 %collective-permute-start.78 = (f32[96,384]{1,0:T(8,128)}, f32[96,384]{1,0:T(8,128)S(1)}, u32[]{:S(2)}, u32[]{:S(2)}) collective-permute-start(f32[96,384]{1,0:T(8,128)} %get-tuple-element.286), channel_id=1, source_target_pairs={{0,4},{1,5},{2,6},{3,7},{4,0},{5,1},{6,2},{7,3},{8,12},{9,13},{10,... | collective-permute-start | bytes 442376 | tf_op jit(solution)/shard_map/ppermute | solution.py:21
  38.4 11.7 %collective-permute-start.76 = (f32[2]{0:T(128)S(1)}, f32[2]{0:T(128)S(1)}, u32[]{:S(2)}, u32[]{:S(2)}) collective-permute-start(f32[2]{0:T(128)S(1)} %broadcast_select_fusion), channel_id=1, source_target_pairs={{0,2},{1,3},{2,0},{3,1},{4,6},{5,7},{6,4},{7,5},{8,10},{9,11},{10,... | collective-permute-start | bytes 32 | tf_op jit(solution)/shard_map/ppermute | solution.py:21
  40.2 3.0 %copy-start.12 = (f32[192,384]{1,0:T(8,128)}, f32[192,384]{1,0:T(8,128)S(1)}, u32[]{:S(2)}) copy-start(f32[192,384]{1,0:T(8,128)S(1)} %collective-permute-done.77.refs_1_) | copy-start | bytes 884740
  43.2 0.7 copy-start.18
  45.8 8.9 %collective-permute-start.79 = (f32[72,384]{1,0:T(8,128)}, f32[72,384]{1,0:T(8,128)S(1)}, u32[]{:S(2)}, u32[]{:S(2)}) collective-permute-start(f32[72,384]{1,0:T(8,128)} %get-tuple-element.288), channel_id=1, source_target_pairs={{0,8},{1,9},{2,10},{3,11},{4,12},{5,13},{6,14},{7,15},{8,0},{9,1},... | collective-permute-start | bytes 331784 | tf_op jit(solution)/shard_map/ppermute | solution.py:21
  47.4 10.6 %collective-permute-start.80 = (f32[72,384]{1,0:T(8,128)}, f32[72,384]{1,0:T(8,128)S(1)}, u32[]{:S(2)}, u32[]{:S(2)}) collective-permute-start(f32[72,384]{1,0:T(8,128)} %get-tuple-element.289), channel_id=1, source_target_pairs={{0,16},{1,17},{2,18},{3,19},{4,20},{5,21},{6,22},{7,23},{8,24},{9,... | collective-permute-start | bytes 331784 | tf_op jit(solution)/shard_map/ppermute | solution.py:21
  50.0 8.1 %collective-permute-start.81 = (f32[72,384]{1,0:T(8,128)}, f32[72,384]{1,0:T(8,128)S(1)}, u32[]{:S(2)}, u32[]{:S(2)}) collective-permute-start(f32[72,384]{1,0:T(8,128)} %get-tuple-element.290), channel_id=1, source_target_pairs={{0,24},{1,25},{2,26},{3,27},{4,28},{5,29},{6,30},{7,31},{8,16},{9,... | collective-permute-start | bytes 331784 | tf_op jit(solution)/shard_map/ppermute | solution.py:21
  58.0 8.6 %copy-start.2 = (bf16[1024,384]{1,0:T(8,128)(2,1)}, bf16[1024,384]{1,0:T(8,128)(2,1)S(1)}, u32[]{:S(2)}) copy-start(bf16[1024,384]{1,0:T(8,128)(2,1)S(1)} %get-tuple-element.162.own_top) | copy-start | bytes 2359300 | tf_op jit(solution)/shard_map/cond
  58.0 5.5 %collective-permute-start.14 = (f32[48,384]{1,0:T(8,128)}, f32[48,384]{1,0:T(8,128)S(1)}, u32[]{:S(2)}, u32[]{:S(2)}) collective-permute-start(f32[48,384]{1,0:T(8,128)} %get-tuple-element.179), channel_id=1, source_target_pairs={{0,6},{1,7},{2,4},{3,5},{4,2},{5,3},{6,0},{7,1},{8,14},{9,15},{10,... | collective-permute-start | bytes 221192 | tf_op jit(solution)/shard_map/cond/branch_1_fun/ppermute | solution.py:21
  59.5 4.7 %collective-permute-start.13 = (f32[48,384]{1,0:T(8,128)S(1)}, f32[48,384]{1,0:T(8,128)S(1)}, u32[]{:S(2)}, u32[]{:S(2)}) collective-permute-start(f32[48,384]{1,0:T(8,128)S(1)} %get-tuple-element.178), channel_id=1, source_target_pairs={{0,2},{1,3},{2,0},{3,1},{4,6},{5,7},{6,4},{7,5},{8,10},{9,11},{10,... | collective-permute-start | bytes 221192 | tf_op jit(solution)/shard_map/cond/branch_1_fun/ppermute | solution.py:21
  60.1 4.4 %collective-permute-start.12 = (f32[48,384]{1,0:T(8,128)S(1)}, f32[48,384]{1,0:T(8,128)S(1)}, u32[]{:S(2)}, u32[]{:S(2)}) collective-permute-start(f32[48,384]{1,0:T(8,128)S(1)} %get-tuple-element.177), channel_id=1, source_target_pairs={{0,4},{1,5},{2,6},{3,7},{4,0},{5,1},{6,2},{7,3},{8,12},{9,13},{10,... | collective-permute-start | bytes 221192 | tf_op jit(solution)/shard_map/cond/branch_1_fun/ppermute | solution.py:21
  63.5 0.9 copy-start.51
  64.3 0.6 copy-start.52
  64.4 0.6 copy-start.53
  66.7 25.4 %copy-start.13 = (f32[48,384]{1,0:T(8,128)S(1)}, f32[48,384]{1,0:T(8,128)}, u32[]{:S(2)}) copy-start(f32[48,384]{1,0:T(8,128)} %branch_1_fun.9.refs_0_) | copy-start | bytes 221188 | tf_op jit(solution)/shard_map/cond
  66.7 18.5 %collective-permute-start.15 = (f32[1536,128]{1,0:T(8,128)}, f32[1536,128]{1,0:T(8,128)S(1)}, u32[]{:S(2)}, u32[]{:S(2)}) collective-permute-start(f32[1536,128]{1,0:T(8,128)} %get-tuple-element.180), channel_id=1, source_target_pairs={{0,2},{1,3},{2,0},{3,1},{4,6},{5,7},{6,4},{7,5},{8,10},{9,11},{10,... | collective-permute-start | bytes 2359304 | tf_op jit(solution)/shard_map/cond/branch_1_fun/ppermute | solution.py:21
  70.7 6.9 %collective-permute-start.8 = (f32[72,384]{1,0:T(8,128)}, f32[72,384]{1,0:T(8,128)S(1)}, u32[]{:S(2)}, u32[]{:S(2)}) collective-permute-start(f32[72,384]{1,0:T(8,128)} %branch_1_fun.6.refs_0_), channel_id=1, source_target_pairs={{0,24},{1,25},{2,26},{3,27},{4,28},{5,29},{6,30},{7,31},{8,16},{9,... | collective-permute-start | bytes 331784 | tf_op jit(solution)/shard_map/cond/branch_1_fun/ppermute | solution.py:21
  73.2 7.2 %collective-permute-start.7 = (f32[72,384]{1,0:T(8,128)}, f32[72,384]{1,0:T(8,128)S(1)}, u32[]{:S(2)}, u32[]{:S(2)}) collective-permute-start(f32[72,384]{1,0:T(8,128)} %branch_1_fun.6.refs_0_), channel_id=1, source_target_pairs={{0,16},{1,17},{2,18},{3,19},{4,20},{5,21},{6,22},{7,23},{8,24},{9,... | collective-permute-start | bytes 331784 | tf_op jit(solution)/shard_map/cond/branch_1_fun/ppermute | solution.py:21
  73.9 6.5 %collective-permute-start.6 = (f32[72,384]{1,0:T(8,128)}, f32[72,384]{1,0:T(8,128)S(1)}, u32[]{:S(2)}, u32[]{:S(2)}) collective-permute-start(f32[72,384]{1,0:T(8,128)} %branch_1_fun.6.refs_0_), channel_id=1, source_target_pairs={{0,8},{1,9},{2,10},{3,11},{4,12},{5,13},{6,14},{7,15},{8,0},{9,1},... | collective-permute-start | bytes 331784 | tf_op jit(solution)/shard_map/cond/branch_1_fun/ppermute | solution.py:21
  77.5 2.8 %copy-start.31 = (f32[72,384]{1,0:T(8,128)}, f32[72,384]{1,0:T(8,128)S(1)}, u32[]{:S(2)}) copy-start(f32[72,384]{1,0:T(8,128)S(1)} %collective-permute-done.8.refs_3_) | copy-start | bytes 331780 | tf_op jit(solution)/shard_map/cond
  80.4 0.6 copy-start.35
  81.0 0.6 copy-start.39
  83.6 8.5 %collective-permute-start.9 = (f32[288,384]{1,0:T(8,128)}, f32[288,384]{1,0:T(8,128)S(1)}, u32[]{:S(2)}, u32[]{:S(2)}) collective-permute-start(f32[288,384]{1,0:T(8,128)} %branch_1_fun.7.keep), channel_id=1, source_target_pairs={{0,4},{1,5},{2,6},{3,7},{4,0},{5,1},{6,2},{7,3},{8,12},{9,13},{10,... | collective-permute-start | bytes 1327112 | tf_op jit(solution)/shard_map/cond/branch_1_fun/ppermute | solution.py:21
  85.1 38.5 %copy-start.1 = (f32[1536,128]{1,0:T(8,128)}, f32[1536,128]{1,0:T(8,128)S(1)}, u32[]{:S(2)}) copy-start(f32[1536,128]{1,0:T(8,128)S(1)} %collective-permute-done.15.far) | copy-start | bytes 2359300 | tf_op jit(solution)/shard_map/cond
  85.1 38.6 %collective-permute-start.16 = (f32[1536,128]{1,0:T(8,128)S(1)}, f32[1536,128]{1,0:T(8,128)}, u32[]{:S(2)}, u32[]{:S(2)}) collective-permute-start(f32[1536,128]{1,0:T(8,128)S(1)} %collective-permute-done.15.far), channel_id=1, source_target_pairs={{0,1},{1,0},{2,3},{3,2},{4,5},{5,4},{6,7},{7,6},{8,9},{9,8},{10,11... | collective-permute-start | bytes 2359304 | tf_op jit(solution)/shard_map/cond/branch_1_fun/ppermute | solution.py:21
  85.1 30.9 %collective-permute-start.10 = (f32[288,384]{1,0:T(8,128)}, f32[288,384]{1,0:T(8,128)}, u32[]{:S(2)}, u32[]{:S(2)}) collective-permute-start(f32[288,384]{1,0:T(8,128)} %branch_1_fun.7.keep), channel_id=1, source_target_pairs={{0,1},{1,0},{2,3},{3,2},{4,5},{5,4},{6,7},{7,6},{8,9},{9,8},{10,11... | collective-permute-start | bytes 1327112 | tf_op jit(solution)/shard_map/cond/branch_1_fun/ppermute | solution.py:21
  92.1 24.6 %copy-start.62 = (f32[288,384]{1,0:T(8,128)}, f32[288,384]{1,0:T(8,128)S(1)}, u32[]{:S(2)}) copy-start(f32[288,384]{1,0:T(8,128)S(1)} %collective-permute-done.9.other) | copy-start | bytes 1327108 | tf_op jit(solution)/shard_map/cond
  92.1 24.5 %collective-permute-start.11 = (f32[288,384]{1,0:T(8,128)S(1)}, f32[288,384]{1,0:T(8,128)}, u32[]{:S(2)}, u32[]{:S(2)}) collective-permute-start(f32[288,384]{1,0:T(8,128)S(1)} %collective-permute-done.9.other), channel_id=1, source_target_pairs={{0,1},{1,0},{2,3},{3,2},{4,5},{5,4},{6,7},{7,6},{8,9},{9,8},{10,11... | collective-permute-start | bytes 1327112 | tf_op jit(solution)/shard_map/cond/branch_1_fun/ppermute | solution.py:21
  92.1 7.1 %collective-permute-start.19 = (f32[48,384]{1,0:T(8,128)S(1)}, f32[48,384]{1,0:T(8,128)S(1)}, u32[]{:S(2)}, u32[]{:S(2)}) collective-permute-start(f32[48,384]{1,0:T(8,128)S(1)} %copy-done.13), channel_id=1, source_target_pairs={{0,24},{1,25},{2,26},{3,27},{4,28},{5,29},{6,30},{7,31},{8,16},{9,... | collective-permute-start | bytes 221192 | tf_op jit(solution)/shard_map/cond/branch_1_fun/ppermute | solution.py:21
  94.6 7.2 %collective-permute-start.18 = (f32[48,384]{1,0:T(8,128)S(1)}, f32[48,384]{1,0:T(8,128)S(1)}, u32[]{:S(2)}, u32[]{:S(2)}) collective-permute-start(f32[48,384]{1,0:T(8,128)S(1)} %copy-done.13), channel_id=1, source_target_pairs={{0,16},{1,17},{2,18},{3,19},{4,20},{5,21},{6,22},{7,23},{8,24},{9,... | collective-permute-start | bytes 221192 | tf_op jit(solution)/shard_map/cond/branch_1_fun/ppermute | solution.py:21
  99.2 4.4 %copy-start.45 = (f32[48,384]{1,0:T(8,128)}, f32[48,384]{1,0:T(8,128)S(1)}, u32[]{:S(2)}) copy-start(f32[48,384]{1,0:T(8,128)S(1)} %collective-permute-done.19.refs_3_) | copy-start | bytes 221188 | tf_op jit(solution)/shard_map/cond
  99.2 4.4 %collective-permute-start.17 = (f32[48,384]{1,0:T(8,128)S(1)}, f32[48,384]{1,0:T(8,128)S(1)}, u32[]{:S(2)}, u32[]{:S(2)}) collective-permute-start(f32[48,384]{1,0:T(8,128)S(1)} %copy-done.13), channel_id=1, source_target_pairs={{0,8},{1,9},{2,10},{3,11},{4,12},{5,13},{6,14},{7,15},{8,0},{9,1},... | collective-permute-start | bytes 221192 | tf_op jit(solution)/shard_map/cond/branch_1_fun/ppermute | solution.py:21
  101.8 1.7 %copy-start.47 = (f32[48,384]{1,0:T(8,128)}, f32[48,384]{1,0:T(8,128)S(1)}, u32[]{:S(2)}) copy-start(f32[48,384]{1,0:T(8,128)S(1)} %collective-permute-done.18.refs_2_) | copy-start | bytes 221188 | tf_op jit(solution)/shard_map/cond
  103.5 0.6 copy-start.49
  106.0 5.5 %collective-permute-start.22 = (f32[48,384]{1,0:T(8,128)}, f32[48,384]{1,0:T(8,128)S(1)}, u32[]{:S(2)}, u32[]{:S(2)}) collective-permute-start(f32[48,384]{1,0:T(8,128)} %branch_1_fun.10.rest_0_), channel_id=1, source_target_pairs={{0,6},{1,7},{2,4},{3,5},{4,2},{5,3},{6,0},{7,1},{8,14},{9,15},{10,... | collective-permute-start | bytes 221192 | tf_op jit(solution)/shard_map/cond/branch_1_fun/ppermute | solution.py:21
  107.4 5.7 %collective-permute-start.21 = (f32[48,384]{1,0:T(8,128)}, f32[48,384]{1,0:T(8,128)S(1)}, u32[]{:S(2)}, u32[]{:S(2)}) collective-permute-start(f32[48,384]{1,0:T(8,128)} %branch_1_fun.10.rest_0_), channel_id=1, source_target_pairs={{0,2},{1,3},{2,0},{3,1},{4,6},{5,7},{6,4},{7,5},{8,10},{9,11},{10,... | collective-permute-start | bytes 221192 | tf_op jit(solution)/shard_map/cond/branch_1_fun/ppermute | solution.py:21
  111.5 12.1 %copy-start.54 = (f32[48,384]{1,0:T(8,128)}, f32[48,384]{1,0:T(8,128)S(1)}, u32[]{:S(2)}) copy-start(f32[48,384]{1,0:T(8,128)S(1)} %collective-permute-done.22.rest_3_) | copy-start | bytes 221188 | tf_op jit(solution)/shard_map/cond
  111.5 4.6 %collective-permute-start.20 = (f32[48,384]{1,0:T(8,128)}, f32[48,384]{1,0:T(8,128)S(1)}, u32[]{:S(2)}, u32[]{:S(2)}) collective-permute-start(f32[48,384]{1,0:T(8,128)} %branch_1_fun.10.rest_0_), channel_id=1, source_target_pairs={{0,4},{1,5},{2,6},{3,7},{4,0},{5,1},{6,2},{7,3},{8,12},{9,13},{10,... | collective-permute-start | bytes 221192 | tf_op jit(solution)/shard_map/cond/branch_1_fun/ppermute | solution.py:21
  113.1 10.4 %copy-start.55 = (f32[48,384]{1,0:T(8,128)}, f32[48,384]{1,0:T(8,128)S(1)}, u32[]{:S(2)}) copy-start(f32[48,384]{1,0:T(8,128)S(1)} %collective-permute-done.21.rest_2_) | copy-start | bytes 221188 | tf_op jit(solution)/shard_map/cond
  113.1 10.5 %collective-permute-start.23 = (f32[48,384]{1,0:T(8,128)}, f32[48,384]{1,0:T(8,128)S(1)}, u32[]{:S(2)}, u32[]{:S(2)}) collective-permute-start(f32[48,384]{1,0:T(8,128)} %branch_1_fun.10.rest_0_), channel_id=1, source_target_pairs={{0,1},{1,0},{2,3},{3,2},{4,5},{5,4},{6,7},{7,6},{8,9},{9,8},{10,11... | collective-permute-start | bytes 221192 | tf_op jit(solution)/shard_map/cond/branch_1_fun/ppermute | solution.py:21
  116.0 7.5 %copy-start.56 = (f32[48,384]{1,0:T(8,128)}, f32[48,384]{1,0:T(8,128)S(1)}, u32[]{:S(2)}) copy-start(f32[48,384]{1,0:T(8,128)S(1)} %collective-permute-done.20.rest_1_) | copy-start | bytes 221188 | tf_op jit(solution)/shard_map/cond
  116.0 7.6 %collective-permute-start.26 = (f32[48,384]{1,0:T(8,128)S(1)}, f32[48,384]{1,0:T(8,128)S(1)}, u32[]{:S(2)}, u32[]{:S(2)}) collective-permute-start(f32[48,384]{1,0:T(8,128)S(1)} %collective-permute-done.22.rest_3_), channel_id=1, source_target_pairs={{0,1},{1,0},{2,3},{3,2},{4,5},{5,4},{6,7},{7,6},{8,9},{9,8},{10,11... | collective-permute-start | bytes 221192 | tf_op jit(solution)/shard_map/cond/branch_1_fun/ppermute | solution.py:21
  116.1 7.6 %collective-permute-start.25 = (f32[48,384]{1,0:T(8,128)S(1)}, f32[48,384]{1,0:T(8,128)S(1)}, u32[]{:S(2)}, u32[]{:S(2)}) collective-permute-start(f32[48,384]{1,0:T(8,128)S(1)} %collective-permute-done.21.rest_2_), channel_id=1, source_target_pairs={{0,1},{1,0},{2,3},{3,2},{4,5},{5,4},{6,7},{7,6},{8,9},{9,8},{10,11... | collective-permute-start | bytes 221192 | tf_op jit(solution)/shard_map/cond/branch_1_fun/ppermute | solution.py:21
  116.6 7.1 %collective-permute-start.24 = (f32[48,384]{1,0:T(8,128)S(1)}, f32[48,384]{1,0:T(8,128)S(1)}, u32[]{:S(2)}, u32[]{:S(2)}) collective-permute-start(f32[48,384]{1,0:T(8,128)S(1)} %collective-permute-done.20.rest_1_), channel_id=1, source_target_pairs={{0,1},{1,0},{2,3},{3,2},{4,5},{5,4},{6,7},{7,6},{8,9},{9,8},{10,11... | collective-permute-start | bytes 221192 | tf_op jit(solution)/shard_map/cond/branch_1_fun/ppermute | solution.py:21
  123.6 0.6 copy-start.57
  123.6 0.7 copy-start.58
  123.6 0.7 copy-start.59
  123.7 0.7 copy-start.60
where the time goes:
time: 130 us; the launch traced here: 128 us
  waiting for transfers between devices  53.5 us (41%)
  Pallas kernels  31.3 us (24%)
  starting transfers between devices  30.9 us (24%)
  local copies, waits for them, and re-layouts  7.18 us (6%)
  between operations  2.65 us (2%)
  other arithmetic  2.06 us (2%)
    ppermute x31, waiting for transfers between devices, across(): return lax.ppermute(value, AXES, moves)  53.5 us
    pallas_call x10, Pallas kernels, call(): pl.pallas_call(kernel, out_shape=outs, in_specs=[IN_SMEM if i in in_smem...  31.3 us
    ppermute x31, starting transfers between devices, across(): return lax.ppermute(value, AXES, moves)  30.9 us
    cond x40, local copies, waits for them, and re-layouts  3.23 us
  transfers between devices with their start and end apart: 31, of which 14 were waited for; matrix products, arithmetic and copies ran while one was open for 4% of the time, Pallas kernels for 21%

commit v1 on v0

--- a/solution.py
+++ b/solution.py
@@ -181,6 +181,7 @@
 SLOTS = (1, 2, 4)
 WHOLE_SLOTS = 2
 STEP = 512
+SPARE_BYTES = 2 << 20
 
 
 def dot_tn(left, right):
@@ -204,14 +205,17 @@
 
 def call(kernel, outs, args, in_smem=(), scratch=(), flops=0):
     outs = [jax.ShapeDtypeStruct(o[:2], o[2] if len(o) > 2 else jnp.float32) for o in outs]
+    scratch = [jax.ShapeDtypeStruct(*s) for s in scratch]
     moved = sum(a.size * a.dtype.itemsize for a in (*args, *outs))
+    held = moved + sum(s.size * s.dtype.itemsize for s in scratch)
     return pl.pallas_call(
         kernel,
         out_shape=outs,
         in_specs=[IN_SMEM if i in in_smem else IN_VMEM for i in range(len(args))],
         out_specs=[IN_VMEM for _ in outs],
-        scratch_shapes=list(scratch),
+        scratch_shapes=[pltpu.VMEM(s.shape, s.dtype) for s in scratch],
         cost_estimate=pl.CostEstimate(flops=flops, bytes_accessed=moved, transcendentals=0),
+        compiler_params=pltpu.CompilerParams(vmem_limit_bytes=held + SPARE_BYTES),
     )(*args)
 
 
@@ -227,29 +231,16 @@
             low_ref[where, c * LANES:(c + 1) * LANES] = low
 
 
-def half_rows(left, right, lane, chunks, spare, store):
-    full = chunks // 2
-
-    def product(chunk):
-        where = pl.ds(pl.multiple_of(chunk * LANES, LANES), LANES)
-        lt, ll = left[0][:, where], left[1][:, where]
-        rt, rl = right[0][...], right[1][...]
-        return dot_tn(lt, rt) + (dot_tn(lt, rl) + dot_tn(ll, rt))
-
-    for t in range(full):
-        store(t * LANES, LANES, product(lane * (chunks - full) + t))
-    if chunks % 2:
-        spare[...] = product(full)
-        part = LANES // 2
-        store(full * LANES, part, spare[pl.ds(pl.multiple_of(lane * part, part), part), :])
-
-
-def row_origin(row, lane, chunks):
-    full = chunks // 2
-    whole = full * LANES
-    return jnp.where(
-        row < whole, lane * (chunks - full) * LANES + row,
-        full * LANES + lane * (LANES // 2) + row - whole)
+def half_rows(left, right, lane, chunks, spare):
+    virt = chunks * LANES
+    width = -(-chunks // 2) * LANES
+    begin = lane * (chunks // 2) * LANES
+    where = pl.ds(pl.multiple_of(begin, LANES), width)
+    lt, ll = left[0][:, where], left[1][:, where]
+    rt, rl = right[0][...], right[1][...]
+    spare[...] = (dot_tn(rt, lt) + (dot_tn(rt, ll) + dot_tn(rl, lt))).T
+    skip = lane * (virt // 2) - begin
+    return spare[pl.ds(pl.multiple_of(skip, 8), virt // 2), :]
 
 
 def own_kernel(rows, chunks, own, keep, send, top, low, acc, cross):
@@ -265,16 +256,12 @@
 def twin_kernel(rows, chunks, own_top, own_low, twin, keep, send, top, low, acc, spare):
     x, _, _, lane, _ = spots()
     unpack(twin, rows, chunks, top, low)
-
-    def store(first, count, value):
-        acc[first:first + count, :] = value
-
     own, other = (own_top, own_low), (top, low)
     for here, left, right in ((0, own, other), (1, other, own)):
 
         @pl.when(lane == here)
         def _(here=here, left=left, right=right):
-            half_rows(left, right, here, chunks, spare, store)
+            acc[...] = half_rows(left, right, here, chunks, spare)
 
     size = keep.shape[0]
     keep[...] = acc[pl.ds(pl.multiple_of(x * size, 8), size), :]
@@ -318,13 +305,9 @@
         def _(number=number, slots=slots):
             for slot in range(slots):
                 first, second, _ = side_pair(mask, slot, slots)
-
-                def store(start, count, value, slot=slot):
-                    at = slot * virt // 2 + start
-                    acc[at:at + count, :] = value
-
-                half_rows((top.at[first], low.at[first]), (top.at[second], low.at[second]),
-                          lane, chunks, spare, store)
+                acc[slot * virt // 2:(slot + 1) * virt // 2, :] = half_rows(
+                    (top.at[first], low.at[first]), (top.at[second], low.at[second]),
+                    lane, chunks, spare)
             mine = outs[4 * number:4 * number + 4]
             size = mine[0].shape[0]
             for step in range(4):
@@ -381,7 +364,7 @@
             if mixed:
                 row = (x * members + z) * (size - own_size) + row - own_size
                 first, second = 2 * side, 2 * side + 1
-                origin = row_origin(row, lane, chunks)
+                origin = lane * (virt // 2) + row
             else:
                 origin = (x * members + z) * own_size + row
                 first = second = pair
@@ -395,7 +378,7 @@
                 first = jnp.where(here, f, first)
                 second = jnp.where(here, s, second)
                 weight = jnp.where(here, w, weight)
-            origin = row_origin(row % (virt // 2), lane, chunks)
+            origin = lane * (virt // 2) + row % (virt // 2)
         here = slice(group * 8, group * 8 + 8)
         total = ins[0][here, :]
         for other in ins[1:]:
@@ -406,15 +389,9 @@
 
 
 def place_block(halves_ref, first, chunks, whole):
-    full = chunks // 2
-    part = LANES // 2
+    part = chunks * LANES // 2
     for lane in range(2):
-        at = lane * (chunks - full) * LANES
-        whole[at:at + full * LANES, :] = halves_ref[lane, pl.ds(first, full * LANES), :]
-        if chunks % 2:
-            at = full * LANES + lane * part
-            whole[at:at + part, :] = halves_ref[
-                lane, pl.ds(first + full * LANES, part), :]
+        whole[lane * part:(lane + 1) * part, :] = halves_ref[lane, pl.ds(first, part), :]
 
 
 def wide(top, low):
@@ -526,6 +503,14 @@
                 pl.ds(pl.multiple_of(at, step), step), c * LANES:(c + 1) * LANES]
 
 
+def pick_branch(pair_mask):
+    live = jnp.sum((pair_mask[:2, 2:] > 0).astype(jnp.int32))
+    branch = jnp.int32(0)
+    for slots in (0, *SLOTS[:-1]):
+        branch = branch + (live > slots).astype(jnp.int32)
+    return branch
+
+
 def opening(three_center, occ_energy, pair_mask):
     rows, _, virt = three_center.shape
     chunks = virt // LANES
@@ -541,22 +526,28 @@
     twin = across(own, 0, 1)
     split = [(rows, virt, bf16)] * 2
     mixed_rows = virt // 2
+    keep_a, send_a, own_top, own_low = call(
+        functools.partial(own_kernel, rows, chunks), [(virt // 2, virt)] * 2 + split, [own],
+        scratch=[((virt, virt), f32)] * 2, flops=block_flops)
+    got_a = across(send_a, 1, 0)
+    twin, send_a = lax.optimization_barrier((twin, send_a))
+    keep_b, send_b, twin_top, twin_low = call(
+        functools.partial(twin_kernel, rows, chunks), [(mixed_rows // 2, virt)] * 2 + split,
+        [own_top, own_low, twin],
+        scratch=[((mixed_rows, virt), f32), ((-(-chunks // 2) * LANES, virt), f32)],
+        flops=block_flops)
+    got_b = across(send_b, 1, 0)
+    occ_energy, send_b = lax.optimization_barrier((occ_energy, send_b))
+    got_a, later_mask = lax.optimization_barrier((got_a, pair_mask))
+    branch = pick_branch(later_mask)
     occ_side = jnp.concatenate([occ_energy, across(occ_energy, 0, 1)])
     occ_side = jnp.where(lane == 0, occ_side, occ_side[::-1])
     occ_other = across(occ_side, 0, 2)
     occ = jnp.where(side == 0, jnp.concatenate([occ_side, occ_other]),
                     jnp.concatenate([occ_other, occ_side]))
-    keep_a, send_a, own_top, own_low = call(
-        functools.partial(own_kernel, rows, chunks), [(virt // 2, virt)] * 2 + split, [own],
-        scratch=[pltpu.VMEM((virt, virt), f32)] * 2, flops=block_flops)
-    got_a = across(send_a, 1, 0)
-    twin, send_a = lax.optimization_barrier((twin, send_a))
-    keep_b, send_b, twin_top, twin_low = call(
-        functools.partial(twin_kernel, rows, chunks), [(mixed_rows // 2, virt)] * 2 + split,
-        [own_top, own_low, twin],
-        scratch=[pltpu.VMEM((mixed_rows, virt), f32), pltpu.VMEM((LANES, virt), f32)],
-        flops=block_flops)
-    got_b = across(send_b, 1, 0)
+    later_own, _ = lax.optimization_barrier((own, send_b))
+    far_send = pick(later_own.reshape(2, half * chunks, LANES), side)
+    keep_a, branch, far_send = lax.optimization_barrier((keep_a, branch, far_send))
     piece_rows = (virt + mixed_rows) // 2 // z_count
     pieces = call(functools.partial(add_kernel, 2, 2), [(piece_rows, virt)] * z_count,
                    [keep_a, got_a, keep_b, got_b])
@@ -567,14 +558,13 @@
         functools.partial(cross_kernel, half, chunks),
         [(n * mixed_rows // 4, virt) for n in SLOTS for _ in range(4)] + split,
         [pair_mask, own_top, own_low, twin_top, twin_low, near, near_t], in_smem=(0,),
-        scratch=[pltpu.VMEM((4, half, virt), bf16)] * 2 + [
-            pltpu.VMEM((most, virt), f32), pltpu.VMEM((LANES, virt), f32)],
+        scratch=[((4, half, virt), bf16)] * 2 + [
+            ((most, virt), f32), ((-(-chunks // 2) * LANES, virt), f32)],
         flops=block_flops)
     cross, faces = cross[:-2], cross[-2:]
-    far_send = pick(flat_pieces, side)
     return lax.optimization_barrier((
         (own_top, own_low, twin_top, twin_low), faces, far_send, occ,
-        [pieces[0], *side_got], cross))
+        [pieces[0], *side_got], cross)), branch
 
 
 def closing(slots, shape, opened, vir_row, vir_col, pair_mask):
@@ -592,8 +582,13 @@
     slab_rows = square_rows // z_count
     flips = [(0, 0), (1, 0), (0, 2), (1, 2)]
 
-    def z_spread(slab):
-        return [across(slab, s << 1, 0) for s in range(1, z_count)]
+    def z_spread(slab, relay):
+        got = {0: slab}
+        for s in range(1, z_count):
+            direct = s & (s - 1) == 0 or not relay
+            got[s] = across(got[0 if direct else s & (s - 1)],
+                           (s if direct else s & -s) << 1, 0)
+        return [got[s] for s in range(1, z_count)]
 
     if slots:
         at = 4 * SLOTS.index(slots)
@@ -602,7 +597,7 @@
     slab, = call(
         functools.partial(scale_kernel, chunks, 0, z_count, True),
         [(piece_rows, virt)], [*energies, *side_parts], in_smem=(0, 1))
-    side_slabs = [slab] + z_spread(slab)
+    side_slabs = [slab] + z_spread(slab, False)
     joined, = call(
         functools.partial(join_kernel, (own_size, piece_rows - own_size)),
         [(piece_rows * z_count, virt)], side_slabs)
@@ -612,15 +607,15 @@
     gamma, = call(
         functools.partial(near_gamma_kernel, rows, chunks), [(rows, virt)],
         [*splits, joined, other, joined_t, other_t],
-        scratch=[pltpu.VMEM((2, virt + virt // 2, virt), f32), pltpu.VMEM((virt, virt), f32),
-                 pltpu.VMEM((2, 3 * virt, virt), bf16)], flops=2 * block_flops)
+        scratch=[((2, virt + virt // 2, virt), f32), ((virt, virt), f32),
+                 ((2, 3 * virt, virt), bf16)], flops=2 * block_flops)
     if not slots:
         gamma, = call(functools.partial(flat_kernel, rows, chunks), [(rows * chunks, LANES)],
                       [gamma])
         return gamma
     if slots <= WHOLE_SLOTS:
         summed, = call(sum_kernel, [(square_rows, virt)], [cross[0], *cross_got])
-        z_got = z_spread(summed)
+        z_got = z_spread(summed, True)
         joined_c, = call(
             functools.partial(scale_kernel, chunks, slots, z_count, False),
             [(square_rows, virt)], [*energies, summed, *z_got], in_smem=(0, 1))
@@ -635,7 +630,7 @@
             [(slab_rows, virt)], [*energies, pieces_c[0], *z_got], in_smem=(0, 1))
         joined_c, = call(
             functools.partial(join_kernel, (slab_rows,)), [(square_rows, virt)],
-            [cross_slab] + z_spread(cross_slab))
+            [cross_slab] + z_spread(cross_slab, False))
     far_send, summed = lax.optimization_barrier((far_send, summed))
     far = across(far_send, 0, 2)
     far_t = across(far, 0, 1)
@@ -647,8 +642,8 @@
         [(rows * chunks, LANES)],
         [pair_mask, gamma, *faces, far, far_t, joined_c, *whole, joined_ct, *whole_t],
         in_smem=(0,),
-        scratch=[pltpu.VMEM((2, total_rows, virt), f32), pltpu.VMEM((virt, virt), f32),
-                 pltpu.VMEM((3 * virt, virt), bf16), pltpu.VMEM((rows, virt), f32)],
+        scratch=[((2, total_rows, virt), f32), ((virt, virt), f32),
+                 ((3 * virt, virt), bf16), ((rows, virt), f32)],
         flops=2 * block_flops)
     return gamma
 
@@ -664,11 +659,7 @@
     args = (three_center, occ_energy, vir_energy, pair_mask)
     if not fits:
         return general_path(*args)
-    live = jnp.sum((pair_mask[:2, 2:] > 0).astype(jnp.int32))
-    branch = jnp.int32(0)
-    for slots in (0, *SLOTS[:-1]):
-        branch = branch + (live > slots).astype(jnp.int32)
-    opened = opening(three_center, occ_energy, pair_mask)
+    opened, branch = opening(three_center, occ_energy, pair_mask)
     gamma = lax.switch(
         branch, [functools.partial(closing, n, three_center.shape)
                  for n in (0, *SLOTS)],

time: 130 us -> 122 us (0.938)
  Pallas kernels: 31.3 us -> 17.9 us
  waiting for transfers between devices: 53.5 us -> 62.2 us
  local copies, waits for them, and re-layouts: 7.18 us -> 2.43 us
  starting transfers between devices: 30.9 us -> 32.8 us
    pallas_call x10, Pallas kernels: 31.3 us -> 17.9 us  [call(): pl.pallas_call(kernel, out_shape=outs, in_specs=[IN_SMEM if i in in_smem...]
    ppermute x31, waiting for transfers between devices: 53.5 us -> 62.2 us  [across(): return lax.ppermute(value, AXES, moves)]
    cond x40 -> x10, local copies, waits for them, and re-layouts: 3.23 us -> 0.02 us
    ppermute x31, starting transfers between devices: 30.9 us -> 32.8 us  [across(): return lax.ppermute(value, AXES, moves)]
  transfers between devices with their start and end apart: 31 -> 31, of which waited for: 14 -> 17; matrix products, arithmetic and copies ran while one was open for 4% -> 4% of each run, Pallas kernels for 21% -> 13%
where the time goes in v1:
time: 122 us; the launch traced here: 121 us
  waiting for transfers between devices  62.2 us (51%)
  starting transfers between devices  32.8 us (27%)
  Pallas kernels  17.9 us (15%)
  between operations  2.71 us (2%)
  local copies, waits for them, and re-layouts  2.43 us (2%)
  other arithmetic  2.27 us (2%)
    ppermute x31, waiting for transfers between devices, across(): return lax.ppermute(value, AXES, moves)  62.2 us
    ppermute x31, starting transfers between devices, across(): return lax.ppermute(value, AXES, moves)  32.8 us
    pallas_call x10, Pallas kernels, call(): pl.pallas_call(kernel, out_shape=outs, in_specs=[IN_SMEM if i in in_smem...  17.9 us
  transfers between devices with their start and end apart: 31, of which 17 were waited for; matrix products, arithmetic and copies ran while one was open for 4% of the time, Pallas kernels for 13%

profile of v1, /device:TPU:0, one launch (start us, length us, event | category | flops | bytes accessed | tf_op | source)
XLA Modules:
  0.0 120.5 jit_solution(16436292185459030879)
XLA Ops:
  0.0 0.5 collective-permute-start.73
  0.5 1.2 dynamic-slice_bitcast_fusion
  1.7 0.0 copy-start.19
  1.7 2.7 %collective-permute-start.74 = (f32[1536,128]{1,0:T(8,128)S(1)}, f32[1536,128]{1,0:T(8,128)S(1)}, u32[]{:S(2)}, u32[]{:S(2)}) collective-permute-start(f32[1536,128]{1,0:T(8,128)S(1)} %dynamic-slice_bitcast_fusion), channel_id=1, source_target_pairs={{0,2},{1,3},{2,0},{3,1},{4,6},{5,7},{6,4},{7,5},{8,10},{9,11},{10,... | collective-permute-start | bytes 2359304 | tf_op jit(solution)/shard_map/ppermute | solution.py:21
  4.4 18.1 %collective-permute-done.74.face = f32[1536,128]{1,0:T(8,128)S(1)} collective-permute-done((f32[1536,128]{1,0:T(8,128)S(1)}, f32[1536,128]{1,0:T(8,128)S(1)}, u32[]{:S(2)}, u32[]{:S(2)}) %collective-permute-start.74) | collective-permute-done | bytes 786464 | tf_op jit(solution)/shard_map/ppermute | solution.py:21
  22.5 2.1 %shard_map.50 = (f32[192,384]{1,0:T(8,128)S(1)}, f32[192,384]{1,0:T(8,128)}, bf16[1024,384]{1,0:T(8,128)(2,1)}, bf16[1024,384]{1,0:T(8,128)(2,1)}) custom-call(f32[3072,128]{1,0:T(8,128)S(1)} %bitcast.13), custom_call_target="tpu_custom_call" | custom-call | flops 905969664 | bytes 3735552 | tf_op jit(solution)/shard_map/pallas_call | solution.py:211
  24.5 1.7 %collective-permute-start.72 = (f32[192,384]{1,0:T(8,128)}, f32[192,384]{1,0:T(8,128)}, u32[]{:S(2)}, u32[]{:S(2)}) collective-permute-start(f32[192,384]{1,0:T(8,128)} %get-tuple-element.283), channel_id=1, source_target_pairs={{0,4},{1,5},{2,6},{3,7},{4,0},{5,1},{6,2},{7,3},{8,12},{9,13},{10,... | collective-permute-start | bytes 884744 | tf_op jit(solution)/shard_map/ppermute | solution.py:21
  26.9 1.0 dynamic-slice_bitcast_fusion.1
  27.9 6.4 %collective-permute-done.72.refs_1_ = f32[192,384]{1,0:T(8,128)} collective-permute-done((f32[192,384]{1,0:T(8,128)}, f32[192,384]{1,0:T(8,128)}, u32[]{:S(2)}, u32[]{:S(2)}) %collective-permute-start.72) | collective-permute-done | bytes 294944 | tf_op jit(solution)/shard_map/ppermute | solution.py:21
  34.3 0.7 fusion
  37.0 3.2 %shard_map.51 = (f32[96,384]{1,0:T(8,128)S(1)}, f32[96,384]{1,0:T(8,128)S(1)}, bf16[1024,384]{1,0:T(8,128)(2,1)S(1)}, bf16[1024,384]{1,0:T(8,128)(2,1)S(1)}) custom-call(bf16[1024,384]{1,0:T(8,128)(2,1)} %get-tuple-element.320.own_top, bf16[1024,384]{1,0:T(8,128)(2,1)} %get-tuple-element.321.own_low, f32[3072,128]{1,0:T(8,128)} %collective-permute-done.73.twin), custom_call_target="tpu_custom_call" | custom-call | flops 905969664 | bytes 5013504 | tf_op jit(solution)/shard_map/pallas_call | solution.py:211
  40.2 1.8 %collective-permute-start.78 = (f32[96,384]{1,0:T(8,128)S(1)}, f32[96,384]{1,0:T(8,128)S(1)}, u32[]{:S(2)}, u32[]{:S(2)}) collective-permute-start(f32[96,384]{1,0:T(8,128)S(1)} %get-tuple-element.294), channel_id=1, source_target_pairs={{0,4},{1,5},{2,6},{3,7},{4,0},{5,1},{6,2},{7,3},{8,12},{9,13},{10,... | collective-permute-start | bytes 442376 | tf_op jit(solution)/shard_map/ppermute | solution.py:21
  42.0 0.0 collective-permute-start.76
  42.0 0.0 collective-permute-done.75.face_twin
  42.0 3.5 %shard_map.52 = (f32[48,384]{1,0:T(8,128)S(1)}, f32[48,384]{1,0:T(8,128)S(1)}, f32[48,384]{1,0:T(8,128)S(1)}, f32[48,384]{1,0:T(8,128)S(1)}, f32[96,384]{1,0:T(8...) custom-call(s32[4,4]{1,0:T(4,128)S(1)} %copy-done.18, ...), custom_call_target="tpu_custom_call" | custom-call | flops 905969664 | bytes 8355904 | tf_op jit(solution)/shard_map/pallas_call | solution.py:211
  45.6 0.0 collective-permute-done.76
  45.6 0.7 pad_maximum_fusion
  46.3 0.1 rev.3
  46.4 0.7 broadcast_select_fusion
  47.2 1.5 %collective-permute-start.77 = (f32[2]{0:T(128)S(1)}, f32[2]{0:T(128)S(1)}, u32[]{:S(2)}, u32[]{:S(2)}) collective-permute-start(f32[2]{0:T(128)S(1)} %broadcast_select_fusion), channel_id=1, source_target_pairs={{0,2},{1,3},{2,0},{3,1},{4,6},{5,7},{6,4},{7,5},{8,10},{9,11},{10,... | collective-permute-start | bytes 32 | tf_op jit(solution)/shard_map/ppermute | solution.py:21
  48.7 1.0 shard_map.53
  49.7 1.6 %collective-permute-start.79 = (f32[72,384]{1,0:T(8,128)S(1)}, f32[72,384]{1,0:T(8,128)S(1)}, u32[]{:S(2)}, u32[]{:S(2)}) collective-permute-start(f32[72,384]{1,0:T(8,128)S(1)} %get-tuple-element.300), channel_id=1, source_target_pairs={{0,8},{1,9},{2,10},{3,11},{4,12},{5,13},{6,14},{7,15},{8,0},{9,1},... | collective-permute-start | bytes 331784 | tf_op jit(solution)/shard_map/ppermute | solution.py:21
  51.3 2.6 %collective-permute-start.80 = (f32[72,384]{1,0:T(8,128)S(1)}, f32[72,384]{1,0:T(8,128)S(1)}, u32[]{:S(2)}, u32[]{:S(2)}) collective-permute-start(f32[72,384]{1,0:T(8,128)S(1)} %get-tuple-element.301), channel_id=1, source_target_pairs={{0,16},{1,17},{2,18},{3,19},{4,20},{5,21},{6,22},{7,23},{8,24},{9,... | collective-permute-start | bytes 331784 | tf_op jit(solution)/shard_map/ppermute | solution.py:21
  53.9 0.2 collective-permute-start.81
  54.2 0.1 broadcast_select_fusion.1
  54.2 2.2 %collective-permute-done.79 = f32[72,384]{1,0:T(8,128)S(1)} collective-permute-done((f32[72,384]{1,0:T(8,128)S(1)}, f32[72,384]{1,0:T(8,128)S(1)}, u32[]{:S(2)}, u32[]{:S(2)}) %collective-permute-start.79) | collective-permute-done | bytes 110624 | tf_op jit(solution)/shard_map/ppermute | solution.py:21
  56.4 6.5 %collective-permute-done.80 = f32[72,384]{1,0:T(8,128)S(1)} collective-permute-done((f32[72,384]{1,0:T(8,128)S(1)}, f32[72,384]{1,0:T(8,128)S(1)}, u32[]{:S(2)}, u32[]{:S(2)}) %collective-permute-start.80) | collective-permute-done | bytes 110624 | tf_op jit(solution)/shard_map/ppermute | solution.py:21
  62.9 0.0 collective-permute-done.81
  62.9 57.6 %conditional.1 = (f32[1024,1,384]{2,1,0:T(1,128)}) conditional(s32[]{:T(128)} %clamp.3, (s32[4,4]{1,0:T(4,128)S(1)}, f32[4]{0:T(128)S(1)}, f32[1,384]{1,0:T(1,128)S(1)}, f32[384,1]{0,1:T(1,128)S(1)}, f32[72,384]{1,0:T(8,128)S(1)}, /*index=5*/f32[72,384]{1,0:T(8,128)S(1)}, f32[72,384]{1,0:T(8,128)S(1)}, ...), branch_computations={%region_1.2_spmd, %region_2.3_spmd, %region_3.4_spmd, %region_4.5_... | conditional | flops 3623878656 | bytes 54950140 | solution.py:663
  62.9 0.5 collective-permute-start.14
  63.4 1.5 %collective-permute-start.13 = (f32[48,384]{1,0:T(8,128)S(1)}, f32[48,384]{1,0:T(8,128)S(1)}, u32[]{:S(2)}, u32[]{:S(2)}) collective-permute-start(f32[48,384]{1,0:T(8,128)S(1)} %get-tuple-element.178), channel_id=1, source_target_pairs={{0,2},{1,3},{2,0},{3,1},{4,6},{5,7},{6,4},{7,5},{8,10},{9,11},{10,... | collective-permute-start | bytes 221192 | tf_op jit(solution)/shard_map/cond/branch_1_fun/ppermute | solution.py:21
  64.9 1.5 %collective-permute-start.12 = (f32[48,384]{1,0:T(8,128)S(1)}, f32[48,384]{1,0:T(8,128)S(1)}, u32[]{:S(2)}, u32[]{:S(2)}) collective-permute-start(f32[48,384]{1,0:T(8,128)S(1)} %get-tuple-element.177), channel_id=1, source_target_pairs={{0,4},{1,5},{2,6},{3,7},{4,0},{5,1},{6,2},{7,3},{8,12},{9,13},{10,... | collective-permute-start | bytes 221192 | tf_op jit(solution)/shard_map/cond/branch_1_fun/ppermute | solution.py:21
  66.4 1.9 %collective-permute-done.14.refs_3_ = f32[48,384]{1,0:T(8,128)S(1)} collective-permute-done((f32[48,384]{1,0:T(8,128)S(1)}, f32[48,384]{1,0:T(8,128)S(1)}, u32[]{:S(2)}, u32[]{:S(2)}) %collective-permute-start.14) | collective-permute-done | bytes 73760 | tf_op jit(solution)/shard_map/cond/branch_1_fun/ppermute | solution.py:21
  68.3 0.3 collective-permute-done.13.refs_2_
  68.5 0.7 collective-permute-done.12.refs_1_
  69.3 0.6 collective-permute-start.15
  69.9 0.1 copy.11.vir_col
  70.0 0.7 branch_1_fun.6.refs_0_
  70.7 2.5 %collective-permute-start.8 = (f32[72,384]{1,0:T(8,128)S(1)}, f32[72,384]{1,0:T(8,128)S(1)}, u32[]{:S(2)}, u32[]{:S(2)}) collective-permute-start(f32[72,384]{1,0:T(8,128)S(1)} %branch_1_fun.6.refs_0_), channel_id=1, source_target_pairs={{0,24},{1,25},{2,26},{3,27},{4,28},{5,29},{6,30},{7,31},{8,16},{9,... | collective-permute-start | bytes 331784 | tf_op jit(solution)/shard_map/cond/branch_1_fun/ppermute | solution.py:21
  73.2 0.9 collective-permute-start.7
  74.2 1.0 collective-permute-start.6
  75.2 3.1 %collective-permute-done.8.refs_3_ = f32[72,384]{1,0:T(8,128)S(1)} collective-permute-done((f32[72,384]{1,0:T(8,128)S(1)}, f32[72,384]{1,0:T(8,128)S(1)}, u32[]{:S(2)}, u32[]{:S(2)}) %collective-permute-start.8) | collective-permute-done | bytes 110624 | tf_op jit(solution)/shard_map/cond/branch_1_fun/ppermute | solution.py:21
  78.2 2.9 %collective-permute-done.7.refs_2_ = f32[72,384]{1,0:T(8,128)S(1)} collective-permute-done((f32[72,384]{1,0:T(8,128)S(1)}, f32[72,384]{1,0:T(8,128)S(1)}, u32[]{:S(2)}, u32[]{:S(2)}) %collective-permute-start.7) | collective-permute-done | bytes 110624 | tf_op jit(solution)/shard_map/cond/branch_1_fun/ppermute | solution.py:21
  81.2 1.8 %collective-permute-start.9 = (f32[288,384]{1,0:T(8,128)S(1)}, f32[288,384]{1,0:T(8,128)S(1)}, u32[]{:S(2)}, u32[]{:S(2)}) collective-permute-start(f32[288,384]{1,0:T(8,128)S(1)} %branch_1_fun.7.keep), channel_id=1, source_target_pairs={{0,4},{1,5},{2,6},{3,7},{4,0},{5,1},{6,2},{7,3},{8,12},{9,13},{10,... | collective-permute-start | bytes 1327112 | tf_op jit(solution)/shard_map/cond/branch_1_fun/ppermute | solution.py:21
  83.1 2.5 %collective-permute-done.15.far = f32[1536,128]{1,0:T(8,128)S(1)} collective-permute-done((f32[1536,128]{1,0:T(8,128)}, f32[1536,128]{1,0:T(8,128)S(1)}, u32[]{:S(2)}, u32[]{:S(2)}) %collective-permute-start.15) | collective-permute-done | bytes 786464 | tf_op jit(solution)/shard_map/cond/branch_1_fun/ppermute | solution.py:21
  85.5 0.0 collective-permute-start.16
  85.5 0.5 collective-permute-start.10
  86.0 4.3 %collective-permute-done.9.other = f32[288,384]{1,0:T(8,128)S(1)} collective-permute-done((f32[288,384]{1,0:T(8,128)S(1)}, f32[288,384]{1,0:T(8,128)S(1)}, u32[]{:S(2)}, u32[]{:S(2)}) %collective-permute-start.9) | collective-permute-done | bytes 442400 | tf_op jit(solution)/shard_map/cond/branch_1_fun/ppermute | solution.py:21
  90.4 0.0 collective-permute-start.11
  90.4 0.7 collective-permute-start.18
  91.1 3.4 %collective-permute-start.17 = (f32[48,384]{1,0:T(8,128)S(1)}, f32[48,384]{1,0:T(8,128)S(1)}, u32[]{:S(2)}, u32[]{:S(2)}) collective-permute-start(f32[48,384]{1,0:T(8,128)S(1)} %branch_1_fun.9.refs_0_), channel_id=1, source_target_pairs={{0,8},{1,9},{2,10},{3,11},{4,12},{5,13},{6,14},{7,15},{8,0},{9,1},... | collective-permute-start | bytes 221192 | tf_op jit(solution)/shard_map/cond/branch_1_fun/ppermute | solution.py:21
  94.5 3.2 %collective-permute-done.18.refs_2_ = f32[48,384]{1,0:T(8,128)S(1)} collective-permute-done((f32[48,384]{1,0:T(8,128)S(1)}, f32[48,384]{1,0:T(8,128)S(1)}, u32[]{:S(2)}, u32[]{:S(2)}) %collective-permute-start.18) | collective-permute-done | bytes 73760 | tf_op jit(solution)/shard_map/cond/branch_1_fun/ppermute | solution.py:21
  97.6 0.1 collective-permute-done.17.refs_1_
  97.7 4.3 %collective-permute-done.19.refs_3_ = f32[48,384]{1,0:T(8,128)S(1)} collective-permute-done((f32[48,384]{1,0:T(8,128)S(1)}, f32[48,384]{1,0:T(8,128)S(1)}, u32[]{:S(2)}, u32[]{:S(2)}) %collective-permute-start.19) | collective-permute-done | bytes 73760 | tf_op jit(solution)/shard_map/cond/branch_1_fun/ppermute | solution.py:21
  102.0 0.7 branch_1_fun.10.rest_0_
  102.7 3.7 %collective-permute-start.22 = (f32[48,384]{1,0:T(8,128)S(1)}, f32[48,384]{1,0:T(8,128)S(1)}, u32[]{:S(2)}, u32[]{:S(2)}) collective-permute-start(f32[48,384]{1,0:T(8,128)S(1)} %branch_1_fun.10.rest_0_), channel_id=1, source_target_pairs={{0,6},{1,7},{2,4},{3,5},{4,2},{5,3},{6,0},{7,1},{8,14},{9,15},{10,... | collective-permute-start | bytes 221192 | tf_op jit(solution)/shard_map/cond/branch_1_fun/ppermute | solution.py:21
  106.3 2.4 %collective-permute-done.22.rest_3_ = f32[48,384]{1,0:T(8,128)S(1)} collective-permute-done((f32[48,384]{1,0:T(8,128)S(1)}, f32[48,384]{1,0:T(8,128)S(1)}, u32[]{:S(2)}, u32[]{:S(2)}) %collective-permute-start.22) | collective-permute-done | bytes 73760 | tf_op jit(solution)/shard_map/cond/branch_1_fun/ppermute | solution.py:21
  108.8 1.0 collective-permute-start.20
  109.7 1.0 collective-permute-done.21.rest_2_
  110.7 2.4 %collective-permute-done.20.rest_1_ = f32[48,384]{1,0:T(8,128)S(1)} collective-permute-done((f32[48,384]{1,0:T(8,128)S(1)}, f32[48,384]{1,0:T(8,128)S(1)}, u32[]{:S(2)}, u32[]{:S(2)}) %collective-permute-start.20) | collective-permute-done | bytes 73760 | tf_op jit(solution)/shard_map/cond/branch_1_fun/ppermute | solution.py:21
  113.1 0.5 collective-permute-start.25
  113.6 0.1 collective-permute-start.24
  113.7 4.7 %branch_1_fun.8.base = f32[1024,384]{1,0:T(8,128)S(1)} custom-call(bf16[1024,384]{1,0:T(8,128)(2,1)S(1)} %copy-done.9, bf16[1024,384]{1,0:T(8,128)(2,1)S(1)} %copy-done.14, bf16[1024,384]{1,0:T(8,128)(2,1)S(1)} %copy-done.16, bf16[1024,384]{1,0:T(8,128)(2,1)} %get-tuple-element.165.twin_low, f32[288,384]{1,0:T(8,128)S(1)} %branch_1_fun.7.keep, ...), custom_call_target="tpu_custom_call" | custom-call | flops 1811939328 | bytes 6488064 | tf_op jit(solution)/shard_map/cond/branch_1_fun/pallas_call | solution.py:211
  118.5 2.0 %branch_1_fun.11 = f32[3072,128]{1,0:T(8,128)} custom-call(s32[4,4]{1,0:T(4,128)S(1)} %get-tuple-element.161.mask, f32[1024,384]{1,0:T(8,128)S(1)} %branch_1_fun.8.base, bf16[1024,384]{1,0:T(8,128)(2,1)S(1)} %copy-done.1, bf16[1024,384]{1,0:T(8,128)(2,1)S(1)} %copy-done.4, f32[1536,128]{1,0:T(8,128)S(1)} %collective-permute-done.15.far, ...), custom_call_target="tpu_custom_call" | custom-call | flops 1811939328 | bytes 6881344 | tf_op jit(solution)/shard_map/cond/branch_1_fun/pallas_call | solution.py:211
  (43 shorter events, 0.2 us)
Async XLA Ops:
  0.0 22.5 %copy-start = (f32[1024,1,384]{2,1,0:T(1,128)S(1)}, f32[1024,1,384]{2,1,0:T(1,128)}, u32[]{:S(2)}) copy-start(f32[1024,1,384]{2,1,0:T(1,128)} %param.8) | copy-start | bytes 4718596
  0.0 36.9 %collective-permute-start.73 = (f32[3072,128]{1,0:T(8,128)}, f32[3072,128]{1,0:T(8,128)}, u32[]{:S(2)}, u32[]{:S(2)}) collective-permute-start(f32[3072,128]{1,0:T(8,128)} %bitcast.11), channel_id=1, source_target_pairs={{0,1},{1,0},{2,3},{3,2},{4,5},{5,4},{6,7},{7,6},{8,9},{9,8},{10,11... | collective-permute-start | bytes 4718600 | tf_op jit(solution)/shard_map/ppermute | solution.py:21
  1.7 24.6 %copy-start.19 = (f32[384]{0:T(512)S(1)}, f32[384]{0:T(512)}, u32[]{:S(2)}) copy-start(f32[384]{0:T(512)} %param.10) | copy-start | bytes 4612
  1.7 20.8 %collective-permute-start.74 = (f32[1536,128]{1,0:T(8,128)S(1)}, f32[1536,128]{1,0:T(8,128)S(1)}, u32[]{:S(2)}, u32[]{:S(2)}) collective-permute-start(f32[1536,128]{1,0:T(8,128)S(1)} %dynamic-slice_bitcast_fusion), channel_id=1, source_target_pairs={{0,2},{1,3},{2,0},{3,1},{4,6},{5,7},{6,4},{7,5},{8,10},{9,11},{10,... | collective-permute-start | bytes 2359304 | tf_op jit(solution)/shard_map/ppermute | solution.py:21
  22.5 19.5 %collective-permute-start.75 = (f32[1536,128]{1,0:T(8,128)S(1)}, f32[1536,128]{1,0:T(8,128)S(1)}, u32[]{:S(2)}, u32[]{:S(2)}) collective-permute-start(f32[1536,128]{1,0:T(8,128)S(1)} %collective-permute-done.74.face), channel_id=1, source_target_pairs={{0,1},{1,0},{2,3},{3,2},{4,5},{5,4},{6,7},{7,6},{8,9},{9,8},{10,11... | collective-permute-start | bytes 2359304 | tf_op jit(solution)/shard_map/ppermute | solution.py:21
  24.5 9.7 %copy-start.18 = (s32[4,4]{1,0:T(4,128)S(1)}, s32[4,4]{1,0:T(4,128)}, u32[]{:S(2)}) copy-start(s32[4,4]{1,0:T(4,128)} %mask.1) | copy-start | bytes 196
  24.5 9.7 %collective-permute-start.72 = (f32[192,384]{1,0:T(8,128)}, f32[192,384]{1,0:T(8,128)}, u32[]{:S(2)}, u32[]{:S(2)}) collective-permute-start(f32[192,384]{1,0:T(8,128)} %get-tuple-element.283), channel_id=1, source_target_pairs={{0,4},{1,5},{2,6},{3,7},{4,0},{5,1},{6,2},{7,3},{8,12},{9,13},{10,... | collective-permute-start | bytes 884744 | tf_op jit(solution)/shard_map/ppermute | solution.py:21
  36.9 5.0 %copy-start.7 = (bf16[1024,384]{1,0:T(8,128)(2,1)S(1)}, bf16[1024,384]{1,0:T(8,128)(2,1)}, u32[]{:S(2)}) copy-start(bf16[1024,384]{1,0:T(8,128)(2,1)} %get-tuple-element.320.own_top) | copy-start | bytes 2359300
  37.0 5.0 %copy-start.12 = (bf16[1024,384]{1,0:T(8,128)(2,1)S(1)}, bf16[1024,384]{1,0:T(8,128)(2,1)}, u32[]{:S(2)}) copy-start(bf16[1024,384]{1,0:T(8,128)(2,1)} %get-tuple-element.321.own_low) | copy-start | bytes 2359300
  40.2 5.4 %copy-start.15 = (bf16[1024,384]{1,0:T(8,128)(2,1)}, bf16[1024,384]{1,0:T(8,128)(2,1)S(1)}, u32[]{:S(2)}) copy-start(bf16[1024,384]{1,0:T(8,128)(2,1)S(1)} %get-tuple-element.322.twin_top) | copy-start | bytes 2359300
  40.2 5.4 %copy-start.17 = (bf16[1024,384]{1,0:T(8,128)(2,1)}, bf16[1024,384]{1,0:T(8,128)(2,1)S(1)}, u32[]{:S(2)}) copy-start(bf16[1024,384]{1,0:T(8,128)(2,1)S(1)} %get-tuple-element.323.twin_low) | copy-start | bytes 2359300
  40.2 8.5 %collective-permute-start.78 = (f32[96,384]{1,0:T(8,128)S(1)}, f32[96,384]{1,0:T(8,128)S(1)}, u32[]{:S(2)}, u32[]{:S(2)}) collective-permute-start(f32[96,384]{1,0:T(8,128)S(1)} %get-tuple-element.294), channel_id=1, source_target_pairs={{0,4},{1,5},{2,6},{3,7},{4,0},{5,1},{6,2},{7,3},{8,12},{9,13},{10,... | collective-permute-start | bytes 442376 | tf_op jit(solution)/shard_map/ppermute | solution.py:21
  42.0 3.6 %collective-permute-start.76 = (f32[1]{0:T(128)}, f32[1]{0:T(128)}, u32[]{:S(2)}, u32[]{:S(2)}) collective-permute-start(f32[1]{0:T(128)} %param.9), channel_id=1, source_target_pairs={{0,1},{1,0},{2,3},{3,2},{4,5},{5,4},{6,7},{7,6},{8,9},{9,8},{10,11... | collective-permute-start | bytes 20 | tf_op jit(solution)/shard_map/ppermute | solution.py:21
  47.2 7.0 %collective-permute-start.77 = (f32[2]{0:T(128)S(1)}, f32[2]{0:T(128)S(1)}, u32[]{:S(2)}, u32[]{:S(2)}) collective-permute-start(f32[2]{0:T(128)S(1)} %broadcast_select_fusion), channel_id=1, source_target_pairs={{0,2},{1,3},{2,0},{3,1},{4,6},{5,7},{6,4},{7,5},{8,10},{9,11},{10,... | collective-permute-start | bytes 32 | tf_op jit(solution)/shard_map/ppermute | solution.py:21
  49.7 6.7 %collective-permute-start.79 = (f32[72,384]{1,0:T(8,128)S(1)}, f32[72,384]{1,0:T(8,128)S(1)}, u32[]{:S(2)}, u32[]{:S(2)}) collective-permute-start(f32[72,384]{1,0:T(8,128)S(1)} %get-tuple-element.300), channel_id=1, source_target_pairs={{0,8},{1,9},{2,10},{3,11},{4,12},{5,13},{6,14},{7,15},{8,0},{9,1},... | collective-permute-start | bytes 331784 | tf_op jit(solution)/shard_map/ppermute | solution.py:21
  51.3 11.6 %collective-permute-start.80 = (f32[72,384]{1,0:T(8,128)S(1)}, f32[72,384]{1,0:T(8,128)S(1)}, u32[]{:S(2)}, u32[]{:S(2)}) collective-permute-start(f32[72,384]{1,0:T(8,128)S(1)} %get-tuple-element.301), channel_id=1, source_target_pairs={{0,16},{1,17},{2,18},{3,19},{4,20},{5,21},{6,22},{7,23},{8,24},{9,... | collective-permute-start | bytes 331784 | tf_op jit(solution)/shard_map/ppermute | solution.py:21
  53.9 9.0 %collective-permute-start.81 = (f32[72,384]{1,0:T(8,128)S(1)}, f32[72,384]{1,0:T(8,128)S(1)}, u32[]{:S(2)}, u32[]{:S(2)}) collective-permute-start(f32[72,384]{1,0:T(8,128)S(1)} %get-tuple-element.302), channel_id=1, source_target_pairs={{0,24},{1,25},{2,26},{3,27},{4,28},{5,29},{6,30},{7,31},{8,16},{9,... | collective-permute-start | bytes 331784 | tf_op jit(solution)/shard_map/ppermute | solution.py:21
  62.9 50.8 %copy-start.9 = (bf16[1024,384]{1,0:T(8,128)(2,1)S(1)}, bf16[1024,384]{1,0:T(8,128)(2,1)}, u32[]{:S(2)}) copy-start(bf16[1024,384]{1,0:T(8,128)(2,1)} %get-tuple-element.162.own_top) | copy-start | bytes 2359300 | tf_op jit(solution)/shard_map/cond
  62.9 5.4 %collective-permute-start.14 = (f32[48,384]{1,0:T(8,128)S(1)}, f32[48,384]{1,0:T(8,128)S(1)}, u32[]{:S(2)}, u32[]{:S(2)}) collective-permute-start(f32[48,384]{1,0:T(8,128)S(1)} %get-tuple-element.179), channel_id=1, source_target_pairs={{0,6},{1,7},{2,4},{3,5},{4,2},{5,3},{6,0},{7,1},{8,14},{9,15},{10,... | collective-permute-start | bytes 221192 | tf_op jit(solution)/shard_map/cond/branch_1_fun/ppermute | solution.py:21
  63.4 5.1 %collective-permute-start.13 = (f32[48,384]{1,0:T(8,128)S(1)}, f32[48,384]{1,0:T(8,128)S(1)}, u32[]{:S(2)}, u32[]{:S(2)}) collective-permute-start(f32[48,384]{1,0:T(8,128)S(1)} %get-tuple-element.178), channel_id=1, source_target_pairs={{0,2},{1,3},{2,0},{3,1},{4,6},{5,7},{6,4},{7,5},{8,10},{9,11},{10,... | collective-permute-start | bytes 221192 | tf_op jit(solution)/shard_map/cond/branch_1_fun/ppermute | solution.py:21
  64.9 4.4 %collective-permute-start.12 = (f32[48,384]{1,0:T(8,128)S(1)}, f32[48,384]{1,0:T(8,128)S(1)}, u32[]{:S(2)}, u32[]{:S(2)}) collective-permute-start(f32[48,384]{1,0:T(8,128)S(1)} %get-tuple-element.177), channel_id=1, source_target_pairs={{0,4},{1,5},{2,6},{3,7},{4,0},{5,1},{6,2},{7,3},{8,12},{9,13},{10,... | collective-permute-start | bytes 221192 | tf_op jit(solution)/shard_map/cond/branch_1_fun/ppermute | solution.py:21
  69.3 16.3 %collective-permute-start.15 = (f32[1536,128]{1,0:T(8,128)}, f32[1536,128]{1,0:T(8,128)S(1)}, u32[]{:S(2)}, u32[]{:S(2)}) collective-permute-start(f32[1536,128]{1,0:T(8,128)} %get-tuple-element.180), channel_id=1, source_target_pairs={{0,2},{1,3},{2,0},{3,1},{4,6},{5,7},{6,4},{7,5},{8,10},{9,11},{10,... | collective-permute-start | bytes 2359304 | tf_op jit(solution)/shard_map/cond/branch_1_fun/ppermute | solution.py:21
  70.0 43.7 %copy-start.14 = (bf16[1024,384]{1,0:T(8,128)(2,1)S(1)}, bf16[1024,384]{1,0:T(8,128)(2,1)}, u32[]{:S(2)}) copy-start(bf16[1024,384]{1,0:T(8,128)(2,1)} %get-tuple-element.163.own_low) | copy-start | bytes 2359300 | tf_op jit(solution)/shard_map/cond
  70.0 43.7 %copy-start.16 = (bf16[1024,384]{1,0:T(8,128)(2,1)S(1)}, bf16[1024,384]{1,0:T(8,128)(2,1)}, u32[]{:S(2)}) copy-start(bf16[1024,384]{1,0:T(8,128)(2,1)} %get-tuple-element.164.twin_top) | copy-start | bytes 2359300 | tf_op jit(solution)/shard_map/cond
  70.7 7.5 %collective-permute-start.8 = (f32[72,384]{1,0:T(8,128)S(1)}, f32[72,384]{1,0:T(8,128)S(1)}, u32[]{:S(2)}, u32[]{:S(2)}) collective-permute-start(f32[72,384]{1,0:T(8,128)S(1)} %branch_1_fun.6.refs_0_), channel_id=1, source_target_pairs={{0,24},{1,25},{2,26},{3,27},{4,28},{5,29},{6,30},{7,31},{8,16},{9,... | collective-permute-start | bytes 331784 | tf_op jit(solution)/shard_map/cond/branch_1_fun/ppermute | solution.py:21
  73.2 7.9 %collective-permute-start.7 = (f32[72,384]{1,0:T(8,128)S(1)}, f32[72,384]{1,0:T(8,128)S(1)}, u32[]{:S(2)}, u32[]{:S(2)}) collective-permute-start(f32[72,384]{1,0:T(8,128)S(1)} %branch_1_fun.6.refs_0_), channel_id=1, source_target_pairs={{0,16},{1,17},{2,18},{3,19},{4,20},{5,21},{6,22},{7,23},{8,24},{9,... | collective-permute-start | bytes 331784 | tf_op jit(solution)/shard_map/cond/branch_1_fun/ppermute | solution.py:21
  74.2 7.0 %collective-permute-start.6 = (f32[72,384]{1,0:T(8,128)S(1)}, f32[72,384]{1,0:T(8,128)S(1)}, u32[]{:S(2)}, u32[]{:S(2)}) collective-permute-start(f32[72,384]{1,0:T(8,128)S(1)} %branch_1_fun.6.refs_0_), channel_id=1, source_target_pairs={{0,8},{1,9},{2,10},{3,11},{4,12},{5,13},{6,14},{7,15},{8,0},{9,1},... | collective-permute-start | bytes 331784 | tf_op jit(solution)/shard_map/cond/branch_1_fun/ppermute | solution.py:21
  81.2 9.1 %collective-permute-start.9 = (f32[288,384]{1,0:T(8,128)S(1)}, f32[288,384]{1,0:T(8,128)S(1)}, u32[]{:S(2)}, u32[]{:S(2)}) collective-permute-start(f32[288,384]{1,0:T(8,128)S(1)} %branch_1_fun.7.keep), channel_id=1, source_target_pairs={{0,4},{1,5},{2,6},{3,7},{4,0},{5,1},{6,2},{7,3},{8,12},{9,13},{10,... | collective-permute-start | bytes 1327112 | tf_op jit(solution)/shard_map/cond/branch_1_fun/ppermute | solution.py:21
  85.5 32.9 %collective-permute-start.16 = (f32[1536,128]{1,0:T(8,128)S(1)}, f32[1536,128]{1,0:T(8,128)S(1)}, u32[]{:S(2)}, u32[]{:S(2)}) collective-permute-start(f32[1536,128]{1,0:T(8,128)S(1)} %collective-permute-done.15.far), channel_id=1, source_target_pairs={{0,1},{1,0},{2,3},{3,2},{4,5},{5,4},{6,7},{7,6},{8,9},{9,8},{10,11... | collective-permute-start | bytes 2359304 | tf_op jit(solution)/shard_map/cond/branch_1_fun/ppermute | solution.py:21
  85.5 27.6 %collective-permute-start.10 = (f32[288,384]{1,0:T(8,128)S(1)}, f32[288,384]{1,0:T(8,128)S(1)}, u32[]{:S(2)}, u32[]{:S(2)}) collective-permute-start(f32[288,384]{1,0:T(8,128)S(1)} %branch_1_fun.7.keep), channel_id=1, source_target_pairs={{0,1},{1,0},{2,3},{3,2},{4,5},{5,4},{6,7},{7,6},{8,9},{9,8},{10,11... | collective-permute-start | bytes 1327112 | tf_op jit(solution)/shard_map/cond/branch_1_fun/ppermute | solution.py:21
  90.4 23.3 %collective-permute-start.11 = (f32[288,384]{1,0:T(8,128)S(1)}, f32[288,384]{1,0:T(8,128)S(1)}, u32[]{:S(2)}, u32[]{:S(2)}) collective-permute-start(f32[288,384]{1,0:T(8,128)S(1)} %collective-permute-done.9.other), channel_id=1, source_target_pairs={{0,1},{1,0},{2,3},{3,2},{4,5},{5,4},{6,7},{7,6},{8,9},{9,8},{10,11... | collective-permute-start | bytes 1327112 | tf_op jit(solution)/shard_map/cond/branch_1_fun/ppermute | solution.py:21
  90.4 7.3 %collective-permute-start.18 = (f32[48,384]{1,0:T(8,128)S(1)}, f32[48,384]{1,0:T(8,128)S(1)}, u32[]{:S(2)}, u32[]{:S(2)}) collective-permute-start(f32[48,384]{1,0:T(8,128)S(1)} %branch_1_fun.9.refs_0_), channel_id=1, source_target_pairs={{0,16},{1,17},{2,18},{3,19},{4,20},{5,21},{6,22},{7,23},{8,24},{9,... | collective-permute-start | bytes 221192 | tf_op jit(solution)/shard_map/cond/branch_1_fun/ppermute | solution.py:21
  91.1 6.6 %collective-permute-start.17 = (f32[48,384]{1,0:T(8,128)S(1)}, f32[48,384]{1,0:T(8,128)S(1)}, u32[]{:S(2)}, u32[]{:S(2)}) collective-permute-start(f32[48,384]{1,0:T(8,128)S(1)} %branch_1_fun.9.refs_0_), channel_id=1, source_target_pairs={{0,8},{1,9},{2,10},{3,11},{4,12},{5,13},{6,14},{7,15},{8,0},{9,1},... | collective-permute-start | bytes 221192 | tf_op jit(solution)/shard_map/cond/branch_1_fun/ppermute | solution.py:21
  97.6 4.4 %collective-permute-start.19 = (f32[48,384]{1,0:T(8,128)S(1)}, f32[48,384]{1,0:T(8,128)S(1)}, u32[]{:S(2)}, u32[]{:S(2)}) collective-permute-start(f32[48,384]{1,0:T(8,128)S(1)} %collective-permute-done.18.refs_2_), channel_id=1, source_target_pairs={{0,8},{1,9},{2,10},{3,11},{4,12},{5,13},{6,14},{7,15},{8,0},{9,1},... | collective-permute-start | bytes 221192 | tf_op jit(solution)/shard_map/cond/branch_1_fun/ppermute | solution.py:21
  102.7 6.1 %collective-permute-start.22 = (f32[48,384]{1,0:T(8,128)S(1)}, f32[48,384]{1,0:T(8,128)S(1)}, u32[]{:S(2)}, u32[]{:S(2)}) collective-permute-start(f32[48,384]{1,0:T(8,128)S(1)} %branch_1_fun.10.rest_0_), channel_id=1, source_target_pairs={{0,6},{1,7},{2,4},{3,5},{4,2},{5,3},{6,0},{7,1},{8,14},{9,15},{10,... | collective-permute-start | bytes 221192 | tf_op jit(solution)/shard_map/cond/branch_1_fun/ppermute | solution.py:21
  106.3 4.4 %collective-permute-start.21 = (f32[48,384]{1,0:T(8,128)S(1)}, f32[48,384]{1,0:T(8,128)S(1)}, u32[]{:S(2)}, u32[]{:S(2)}) collective-permute-start(f32[48,384]{1,0:T(8,128)S(1)} %branch_1_fun.10.rest_0_), channel_id=1, source_target_pairs={{0,2},{1,3},{2,0},{3,1},{4,6},{5,7},{6,4},{7,5},{8,10},{9,11},{10,... | collective-permute-start | bytes 221192 | tf_op jit(solution)/shard_map/cond/branch_1_fun/ppermute | solution.py:21
  108.8 4.4 %collective-permute-start.20 = (f32[48,384]{1,0:T(8,128)S(1)}, f32[48,384]{1,0:T(8,128)S(1)}, u32[]{:S(2)}, u32[]{:S(2)}) collective-permute-start(f32[48,384]{1,0:T(8,128)S(1)} %branch_1_fun.10.rest_0_), channel_id=1, source_target_pairs={{0,4},{1,5},{2,6},{3,7},{4,0},{5,1},{6,2},{7,3},{8,12},{9,13},{10,... | collective-permute-start | bytes 221192 | tf_op jit(solution)/shard_map/cond/branch_1_fun/ppermute | solution.py:21
  110.7 7.7 %collective-permute-start.23 = (f32[48,384]{1,0:T(8,128)S(1)}, f32[48,384]{1,0:T(8,128)S(1)}, u32[]{:S(2)}, u32[]{:S(2)}) collective-permute-start(f32[48,384]{1,0:T(8,128)S(1)} %branch_1_fun.10.rest_0_), channel_id=1, source_target_pairs={{0,1},{1,0},{2,3},{3,2},{4,5},{5,4},{6,7},{7,6},{8,9},{9,8},{10,11... | collective-permute-start | bytes 221192 | tf_op jit(solution)/shard_map/cond/branch_1_fun/ppermute | solution.py:21
  113.1 5.3 %collective-permute-start.26 = (f32[48,384]{1,0:T(8,128)S(1)}, f32[48,384]{1,0:T(8,128)S(1)}, u32[]{:S(2)}, u32[]{:S(2)}) collective-permute-start(f32[48,384]{1,0:T(8,128)S(1)} %collective-permute-done.22.rest_3_), channel_id=1, source_target_pairs={{0,1},{1,0},{2,3},{3,2},{4,5},{5,4},{6,7},{7,6},{8,9},{9,8},{10,11... | collective-permute-start | bytes 221192 | tf_op jit(solution)/shard_map/cond/branch_1_fun/ppermute | solution.py:21
  113.1 5.3 %collective-permute-start.25 = (f32[48,384]{1,0:T(8,128)S(1)}, f32[48,384]{1,0:T(8,128)S(1)}, u32[]{:S(2)}, u32[]{:S(2)}) collective-permute-start(f32[48,384]{1,0:T(8,128)S(1)} %collective-permute-done.21.rest_2_), channel_id=1, source_target_pairs={{0,1},{1,0},{2,3},{3,2},{4,5},{5,4},{6,7},{7,6},{8,9},{9,8},{10,11... | collective-permute-start | bytes 221192 | tf_op jit(solution)/shard_map/cond/branch_1_fun/ppermute | solution.py:21
  113.6 4.8 %collective-permute-start.24 = (f32[48,384]{1,0:T(8,128)S(1)}, f32[48,384]{1,0:T(8,128)S(1)}, u32[]{:S(2)}, u32[]{:S(2)}) collective-permute-start(f32[48,384]{1,0:T(8,128)S(1)} %collective-permute-done.20.rest_1_), channel_id=1, source_target_pairs={{0,1},{1,0},{2,3},{3,2},{4,5},{5,4},{6,7},{7,6},{8,9},{9,8},{10,11... | collective-permute-start | bytes 221192 | tf_op jit(solution)/shard_map/cond/branch_1_fun/ppermute | solution.py:21
  113.7 4.8 %copy-start.1 = (bf16[1024,384]{1,0:T(8,128)(2,1)S(1)}, bf16[1024,384]{1,0:T(8,128)(2,1)}, u32[]{:S(2)}) copy-start(bf16[1024,384]{1,0:T(8,128)(2,1)} %get-tuple-element.173.face_tops) | copy-start | bytes 2359300 | tf_op jit(solution)/shard_map/cond
  113.7 4.8 %copy-start.4 = (bf16[1024,384]{1,0:T(8,128)(2,1)S(1)}, bf16[1024,384]{1,0:T(8,128)(2,1)}, u32[]{:S(2)}) copy-start(bf16[1024,384]{1,0:T(8,128)(2,1)} %get-tuple-element.174.face_lows) | copy-start | bytes 2359300 | tf_op jit(solution)/shard_map/cond

commit v2 on v1

--- a/solution.py
+++ b/solution.py
@@ -179,7 +179,7 @@
 IN_VMEM = pl.BlockSpec(memory_space=pltpu.VMEM)
 IN_SMEM = pl.BlockSpec(memory_space=pltpu.SMEM)
 SLOTS = (1, 2, 4)
-WHOLE_SLOTS = 2
+WHOLE_SLOTS = 4
 STEP = 512
 SPARE_BYTES = 2 << 20
 
@@ -243,14 +243,34 @@
     return spare[pl.ds(pl.multiple_of(skip, 8), virt // 2), :]
 
 
-def own_kernel(rows, chunks, own, keep, send, top, low, acc, cross):
+def packed_rows(chunks):
+    return (chunks + 1) // 2 * LANES
+
+
+def own_share(size, chunks):
+    packed = packed_rows(chunks)
+    return size * packed // (packed + chunks * LANES // 2)
+
+
+def triangle_parts(chunks):
+    for r in range((chunks + 1) // 2):
+        yield r, 0, r
+        if r:
+            yield r, (chunks - r) * LANES, chunks - r
+
+
+def own_kernel(rows, chunks, own, keep, send, top, low, acc, cross, packed):
     x, _, _, _, _ = spots()
     unpack(own, rows, chunks, top, low)
     cross[...] = dot_tn(top[...], low[...])
     acc[...] = dot_tn(top[...], top[...]) + (cross[...] + cross[...].T)
+    for r, column, block in triangle_parts(chunks):
+        width = (chunks - block) * LANES
+        packed[r * LANES:(r + 1) * LANES, column:column + width] = acc[
+            block * LANES:(block + 1) * LANES, block * LANES:]
     size = keep.shape[0]
-    keep[...] = acc[pl.ds(pl.multiple_of(x * size, 8), size), :]
-    send[...] = acc[pl.ds(pl.multiple_of((1 - x) * size, 8), size), :]
+    keep[...] = packed[pl.ds(pl.multiple_of(x * size, 8), size), :]
+    send[...] = packed[pl.ds(pl.multiple_of((1 - x) * size, 8), size), :]
 
 
 def twin_kernel(rows, chunks, own_top, own_low, twin, keep, send, top, low, acc, spare):
@@ -332,6 +352,15 @@
         at += size
 
 
+def x_add_kernel(vir, *refs):
+    vir_row, vir_col = refs[-2:]
+    virt = vir.shape[1]
+    vir_row[:, :virt] = vir[...]
+    vir_row[:, virt:] = vir[...]
+    vir_col[...] = jnp.broadcast_to(vir[...], (LANES, virt)).T
+    add_kernel(2, 2, *refs[:-2])
+
+
 def sum_kernel(*refs):
     total = refs[0][...]
     for other in refs[1:-1]:
@@ -351,40 +380,59 @@
         outer += size * len(ins)
 
 
-def scale_kernel(chunks, slots, members, cut, mask, occ, vir_row, vir_col, *refs):
+def scale_kernel(chunks, slots, members, cut, mask, occ_side, occ_other, vir_row, vir_col,
+                 *refs):
     x, z, side, lane, pair = spots()
     ins, out = refs[:members], refs[members]
+
+    def occ(which):
+        mine, lane_of = (which >> 1) == side, which & 1
+        return jnp.where(mine, occ_side[lane_of], occ_other[lane_of])
+
     virt = chunks * LANES
     size = out.shape[0]
-    own_size = size * 2 // 3
+    own_size = own_share(size, chunks)
+    lanes = lax.broadcasted_iota(jnp.int32, (8, virt), 1)
     for group in range(size // 8):
         row = group * 8
-        if slots == 0:
-            mixed = row >= own_size
-            if mixed:
-                row = (x * members + z) * (size - own_size) + row - own_size
-                first, second = 2 * side, 2 * side + 1
-                origin = lane * (virt // 2) + row
-            else:
-                origin = (x * members + z) * own_size + row
-                first = second = pair
+        packed = slots == 0 and row < own_size
+        if packed:
+            row = (x * members + z) * own_size + row
+            tile, inner = row >> (LANES.bit_length() - 1), row & (LANES - 1)
+            first = second = pair
+            weight = mask[pair, pair]
+        elif slots == 0:
+            row = (x * members + z) * (size - own_size) + row - own_size
+            first, second = 2 * side, 2 * side + 1
             weight = mask[first, second]
+            origin = lane * (virt // 2) + row
         else:
             row = ((x + 2 * side) * (members if cut else 1) + (z if cut else 0)) * size + row
             first, second, weight = side_pair(mask, 0, slots)
+            inner = row
             for slot in range(1, slots):
                 f, s, w = side_pair(mask, slot, slots)
-                here = row >= slot * virt // 2
+                here = row >= slot * (virt // 2)
                 first = jnp.where(here, f, first)
                 second = jnp.where(here, s, second)
                 weight = jnp.where(here, w, weight)
-            origin = lane * (virt // 2) + row % (virt // 2)
+                inner = jnp.where(here, row - slot * (virt // 2), inner)
+            origin = lane * (virt // 2) + inner
         here = slice(group * 8, group * 8 + 8)
         total = ins[0][here, :]
         for other in ins[1:]:
             total = total + other[here, :]
-        energy = vir_col[pl.ds(pl.multiple_of(origin, 8), 8), :] + vir_row[...]
-        energy = energy - occ[first] - occ[second]
+        if packed:
+            ahead = pl.multiple_of(tile * LANES, LANES)
+            behind = jnp.minimum(virt - tile * LANES, virt - LANES)
+            energy = jnp.where(
+                lanes < virt - tile * LANES,
+                vir_col[pl.ds(pl.multiple_of(ahead + inner, 8), 8), 0:1]
+                + vir_row[:, pl.ds(ahead, virt)],
+                vir_col[pl.ds(pl.multiple_of(behind + inner, 8), 8), 0:1] + vir_row[:, :virt])
+        else:
+            energy = vir_col[pl.ds(pl.multiple_of(origin, 8), 8), 0:1] + vir_row[:, :virt]
+        energy = energy - occ(first) - occ(second)
         out[here, :] = weight.astype(jnp.float32) * total / energy
 
 
@@ -409,16 +457,24 @@
 def near_gamma_kernel(rows, chunks, own_top, own_low, twin_top, twin_low,
                       keep, other, keep_t, other_t, out, parts, whole, stacked):
     x, _, _, lane, _ = spots()
-    virt = chunks * LANES
     size = keep.shape[0]
-    own_size = size * 2 // 3
+    own_size = own_share(size, chunks)
     mixed = size - own_size
+    mixed_start = packed_rows(chunks)
     for ref, slot, piece in ((keep, lane, x), (other, lane, 1 - x),
                              (keep_t, 1 - lane, x), (other_t, 1 - lane, 1 - x)):
         parts[slot, pl.ds(pl.multiple_of(piece * own_size, 8), own_size), :] = ref[:own_size, :]
-        parts[slot, pl.ds(pl.multiple_of(virt + piece * mixed, 8), mixed), :] = ref[own_size:, :]
-    stack(parts[lane, 0:virt, :], stacked.at[0])
-    place_block(parts, virt, chunks, whole)
+        parts[slot, pl.ds(pl.multiple_of(mixed_start + piece * mixed, 8), mixed), :] = ref[own_size:, :]
+    for r, column, block in triangle_parts(chunks):
+        for other_block in range(block, chunks):
+            at = column + (other_block - block) * LANES
+            tile = parts[lane, r * LANES:(r + 1) * LANES, at:at + LANES]
+            mine, theirs = (slice(b * LANES, (b + 1) * LANES) for b in (block, other_block))
+            whole[mine, theirs] = tile
+            if other_block != block:
+                whole[theirs, mine] = tile.T
+    stack(whole[...], stacked.at[0])
+    place_block(parts, mixed_start, chunks, whole)
 
     @pl.when(lane == 0)
     def _():
@@ -511,7 +567,7 @@
     return branch
 
 
-def opening(three_center, occ_energy, pair_mask):
+def opening(three_center, occ_energy, vir_energy, pair_mask):
     rows, _, virt = three_center.shape
     chunks = virt // LANES
     half = rows // 2
@@ -525,10 +581,10 @@
     near = across(pick(flat_pieces, 1 - side), 0, 2)
     twin = across(own, 0, 1)
     split = [(rows, virt, bf16)] * 2
-    mixed_rows = virt // 2
+    mixed_rows, packed = virt // 2, packed_rows(chunks)
     keep_a, send_a, own_top, own_low = call(
-        functools.partial(own_kernel, rows, chunks), [(virt // 2, virt)] * 2 + split, [own],
-        scratch=[((virt, virt), f32)] * 2, flops=block_flops)
+        functools.partial(own_kernel, rows, chunks), [(packed // 2, virt)] * 2 + split, [own],
+        scratch=[((virt, virt), f32)] * 2 + [((packed, virt), f32)], flops=block_flops)
     got_a = across(send_a, 1, 0)
     twin, send_a = lax.optimization_barrier((twin, send_a))
     keep_b, send_b, twin_top, twin_low = call(
@@ -543,14 +599,15 @@
     occ_side = jnp.concatenate([occ_energy, across(occ_energy, 0, 1)])
     occ_side = jnp.where(lane == 0, occ_side, occ_side[::-1])
     occ_other = across(occ_side, 0, 2)
-    occ = jnp.where(side == 0, jnp.concatenate([occ_side, occ_other]),
-                    jnp.concatenate([occ_other, occ_side]))
+    occ = (occ_side, occ_other)
     later_own, _ = lax.optimization_barrier((own, send_b))
     far_send = pick(later_own.reshape(2, half * chunks, LANES), side)
     keep_a, branch, far_send = lax.optimization_barrier((keep_a, branch, far_send))
-    piece_rows = (virt + mixed_rows) // 2 // z_count
-    pieces = call(functools.partial(add_kernel, 2, 2), [(piece_rows, virt)] * z_count,
-                   [keep_a, got_a, keep_b, got_b])
+    piece_rows = (packed + mixed_rows) // 2 // z_count
+    *pieces, vir_row, vir_col = call(
+        x_add_kernel,
+        [(piece_rows, virt)] * z_count + [(1, 2 * virt), (virt, LANES)],
+        [vir_energy.reshape(1, virt), keep_a, got_a, keep_b, got_b])
     side_got = [across(pieces[s], s << 1, 0) for s in range(1, z_count)]
     near_t = across(near, 0, 1)
     most = SLOTS[-1] * mixed_rows
@@ -564,19 +621,19 @@
     cross, faces = cross[:-2], cross[-2:]
     return lax.optimization_barrier((
         (own_top, own_low, twin_top, twin_low), faces, far_send, occ,
-        [pieces[0], *side_got], cross)), branch
-
-
-def closing(slots, shape, opened, vir_row, vir_col, pair_mask):
-    splits, faces, far_send, occ, side_parts, cross = opened
+        [pieces[0], *side_got], cross, (vir_row, vir_col))), branch
+
+
+def closing(slots, shape, opened, pair_mask):
+    splits, faces, far_send, occ, side_parts, cross, virs = opened
     rows, _, virt = shape
     chunks = virt // LANES
     z_count = lax.axis_size("aux") // 2
     bf16, f32 = jnp.bfloat16, jnp.float32
     block_flops = 6 * rows * virt * virt
-    energies = [pair_mask, occ, vir_row, vir_col]
+    energies = [pair_mask, *occ, *virs]
     piece_rows = side_parts[0].shape[0]
-    own_size = piece_rows * 2 // 3
+    own_size = own_share(piece_rows, chunks)
     total_rows = slots * virt // 2
     square_rows = total_rows // 4
     slab_rows = square_rows // z_count
@@ -596,7 +653,7 @@
         cross_got = [across(cross[s], *flips[s]) for s in range(1, 4)]
     slab, = call(
         functools.partial(scale_kernel, chunks, 0, z_count, True),
-        [(piece_rows, virt)], [*energies, *side_parts], in_smem=(0, 1))
+        [(piece_rows, virt)], [*energies, *side_parts], in_smem=(0, 1, 2))
     side_slabs = [slab] + z_spread(slab, False)
     joined, = call(
         functools.partial(join_kernel, (own_size, piece_rows - own_size)),
@@ -607,7 +664,7 @@
     gamma, = call(
         functools.partial(near_gamma_kernel, rows, chunks), [(rows, virt)],
         [*splits, joined, other, joined_t, other_t],
-        scratch=[((2, virt + virt // 2, virt), f32), ((virt, virt), f32),
+        scratch=[((2, packed_rows(chunks) + virt // 2, virt), f32), ((virt, virt), f32),
                  ((2, 3 * virt, virt), bf16)], flops=2 * block_flops)
     if not slots:
         gamma, = call(functools.partial(flat_kernel, rows, chunks), [(rows * chunks, LANES)],
@@ -618,7 +675,7 @@
         z_got = z_spread(summed, True)
         joined_c, = call(
             functools.partial(scale_kernel, chunks, slots, z_count, False),
-            [(square_rows, virt)], [*energies, summed, *z_got], in_smem=(0, 1))
+            [(square_rows, virt)], [*energies, summed, *z_got], in_smem=(0, 1, 2))
     else:
         pieces_c = call(
             functools.partial(add_kernel, 4, 1), [(slab_rows, virt)] * z_count,
@@ -627,7 +684,7 @@
         z_got = [across(pieces_c[s], s << 1, 0) for s in range(1, z_count)]
         cross_slab, = call(
             functools.partial(scale_kernel, chunks, slots, z_count, True),
-            [(slab_rows, virt)], [*energies, pieces_c[0], *z_got], in_smem=(0, 1))
+            [(slab_rows, virt)], [*energies, pieces_c[0], *z_got], in_smem=(0, 1, 2))
         joined_c, = call(
             functools.partial(join_kernel, (slab_rows,)), [(square_rows, virt)],
             [cross_slab] + z_spread(cross_slab, False))
@@ -655,15 +712,16 @@
     fits = (
         occ_count == 1 and pair_count == 4 and z_count in (2, 4) and aux_count == 2 * z_count
         and virt % LANES == 0 and rows % 16 == 0
-        and virt % (8 * z_count * 8 // 2) == 0 and (virt + virt // 2) % (16 * z_count) == 0)
+        and virt // LANES % 2 == 1 and virt % (32 * z_count) == 0
+        and packed_rows(virt // LANES) % (16 * z_count) == 0)
     args = (three_center, occ_energy, vir_energy, pair_mask)
     if not fits:
         return general_path(*args)
-    opened, branch = opening(three_center, occ_energy, pair_mask)
+    opened, branch = opening(three_center, occ_energy, vir_energy, pair_mask)
     gamma = lax.switch(
         branch, [functools.partial(closing, n, three_center.shape)
                  for n in (0, *SLOTS)],
-        opened, vir_energy.reshape(1, virt), vir_energy.reshape(virt, 1), pair_mask)
+        opened, pair_mask)
     return gamma.reshape(three_center.shape)
 
 

time: 122 us -> 113 us (0.926)
  waiting for transfers between devices: 62.2 us -> 53.9 us
    ppermute x31, waiting for transfers between devices: 62.2 us -> 53.9 us  [across(): return lax.ppermute(value, AXES, moves)]
  transfers between devices with their start and end apart: 31 -> 31, of which waited for: 17 -> 15; matrix products, arithmetic and copies ran while one was open for 4% -> 4% of each run, Pallas kernels for 13% -> 13%
where the time goes in v2:
time: 113 us; the launch traced here: 112 us
  waiting for transfers between devices  53.9 us (48%)
  starting transfers between devices  32.6 us (29%)
  Pallas kernels  16.8 us (15%)
  local copies, waits for them, and re-layouts  3.41 us (3%)
  between operations  2.44 us (2%)
  other arithmetic  2.08 us (2%)
    ppermute x31, waiting for transfers between devices, across(): return lax.ppermute(value, AXES, moves)  53.9 us
    ppermute x31, starting transfers between devices, across(): return lax.ppermute(value, AXES, moves)  32.6 us
    pallas_call x10, Pallas kernels, call(): pl.pallas_call(kernel, out_shape=outs, in_specs=[IN_SMEM if i in in_smem...  16.8 us
  transfers between devices with their start and end apart: 31, of which 15 were waited for; matrix products, arithmetic and copies ran while one was open for 4% of the time, Pallas kernels for 13%

profile of v2, /device:TPU:0, one launch (start us, length us, event | category | flops | bytes accessed | tf_op | source)
XLA Modules:
  0.0 111.5 jit_solution(17355988398954082526)
XLA Ops:
  0.0 0.5 collective-permute-start.70
  0.5 1.2 %dynamic-slice_bitcast_fusion = f32[1536,128]{1,0:T(8,128)S(1)} fusion(f32[2,1536,128]{2,1,0:T(8,128)} %bitcast.12, s32[]{:T(128)S(6)} %select_n.28), kind=kLoop, calls=%fused_computation | loop fusion | bytes 1572868 | tf_op jit(solution)/shard_map/jit(dynamic_index_in_dim)/squeeze | solution.py:25
  1.7 0.0 copy-start.19
  1.7 2.7 %collective-permute-start.71 = (f32[1536,128]{1,0:T(8,128)S(1)}, f32[1536,128]{1,0:T(8,128)S(1)}, u32[]{:S(2)}, u32[]{:S(2)}) collective-permute-start(f32[1536,128]{1,0:T(8,128)S(1)} %dynamic-slice_bitcast_fusion), channel_id=1, source_target_pairs={{0,2},{1,3},{2,0},{3,1},{4,6},{5,7},{6,4},{7,5},{8,10},{9,11},{10,... | collective-permute-start | bytes 2359304 | tf_op jit(solution)/shard_map/ppermute | solution.py:21
  4.4 18.1 %collective-permute-done.71.face = f32[1536,128]{1,0:T(8,128)S(1)} collective-permute-done((f32[1536,128]{1,0:T(8,128)S(1)}, f32[1536,128]{1,0:T(8,128)S(1)}, u32[]{:S(2)}, u32[]{:S(2)}) %collective-permute-start.71) | collective-permute-done | bytes 786464 | tf_op jit(solution)/shard_map/ppermute | solution.py:21
  22.5 2.0 %shard_map.50 = (f32[128,384]{1,0:T(8,128)S(1)}, f32[128,384]{1,0:T(8,128)}, bf16[1024,384]{1,0:T(8,128)(2,1)}, bf16[1024,384]{1,0:T(8,128)(2,1)}) custom-call(f32[3072,128]{1,0:T(8,128)S(1)} %bitcast.13), custom_call_target="tpu_custom_call" | custom-call | flops 905969664 | bytes 3538944 | tf_op jit(solution)/shard_map/pallas_call | solution.py:211
  24.5 1.7 %collective-permute-start.69 = (f32[128,384]{1,0:T(8,128)}, f32[128,384]{1,0:T(8,128)S(1)}, u32[]{:S(2)}, u32[]{:S(2)}) collective-permute-start(f32[128,384]{1,0:T(8,128)} %get-tuple-element.296), channel_id=1, source_target_pairs={{0,4},{1,5},{2,6},{3,7},{4,0},{5,1},{6,2},{7,3},{8,12},{9,13},{10,... | collective-permute-start | bytes 589832 | tf_op jit(solution)/shard_map/ppermute | solution.py:21
  26.9 0.9 dynamic-slice_bitcast_fusion.1
  27.9 4.2 %collective-permute-done.69.refs_1_ = f32[128,384]{1,0:T(8,128)S(1)} collective-permute-done((f32[128,384]{1,0:T(8,128)}, f32[128,384]{1,0:T(8,128)S(1)}, u32[]{:S(2)}, u32[]{:S(2)}) %collective-permute-start.69) | collective-permute-done | bytes 196640 | tf_op jit(solution)/shard_map/ppermute | solution.py:21
  32.0 0.7 fusion
  34.4 0.0 copy-start.5
  34.4 3.2 %shard_map.51 = (f32[96,384]{1,0:T(8,128)S(1)}, f32[96,384]{1,0:T(8,128)S(1)}, bf16[1024,384]{1,0:T(8,128)(2,1)S(1)}, bf16[1024,384]{1,0:T(8,128)(2,1)S(1)}) custom-call(bf16[1024,384]{1,0:T(8,128)(2,1)} %get-tuple-element.338.own_top, bf16[1024,384]{1,0:T(8,128)(2,1)} %get-tuple-element.339.own_low, f32[3072,128]{1,0:T(8,128)} %collective-permute-done.70.twin), custom_call_target="tpu_custom_call" | custom-call | flops 905969664 | bytes 5013504 | tf_op jit(solution)/shard_map/pallas_call | solution.py:211
  37.6 1.8 %collective-permute-start.75 = (f32[96,384]{1,0:T(8,128)S(1)}, f32[96,384]{1,0:T(8,128)S(1)}, u32[]{:S(2)}, u32[]{:S(2)}) collective-permute-start(f32[96,384]{1,0:T(8,128)S(1)} %get-tuple-element.307), channel_id=1, source_target_pairs={{0,4},{1,5},{2,6},{3,7},{4,0},{5,1},{6,2},{7,3},{8,12},{9,13},{10,... | collective-permute-start | bytes 442376 | tf_op jit(solution)/shard_map/ppermute | solution.py:21
  39.4 3.4 %shard_map.52 = (f32[48,384]{1,0:T(8,128)}, f32[48,384]{1,0:T(8,128)}, f32[48,384]{1,0:T(8,128)}, f32[48,384]{1,0:T(8,128)}, f32[96,384]{1,0:T(8,128)}, /*index=...) custom-call(s32[4,4]{1,0:T(4,128)S(1)} %copy-done.18, ...), custom_call_target="tpu_custom_call" | custom-call | flops 905969664 | bytes 8355904 | tf_op jit(solution)/shard_map/pallas_call | solution.py:211
  42.8 0.0 collective-permute-done.73
  42.8 0.7 pad_maximum_fusion
  43.5 0.1 rev.3
  43.6 0.0 collective-permute-done.75.refs_3_
  43.6 0.1 shard_map.53
  43.8 1.6 %collective-permute-start.76 = (f32[56,384]{1,0:T(8,128)S(1)}, f32[56,384]{1,0:T(8,128)S(1)}, u32[]{:S(2)}, u32[]{:S(2)}) collective-permute-start(f32[56,384]{1,0:T(8,128)S(1)} %get-tuple-element.313), channel_id=1, source_target_pairs={{0,8},{1,9},{2,10},{3,11},{4,12},{5,13},{6,14},{7,15},{8,0},{9,1},... | collective-permute-start | bytes 258056 | tf_op jit(solution)/shard_map/ppermute | solution.py:21
  45.4 2.6 %collective-permute-start.77 = (f32[56,384]{1,0:T(8,128)S(1)}, f32[56,384]{1,0:T(8,128)S(1)}, u32[]{:S(2)}, u32[]{:S(2)}) collective-permute-start(f32[56,384]{1,0:T(8,128)S(1)} %get-tuple-element.314), channel_id=1, source_target_pairs={{0,16},{1,17},{2,18},{3,19},{4,20},{5,21},{6,22},{7,23},{8,24},{9,... | collective-permute-start | bytes 258056 | tf_op jit(solution)/shard_map/ppermute | solution.py:21
  48.0 0.2 collective-permute-start.78
  48.2 0.7 broadcast_select_fusion
  48.9 1.5 %collective-permute-start.74 = (f32[2]{0:T(128)S(1)}, f32[2]{0:T(128)S(1)}, u32[]{:S(2)}, u32[]{:S(2)}) collective-permute-start(f32[2]{0:T(128)S(1)} %broadcast_select_fusion), channel_id=1, source_target_pairs={{0,2},{1,3},{2,0},{3,1},{4,6},{5,7},{6,4},{7,5},{8,10},{9,11},{10,... | collective-permute-start | bytes 32 | tf_op jit(solution)/shard_map/ppermute | solution.py:21
  50.5 2.0 %collective-permute-done.74 = f32[2]{0:T(128)S(1)} collective-permute-done((f32[2]{0:T(128)S(1)}, f32[2]{0:T(128)S(1)}, u32[]{:S(2)}, u32[]{:S(2)}) %collective-permute-start.74) | collective-permute-done | bytes 40 | tf_op jit(solution)/shard_map/ppermute | solution.py:21
  52.5 0.0 collective-permute-done.76
  52.5 2.8 %collective-permute-done.77 = f32[56,384]{1,0:T(8,128)S(1)} collective-permute-done((f32[56,384]{1,0:T(8,128)S(1)}, f32[56,384]{1,0:T(8,128)S(1)}, u32[]{:S(2)}, u32[]{:S(2)}) %collective-permute-start.77) | collective-permute-done | bytes 86048 | tf_op jit(solution)/shard_map/ppermute | solution.py:21
  55.3 0.0 collective-permute-done.78
  55.3 55.1 %conditional.1 = (f32[1024,1,384]{2,1,0:T(1,128)S(1)}) conditional(s32[]{:T(128)} %clamp.3, (s32[4,4]{1,0:T(4,128)S(1)}, f32[2]{0:T(128)S(1)}, f32[2]{0:T(128)S(1)}, f32[1,768]{1,0:T(1,128)S(1)}, f32[384,128]{1,0:T(8,128)S(1)}, /*index=5*/f32[56,384]{1,0:T(8,128)S(1)}, f32[56,384]{1,0:T(8,128)S(1)}, ...), branch_computations={%region_1.2_spmd, %region_2.3_spmd, %region_3.4_spmd, %region_4.5_... | conditional | flops 3623878656 | bytes 61729980 | solution.py:721
  55.3 1.0 collective-permute-start.12
  56.2 1.5 %collective-permute-start.13 = (f32[48,384]{1,0:T(8,128)}, f32[48,384]{1,0:T(8,128)S(1)}, u32[]{:S(2)}, u32[]{:S(2)}) collective-permute-start(f32[48,384]{1,0:T(8,128)} %get-tuple-element.188), channel_id=1, source_target_pairs={{0,2},{1,3},{2,0},{3,1},{4,6},{5,7},{6,4},{7,5},{8,10},{9,11},{10,... | collective-permute-start | bytes 221192 | tf_op jit(solution)/shard_map/cond/branch_1_fun/ppermute | solution.py:21
  57.8 1.1 collective-permute-start.14
  58.8 1.1 collective-permute-done.12.refs_1_
  59.9 0.9 collective-permute-done.13.refs_2_
  60.8 2.4 %collective-permute-done.14.refs_3_ = f32[48,384]{1,0:T(8,128)S(1)} collective-permute-done((f32[48,384]{1,0:T(8,128)}, f32[48,384]{1,0:T(8,128)S(1)}, u32[]{:S(2)}, u32[]{:S(2)}) %collective-permute-start.14) | collective-permute-done | bytes 73760 | tf_op jit(solution)/shard_map/cond/branch_1_fun/ppermute | solution.py:21
  63.2 0.9 branch_1_fun.9.refs_0_
  64.1 0.6 collective-permute-start.15
  64.7 0.7 branch_1_fun.6.refs_0_
  65.4 2.5 %collective-permute-start.8 = (f32[56,384]{1,0:T(8,128)S(1)}, f32[56,384]{1,0:T(8,128)S(1)}, u32[]{:S(2)}, u32[]{:S(2)}) collective-permute-start(f32[56,384]{1,0:T(8,128)S(1)} %branch_1_fun.6.refs_0_), channel_id=1, source_target_pairs={{0,24},{1,25},{2,26},{3,27},{4,28},{5,29},{6,30},{7,31},{8,16},{9,... | collective-permute-start | bytes 258056 | tf_op jit(solution)/shard_map/cond/branch_1_fun/ppermute | solution.py:21
  67.9 0.4 collective-permute-start.7
  68.3 1.5 %collective-permute-start.6 = (f32[56,384]{1,0:T(8,128)S(1)}, f32[56,384]{1,0:T(8,128)S(1)}, u32[]{:S(2)}, u32[]{:S(2)}) collective-permute-start(f32[56,384]{1,0:T(8,128)S(1)} %branch_1_fun.6.refs_0_), channel_id=1, source_target_pairs={{0,8},{1,9},{2,10},{3,11},{4,12},{5,13},{6,14},{7,15},{8,0},{9,1},... | collective-permute-start | bytes 258056 | tf_op jit(solution)/shard_map/cond/branch_1_fun/ppermute | solution.py:21
  69.8 1.9 %collective-permute-done.8.refs_3_ = f32[56,384]{1,0:T(8,128)S(1)} collective-permute-done((f32[56,384]{1,0:T(8,128)S(1)}, f32[56,384]{1,0:T(8,128)S(1)}, u32[]{:S(2)}, u32[]{:S(2)}) %collective-permute-start.8) | collective-permute-done | bytes 86048 | tf_op jit(solution)/shard_map/cond/branch_1_fun/ppermute | solution.py:21
  71.7 2.4 %collective-permute-done.7.refs_2_ = f32[56,384]{1,0:T(8,128)S(1)} collective-permute-done((f32[56,384]{1,0:T(8,128)S(1)}, f32[56,384]{1,0:T(8,128)S(1)}, u32[]{:S(2)}, u32[]{:S(2)}) %collective-permute-start.7) | collective-permute-done | bytes 86048 | tf_op jit(solution)/shard_map/cond/branch_1_fun/ppermute | solution.py:21
  74.2 0.0 collective-permute-done.6.refs_1_
  74.2 1.5 %collective-permute-start.9 = (f32[224,384]{1,0:T(8,128)S(1)}, f32[224,384]{1,0:T(8,128)S(1)}, u32[]{:S(2)}, u32[]{:S(2)}) collective-permute-start(f32[224,384]{1,0:T(8,128)S(1)} %branch_1_fun.7.keep), channel_id=1, source_target_pairs={{0,4},{1,5},{2,6},{3,7},{4,0},{5,1},{6,2},{7,3},{8,12},{9,13},{10,... | collective-permute-start | bytes 1032200 | tf_op jit(solution)/shard_map/cond/branch_1_fun/ppermute | solution.py:21
  75.7 4.6 %collective-permute-done.15.far = f32[1536,128]{1,0:T(8,128)S(1)} collective-permute-done((f32[1536,128]{1,0:T(8,128)}, f32[1536,128]{1,0:T(8,128)S(1)}, u32[]{:S(2)}, u32[]{:S(2)}) %collective-permute-start.15) | collective-permute-done | bytes 786464 | tf_op jit(solution)/shard_map/cond/branch_1_fun/ppermute | solution.py:21
  80.2 0.5 collective-permute-start.10
  80.8 0.8 collective-permute-done.9.other
  81.5 3.2 %collective-permute-start.18 = (f32[48,384]{1,0:T(8,128)S(1)}, f32[48,384]{1,0:T(8,128)S(1)}, u32[]{:S(2)}, u32[]{:S(2)}) collective-permute-start(f32[48,384]{1,0:T(8,128)S(1)} %branch_1_fun.9.refs_0_), channel_id=1, source_target_pairs={{0,16},{1,17},{2,18},{3,19},{4,20},{5,21},{6,22},{7,23},{8,24},{9,... | collective-permute-start | bytes 221192 | tf_op jit(solution)/shard_map/cond/branch_1_fun/ppermute | solution.py:21
  84.7 4.3 %collective-permute-done.18.refs_2_ = f32[48,384]{1,0:T(8,128)S(1)} collective-permute-done((f32[48,384]{1,0:T(8,128)S(1)}, f32[48,384]{1,0:T(8,128)S(1)}, u32[]{:S(2)}, u32[]{:S(2)}) %collective-permute-start.18) | collective-permute-done | bytes 73760 | tf_op jit(solution)/shard_map/cond/branch_1_fun/ppermute | solution.py:21
  89.0 1.1 collective-permute-start.19
  90.1 3.3 %collective-permute-done.19.refs_3_ = f32[48,384]{1,0:T(8,128)S(1)} collective-permute-done((f32[48,384]{1,0:T(8,128)S(1)}, f32[48,384]{1,0:T(8,128)S(1)}, u32[]{:S(2)}, u32[]{:S(2)}) %collective-permute-start.19) | collective-permute-done | bytes 73760 | tf_op jit(solution)/shard_map/cond/branch_1_fun/ppermute | solution.py:21
  93.4 0.7 branch_1_fun.10.rest_0_
  94.0 2.3 %collective-permute-start.22 = (f32[48,384]{1,0:T(8,128)S(1)}, f32[48,384]{1,0:T(8,128)S(1)}, u32[]{:S(2)}, u32[]{:S(2)}) collective-permute-start(f32[48,384]{1,0:T(8,128)S(1)} %branch_1_fun.10.rest_0_), channel_id=1, source_target_pairs={{0,6},{1,7},{2,4},{3,5},{4,2},{5,3},{6,0},{7,1},{8,14},{9,15},{10,... | collective-permute-start | bytes 221192 | tf_op jit(solution)/shard_map/cond/branch_1_fun/ppermute | solution.py:21
  96.4 0.7 collective-permute-start.21
  97.0 2.3 %collective-permute-done.22.rest_3_ = f32[48,384]{1,0:T(8,128)S(1)} collective-permute-done((f32[48,384]{1,0:T(8,128)S(1)}, f32[48,384]{1,0:T(8,128)S(1)}, u32[]{:S(2)}, u32[]{:S(2)}) %collective-permute-start.22) | collective-permute-done | bytes 73760 | tf_op jit(solution)/shard_map/cond/branch_1_fun/ppermute | solution.py:21
  99.4 1.5 %collective-permute-start.20 = (f32[48,384]{1,0:T(8,128)S(1)}, f32[48,384]{1,0:T(8,128)S(1)}, u32[]{:S(2)}, u32[]{:S(2)}) collective-permute-start(f32[48,384]{1,0:T(8,128)S(1)} %branch_1_fun.10.rest_0_), channel_id=1, source_target_pairs={{0,4},{1,5},{2,6},{3,7},{4,0},{5,1},{6,2},{7,3},{8,12},{9,13},{10,... | collective-permute-start | bytes 221192 | tf_op jit(solution)/shard_map/cond/branch_1_fun/ppermute | solution.py:21
  100.9 2.8 %collective-permute-done.20.rest_1_ = f32[48,384]{1,0:T(8,128)S(1)} collective-permute-done((f32[48,384]{1,0:T(8,128)S(1)}, f32[48,384]{1,0:T(8,128)S(1)}, u32[]{:S(2)}, u32[]{:S(2)}) %collective-permute-start.20) | collective-permute-done | bytes 73760 | tf_op jit(solution)/shard_map/cond/branch_1_fun/ppermute | solution.py:21
  103.7 0.5 collective-permute-start.25
  104.2 0.1 collective-permute-start.24
  104.3 4.9 %branch_1_fun.8.base = f32[1024,384]{1,0:T(8,128)S(1)} custom-call(bf16[1024,384]{1,0:T(8,128)(2,1)S(1)} %copy-done.6, bf16[1024,384]{1,0:T(8,128)(2,1)S(1)} %copy-done.10, bf16[1024,384]{1,0:T(8,128)(2,1)} %get-tuple-element.173.twin_top, bf16[1024,384]{1,0:T(8,128)(2,1)} %get-tuple-element.174.twin_low, f32[224,384]{1,0:T(8,128)S(1)} %branch_1_fun.7.keep, ...), custom_call_target="tpu_custom_call" | custom-call | flops 1811939328 | bytes 6094848 | tf_op jit(solution)/shard_map/cond/branch_1_fun/pallas_call | solution.py:211
  109.3 0.9 branch_1_fun.11
  110.4 0.0 copy-start.4
  110.4 1.1 %copy-done.4 = f32[1024,1,384]{2,1,0:T(1,128)} copy-done((f32[1024,1,384]{2,1,0:T(1,128)}, f32[1024,1,384]{2,1,0:T(1,128)S(1)}, u32[]{:S(2)}) %copy-start.4) | copy-done | bytes 1572888
  (38 shorter events, 0.1 us)
Async XLA Ops:
  0.0 22.5 %copy-start = (f32[1024,1,384]{2,1,0:T(1,128)S(1)}, f32[1024,1,384]{2,1,0:T(1,128)}, u32[]{:S(2)}) copy-start(f32[1024,1,384]{2,1,0:T(1,128)} %param.8) | copy-start | bytes 4718596
  0.0 34.4 %collective-permute-start.70 = (f32[3072,128]{1,0:T(8,128)}, f32[3072,128]{1,0:T(8,128)}, u32[]{:S(2)}, u32[]{:S(2)}) collective-permute-start(f32[3072,128]{1,0:T(8,128)} %bitcast.11), channel_id=1, source_target_pairs={{0,1},{1,0},{2,3},{3,2},{4,5},{5,4},{6,7},{7,6},{8,9},{9,8},{10,11... | collective-permute-start | bytes 4718600 | tf_op jit(solution)/shard_map/ppermute | solution.py:21
  1.7 25.2 %copy-start.19 = (f32[384]{0:T(512)S(1)}, f32[384]{0:T(512)}, u32[]{:S(2)}) copy-start(f32[384]{0:T(512)} %param.10) | copy-start | bytes 4612
  1.7 20.8 %collective-permute-start.71 = (f32[1536,128]{1,0:T(8,128)S(1)}, f32[1536,128]{1,0:T(8,128)S(1)}, u32[]{:S(2)}, u32[]{:S(2)}) collective-permute-start(f32[1536,128]{1,0:T(8,128)S(1)} %dynamic-slice_bitcast_fusion), channel_id=1, source_target_pairs={{0,2},{1,3},{2,0},{3,1},{4,6},{5,7},{6,4},{7,5},{8,10},{9,11},{10,... | collective-permute-start | bytes 2359304 | tf_op jit(solution)/shard_map/ppermute | solution.py:21
  22.5 16.9 %collective-permute-start.72 = (f32[1536,128]{1,0:T(8,128)S(1)}, f32[1536,128]{1,0:T(8,128)S(1)}, u32[]{:S(2)}, u32[]{:S(2)}) collective-permute-start(f32[1536,128]{1,0:T(8,128)S(1)} %collective-permute-done.71.face), channel_id=1, source_target_pairs={{0,1},{1,0},{2,3},{3,2},{4,5},{5,4},{6,7},{7,6},{8,9},{9,8},{10,11... | collective-permute-start | bytes 2359304 | tf_op jit(solution)/shard_map/ppermute | solution.py:21
  24.5 7.5 %copy-start.18 = (s32[4,4]{1,0:T(4,128)S(1)}, s32[4,4]{1,0:T(4,128)}, u32[]{:S(2)}) copy-start(s32[4,4]{1,0:T(4,128)} %mask.1) | copy-start | bytes 196
  24.5 7.5 %collective-permute-start.69 = (f32[128,384]{1,0:T(8,128)}, f32[128,384]{1,0:T(8,128)S(1)}, u32[]{:S(2)}, u32[]{:S(2)}) collective-permute-start(f32[128,384]{1,0:T(8,128)} %get-tuple-element.296), channel_id=1, source_target_pairs={{0,4},{1,5},{2,6},{3,7},{4,0},{5,1},{6,2},{7,3},{8,12},{9,13},{10,... | collective-permute-start | bytes 589832 | tf_op jit(solution)/shard_map/ppermute | solution.py:21
  34.4 5.0 %copy-start.5 = (bf16[1024,384]{1,0:T(8,128)(2,1)S(1)}, bf16[1024,384]{1,0:T(8,128)(2,1)}, u32[]{:S(2)}) copy-start(bf16[1024,384]{1,0:T(8,128)(2,1)} %get-tuple-element.338.own_top) | copy-start | bytes 2359300
  34.4 5.0 %copy-start.9 = (bf16[1024,384]{1,0:T(8,128)(2,1)S(1)}, bf16[1024,384]{1,0:T(8,128)(2,1)}, u32[]{:S(2)}) copy-start(bf16[1024,384]{1,0:T(8,128)(2,1)} %get-tuple-element.339.own_low) | copy-start | bytes 2359300
  37.6 5.2 %copy-start.13 = (bf16[1024,384]{1,0:T(8,128)(2,1)}, bf16[1024,384]{1,0:T(8,128)(2,1)S(1)}, u32[]{:S(2)}) copy-start(bf16[1024,384]{1,0:T(8,128)(2,1)S(1)} %get-tuple-element.340.twin_top) | copy-start | bytes 2359300
  37.6 5.2 %copy-start.16 = (bf16[1024,384]{1,0:T(8,128)(2,1)}, bf16[1024,384]{1,0:T(8,128)(2,1)S(1)}, u32[]{:S(2)}) copy-start(bf16[1024,384]{1,0:T(8,128)(2,1)S(1)} %get-tuple-element.341.twin_low) | copy-start | bytes 2359300
  37.6 6.0 %collective-permute-start.75 = (f32[96,384]{1,0:T(8,128)S(1)}, f32[96,384]{1,0:T(8,128)S(1)}, u32[]{:S(2)}, u32[]{:S(2)}) collective-permute-start(f32[96,384]{1,0:T(8,128)S(1)} %get-tuple-element.307), channel_id=1, source_target_pairs={{0,4},{1,5},{2,6},{3,7},{4,0},{5,1},{6,2},{7,3},{8,12},{9,13},{10,... | collective-permute-start | bytes 442376 | tf_op jit(solution)/shard_map/ppermute | solution.py:21
  39.4 3.4 %collective-permute-start.73 = (f32[1]{0:T(128)}, f32[1]{0:T(128)}, u32[]{:S(2)}, u32[]{:S(2)}) collective-permute-start(f32[1]{0:T(128)} %param.9), channel_id=1, source_target_pairs={{0,1},{1,0},{2,3},{3,2},{4,5},{5,4},{6,7},{7,6},{8,9},{9,8},{10,11... | collective-permute-start | bytes 20 | tf_op jit(solution)/shard_map/ppermute | solution.py:21
  43.8 8.7 %collective-permute-start.76 = (f32[56,384]{1,0:T(8,128)S(1)}, f32[56,384]{1,0:T(8,128)S(1)}, u32[]{:S(2)}, u32[]{:S(2)}) collective-permute-start(f32[56,384]{1,0:T(8,128)S(1)} %get-tuple-element.313), channel_id=1, source_target_pairs={{0,8},{1,9},{2,10},{3,11},{4,12},{5,13},{6,14},{7,15},{8,0},{9,1},... | collective-permute-start | bytes 258056 | tf_op jit(solution)/shard_map/ppermute | solution.py:21
  45.4 9.8 %collective-permute-start.77 = (f32[56,384]{1,0:T(8,128)S(1)}, f32[56,384]{1,0:T(8,128)S(1)}, u32[]{:S(2)}, u32[]{:S(2)}) collective-permute-start(f32[56,384]{1,0:T(8,128)S(1)} %get-tuple-element.314), channel_id=1, source_target_pairs={{0,16},{1,17},{2,18},{3,19},{4,20},{5,21},{6,22},{7,23},{8,24},{9,... | collective-permute-start | bytes 258056 | tf_op jit(solution)/shard_map/ppermute | solution.py:21
  48.0 7.2 %collective-permute-start.78 = (f32[56,384]{1,0:T(8,128)S(1)}, f32[56,384]{1,0:T(8,128)S(1)}, u32[]{:S(2)}, u32[]{:S(2)}) collective-permute-start(f32[56,384]{1,0:T(8,128)S(1)} %get-tuple-element.315), channel_id=1, source_target_pairs={{0,24},{1,25},{2,26},{3,27},{4,28},{5,29},{6,30},{7,31},{8,16},{9,... | collective-permute-start | bytes 258056 | tf_op jit(solution)/shard_map/ppermute | solution.py:21
  48.9 3.6 %collective-permute-start.74 = (f32[2]{0:T(128)S(1)}, f32[2]{0:T(128)S(1)}, u32[]{:S(2)}, u32[]{:S(2)}) collective-permute-start(f32[2]{0:T(128)S(1)} %broadcast_select_fusion), channel_id=1, source_target_pairs={{0,2},{1,3},{2,0},{3,1},{4,6},{5,7},{6,4},{7,5},{8,10},{9,11},{10,... | collective-permute-start | bytes 32 | tf_op jit(solution)/shard_map/ppermute | solution.py:21
  55.3 49.0 %copy-start.6 = (bf16[1024,384]{1,0:T(8,128)(2,1)S(1)}, bf16[1024,384]{1,0:T(8,128)(2,1)}, u32[]{:S(2)}) copy-start(bf16[1024,384]{1,0:T(8,128)(2,1)} %get-tuple-element.171.own_top) | copy-start | bytes 2359300 | tf_op jit(solution)/shard_map/cond
  55.3 49.0 %copy-start.10 = (bf16[1024,384]{1,0:T(8,128)(2,1)S(1)}, bf16[1024,384]{1,0:T(8,128)(2,1)}, u32[]{:S(2)}) copy-start(bf16[1024,384]{1,0:T(8,128)(2,1)} %get-tuple-element.172.own_low) | copy-start | bytes 2359300 | tf_op jit(solution)/shard_map/cond
  55.3 4.6 %collective-permute-start.12 = (f32[48,384]{1,0:T(8,128)}, f32[48,384]{1,0:T(8,128)S(1)}, u32[]{:S(2)}, u32[]{:S(2)}) collective-permute-start(f32[48,384]{1,0:T(8,128)} %get-tuple-element.187), channel_id=1, source_target_pairs={{0,4},{1,5},{2,6},{3,7},{4,0},{5,1},{6,2},{7,3},{8,12},{9,13},{10,... | collective-permute-start | bytes 221192 | tf_op jit(solution)/shard_map/cond/branch_1_fun/ppermute | solution.py:21
  56.2 4.6 %collective-permute-start.13 = (f32[48,384]{1,0:T(8,128)}, f32[48,384]{1,0:T(8,128)S(1)}, u32[]{:S(2)}, u32[]{:S(2)}) collective-permute-start(f32[48,384]{1,0:T(8,128)} %get-tuple-element.188), channel_id=1, source_target_pairs={{0,2},{1,3},{2,0},{3,1},{4,6},{5,7},{6,4},{7,5},{8,10},{9,11},{10,... | collective-permute-start | bytes 221192 | tf_op jit(solution)/shard_map/cond/branch_1_fun/ppermute | solution.py:21
  57.8 5.5 %collective-permute-start.14 = (f32[48,384]{1,0:T(8,128)}, f32[48,384]{1,0:T(8,128)S(1)}, u32[]{:S(2)}, u32[]{:S(2)}) collective-permute-start(f32[48,384]{1,0:T(8,128)} %get-tuple-element.189), channel_id=1, source_target_pairs={{0,6},{1,7},{2,4},{3,5},{4,2},{5,3},{6,0},{7,1},{8,14},{9,15},{10,... | collective-permute-start | bytes 221192 | tf_op jit(solution)/shard_map/cond/branch_1_fun/ppermute | solution.py:21
  64.1 16.1 %collective-permute-start.15 = (f32[1536,128]{1,0:T(8,128)}, f32[1536,128]{1,0:T(8,128)S(1)}, u32[]{:S(2)}, u32[]{:S(2)}) collective-permute-start(f32[1536,128]{1,0:T(8,128)} %get-tuple-element.190), channel_id=1, source_target_pairs={{0,2},{1,3},{2,0},{3,1},{4,6},{5,7},{6,4},{7,5},{8,10},{9,11},{10,... | collective-permute-start | bytes 2359304 | tf_op jit(solution)/shard_map/cond/branch_1_fun/ppermute | solution.py:21
  65.4 6.3 %collective-permute-start.8 = (f32[56,384]{1,0:T(8,128)S(1)}, f32[56,384]{1,0:T(8,128)S(1)}, u32[]{:S(2)}, u32[]{:S(2)}) collective-permute-start(f32[56,384]{1,0:T(8,128)S(1)} %branch_1_fun.6.refs_0_), channel_id=1, source_target_pairs={{0,24},{1,25},{2,26},{3,27},{4,28},{5,29},{6,30},{7,31},{8,16},{9,... | collective-permute-start | bytes 258056 | tf_op jit(solution)/shard_map/cond/branch_1_fun/ppermute | solution.py:21
  67.9 6.3 %collective-permute-start.7 = (f32[56,384]{1,0:T(8,128)S(1)}, f32[56,384]{1,0:T(8,128)S(1)}, u32[]{:S(2)}, u32[]{:S(2)}) collective-permute-start(f32[56,384]{1,0:T(8,128)S(1)} %branch_1_fun.6.refs_0_), channel_id=1, source_target_pairs={{0,16},{1,17},{2,18},{3,19},{4,20},{5,21},{6,22},{7,23},{8,24},{9,... | collective-permute-start | bytes 258056 | tf_op jit(solution)/shard_map/cond/branch_1_fun/ppermute | solution.py:21
  68.3 5.8 %collective-permute-start.6 = (f32[56,384]{1,0:T(8,128)S(1)}, f32[56,384]{1,0:T(8,128)S(1)}, u32[]{:S(2)}, u32[]{:S(2)}) collective-permute-start(f32[56,384]{1,0:T(8,128)S(1)} %branch_1_fun.6.refs_0_), channel_id=1, source_target_pairs={{0,8},{1,9},{2,10},{3,11},{4,12},{5,13},{6,14},{7,15},{8,0},{9,1},... | collective-permute-start | bytes 258056 | tf_op jit(solution)/shard_map/cond/branch_1_fun/ppermute | solution.py:21
  74.2 7.3 %collective-permute-start.9 = (f32[224,384]{1,0:T(8,128)S(1)}, f32[224,384]{1,0:T(8,128)S(1)}, u32[]{:S(2)}, u32[]{:S(2)}) collective-permute-start(f32[224,384]{1,0:T(8,128)S(1)} %branch_1_fun.7.keep), channel_id=1, source_target_pairs={{0,4},{1,5},{2,6},{3,7},{4,0},{5,1},{6,2},{7,3},{8,12},{9,13},{10,... | collective-permute-start | bytes 1032200 | tf_op jit(solution)/shard_map/cond/branch_1_fun/ppermute | solution.py:21
  80.2 29.0 %collective-permute-start.16 = (f32[1536,128]{1,0:T(8,128)S(1)}, f32[1536,128]{1,0:T(8,128)S(1)}, u32[]{:S(2)}, u32[]{:S(2)}) collective-permute-start(f32[1536,128]{1,0:T(8,128)S(1)} %collective-permute-done.15.far), channel_id=1, source_target_pairs={{0,1},{1,0},{2,3},{3,2},{4,5},{5,4},{6,7},{7,6},{8,9},{9,8},{10,11... | collective-permute-start | bytes 2359304 | tf_op jit(solution)/shard_map/cond/branch_1_fun/ppermute | solution.py:21
  80.2 23.5 %collective-permute-start.10 = (f32[224,384]{1,0:T(8,128)S(1)}, f32[224,384]{1,0:T(8,128)S(1)}, u32[]{:S(2)}, u32[]{:S(2)}) collective-permute-start(f32[224,384]{1,0:T(8,128)S(1)} %branch_1_fun.7.keep), channel_id=1, source_target_pairs={{0,1},{1,0},{2,3},{3,2},{4,5},{5,4},{6,7},{7,6},{8,9},{9,8},{10,11... | collective-permute-start | bytes 1032200 | tf_op jit(solution)/shard_map/cond/branch_1_fun/ppermute | solution.py:21
  81.5 22.7 %collective-permute-start.11 = (f32[224,384]{1,0:T(8,128)S(1)}, f32[224,384]{1,0:T(8,128)S(1)}, u32[]{:S(2)}, u32[]{:S(2)}) collective-permute-start(f32[224,384]{1,0:T(8,128)S(1)} %collective-permute-done.9.other), channel_id=1, source_target_pairs={{0,1},{1,0},{2,3},{3,2},{4,5},{5,4},{6,7},{7,6},{8,9},{9,8},{10,11... | collective-permute-start | bytes 1032200 | tf_op jit(solution)/shard_map/cond/branch_1_fun/ppermute | solution.py:21
  81.5 7.5 %collective-permute-start.18 = (f32[48,384]{1,0:T(8,128)S(1)}, f32[48,384]{1,0:T(8,128)S(1)}, u32[]{:S(2)}, u32[]{:S(2)}) collective-permute-start(f32[48,384]{1,0:T(8,128)S(1)} %branch_1_fun.9.refs_0_), channel_id=1, source_target_pairs={{0,16},{1,17},{2,18},{3,19},{4,20},{5,21},{6,22},{7,23},{8,24},{9,... | collective-permute-start | bytes 221192 | tf_op jit(solution)/shard_map/cond/branch_1_fun/ppermute | solution.py:21
  84.7 5.3 %collective-permute-start.17 = (f32[48,384]{1,0:T(8,128)S(1)}, f32[48,384]{1,0:T(8,128)S(1)}, u32[]{:S(2)}, u32[]{:S(2)}) collective-permute-start(f32[48,384]{1,0:T(8,128)S(1)} %branch_1_fun.9.refs_0_), channel_id=1, source_target_pairs={{0,8},{1,9},{2,10},{3,11},{4,12},{5,13},{6,14},{7,15},{8,0},{9,1},... | collective-permute-start | bytes 221192 | tf_op jit(solution)/shard_map/cond/branch_1_fun/ppermute | solution.py:21
  89.0 4.4 %collective-permute-start.19 = (f32[48,384]{1,0:T(8,128)S(1)}, f32[48,384]{1,0:T(8,128)S(1)}, u32[]{:S(2)}, u32[]{:S(2)}) collective-permute-start(f32[48,384]{1,0:T(8,128)S(1)} %collective-permute-done.18.refs_2_), channel_id=1, source_target_pairs={{0,8},{1,9},{2,10},{3,11},{4,12},{5,13},{6,14},{7,15},{8,0},{9,1},... | collective-permute-start | bytes 221192 | tf_op jit(solution)/shard_map/cond/branch_1_fun/ppermute | solution.py:21
  94.0 5.3 %collective-permute-start.22 = (f32[48,384]{1,0:T(8,128)S(1)}, f32[48,384]{1,0:T(8,128)S(1)}, u32[]{:S(2)}, u32[]{:S(2)}) collective-permute-start(f32[48,384]{1,0:T(8,128)S(1)} %branch_1_fun.10.rest_0_), channel_id=1, source_target_pairs={{0,6},{1,7},{2,4},{3,5},{4,2},{5,3},{6,0},{7,1},{8,14},{9,15},{10,... | collective-permute-start | bytes 221192 | tf_op jit(solution)/shard_map/cond/branch_1_fun/ppermute | solution.py:21
  96.4 4.5 %collective-permute-start.21 = (f32[48,384]{1,0:T(8,128)S(1)}, f32[48,384]{1,0:T(8,128)S(1)}, u32[]{:S(2)}, u32[]{:S(2)}) collective-permute-start(f32[48,384]{1,0:T(8,128)S(1)} %branch_1_fun.10.rest_0_), channel_id=1, source_target_pairs={{0,2},{1,3},{2,0},{3,1},{4,6},{5,7},{6,4},{7,5},{8,10},{9,11},{10,... | collective-permute-start | bytes 221192 | tf_op jit(solution)/shard_map/cond/branch_1_fun/ppermute | solution.py:21
  99.4 4.4 %collective-permute-start.20 = (f32[48,384]{1,0:T(8,128)S(1)}, f32[48,384]{1,0:T(8,128)S(1)}, u32[]{:S(2)}, u32[]{:S(2)}) collective-permute-start(f32[48,384]{1,0:T(8,128)S(1)} %branch_1_fun.10.rest_0_), channel_id=1, source_target_pairs={{0,4},{1,5},{2,6},{3,7},{4,0},{5,1},{6,2},{7,3},{8,12},{9,13},{10,... | collective-permute-start | bytes 221192 | tf_op jit(solution)/shard_map/cond/branch_1_fun/ppermute | solution.py:21
  100.9 8.3 %collective-permute-start.23 = (f32[48,384]{1,0:T(8,128)S(1)}, f32[48,384]{1,0:T(8,128)S(1)}, u32[]{:S(2)}, u32[]{:S(2)}) collective-permute-start(f32[48,384]{1,0:T(8,128)S(1)} %branch_1_fun.10.rest_0_), channel_id=1, source_target_pairs={{0,1},{1,0},{2,3},{3,2},{4,5},{5,4},{6,7},{7,6},{8,9},{9,8},{10,11... | collective-permute-start | bytes 221192 | tf_op jit(solution)/shard_map/cond/branch_1_fun/ppermute | solution.py:21
  103.7 5.5 %collective-permute-start.26 = (f32[48,384]{1,0:T(8,128)S(1)}, f32[48,384]{1,0:T(8,128)S(1)}, u32[]{:S(2)}, u32[]{:S(2)}) collective-permute-start(f32[48,384]{1,0:T(8,128)S(1)} %collective-permute-done.22.rest_3_), channel_id=1, source_target_pairs={{0,1},{1,0},{2,3},{3,2},{4,5},{5,4},{6,7},{7,6},{8,9},{9,8},{10,11... | collective-permute-start | bytes 221192 | tf_op jit(solution)/shard_map/cond/branch_1_fun/ppermute | solution.py:21
  103.7 5.5 %collective-permute-start.25 = (f32[48,384]{1,0:T(8,128)S(1)}, f32[48,384]{1,0:T(8,128)S(1)}, u32[]{:S(2)}, u32[]{:S(2)}) collective-permute-start(f32[48,384]{1,0:T(8,128)S(1)} %collective-permute-done.21.rest_2_), channel_id=1, source_target_pairs={{0,1},{1,0},{2,3},{3,2},{4,5},{5,4},{6,7},{7,6},{8,9},{9,8},{10,11... | collective-permute-start | bytes 221192 | tf_op jit(solution)/shard_map/cond/branch_1_fun/ppermute | solution.py:21
  104.2 5.0 %collective-permute-start.24 = (f32[48,384]{1,0:T(8,128)S(1)}, f32[48,384]{1,0:T(8,128)S(1)}, u32[]{:S(2)}, u32[]{:S(2)}) collective-permute-start(f32[48,384]{1,0:T(8,128)S(1)} %collective-permute-done.20.rest_1_), channel_id=1, source_target_pairs={{0,1},{1,0},{2,3},{3,2},{4,5},{5,4},{6,7},{7,6},{8,9},{9,8},{10,11... | collective-permute-start | bytes 221192 | tf_op jit(solution)/shard_map/cond/branch_1_fun/ppermute | solution.py:21
  104.3 5.0 %copy-start.1 = (bf16[1024,384]{1,0:T(8,128)(2,1)S(1)}, bf16[1024,384]{1,0:T(8,128)(2,1)}, u32[]{:S(2)}) copy-start(bf16[1024,384]{1,0:T(8,128)(2,1)} %get-tuple-element.184.face_lows) | copy-start | bytes 2359300 | tf_op jit(solution)/shard_map/cond
  110.4 1.1 %copy-start.4 = (f32[1024,1,384]{2,1,0:T(1,128)}, f32[1024,1,384]{2,1,0:T(1,128)S(1)}, u32[]{:S(2)}) copy-start(f32[1024,1,384]{2,1,0:T(1,128)S(1)} %get-tuple-element.499) | copy-start | bytes 4718596

commit v3 on v2

--- a/solution.py
+++ b/solution.py
@@ -180,7 +180,7 @@
 IN_SMEM = pl.BlockSpec(memory_space=pltpu.SMEM)
 SLOTS = (1, 2, 4)
 WHOLE_SLOTS = 4
-STEP = 512
+STEP = 1024
 SPARE_BYTES = 2 << 20
 
 
@@ -259,8 +259,10 @@
             yield r, (chunks - r) * LANES, chunks - r
 
 
-def own_kernel(rows, chunks, own, keep, send, top, low, acc, cross, packed):
-    x, _, _, _, _ = spots()
+def own_kernel(rows, chunks, own, keep, send, far, top, low, acc, cross, packed):
+    x, _, side, _, _ = spots()
+    count = far.shape[0]
+    far[...] = own[pl.ds(pl.multiple_of(side * count, 8), count), :]
     unpack(own, rows, chunks, top, low)
     cross[...] = dot_tn(top[...], low[...])
     acc[...] = dot_tn(top[...], top[...]) + (cross[...] + cross[...].T)
@@ -582,8 +584,9 @@
     twin = across(own, 0, 1)
     split = [(rows, virt, bf16)] * 2
     mixed_rows, packed = virt // 2, packed_rows(chunks)
-    keep_a, send_a, own_top, own_low = call(
-        functools.partial(own_kernel, rows, chunks), [(packed // 2, virt)] * 2 + split, [own],
+    keep_a, send_a, far_send, own_top, own_low = call(
+        functools.partial(own_kernel, rows, chunks),
+        [(packed // 2, virt)] * 2 + [(half * chunks, LANES)] + split, [own],
         scratch=[((virt, virt), f32)] * 2 + [((packed, virt), f32)], flops=block_flops)
     got_a = across(send_a, 1, 0)
     twin, send_a = lax.optimization_barrier((twin, send_a))
@@ -600,9 +603,6 @@
     occ_side = jnp.where(lane == 0, occ_side, occ_side[::-1])
     occ_other = across(occ_side, 0, 2)
     occ = (occ_side, occ_other)
-    later_own, _ = lax.optimization_barrier((own, send_b))
-    far_send = pick(later_own.reshape(2, half * chunks, LANES), side)
-    keep_a, branch, far_send = lax.optimization_barrier((keep_a, branch, far_send))
     piece_rows = (packed + mixed_rows) // 2 // z_count
     *pieces, vir_row, vir_col = call(
         x_add_kernel,

time: 113 us -> 113 us (level)
  transfers between devices with their start and end apart: 31 -> 31, of which waited for: 15 -> 15; matrix products, arithmetic and copies ran while one was open for 4% -> 3% of each run, Pallas kernels for 13% -> 13%
where the time goes in v3:
time: 113 us; the launch traced here: 111 us
  waiting for transfers between devices  54.6 us (48%)
  starting transfers between devices  32.6 us (29%)
  Pallas kernels  15.7 us (14%)
  between operations  2.87 us (3%)
  local copies, waits for them, and re-layouts  2.47 us (2%)
  other arithmetic  2.19 us (2%)
    ppermute x31, waiting for transfers between devices, across(): return lax.ppermute(value, AXES, moves)  54.6 us
    ppermute x31, starting transfers between devices, across(): return lax.ppermute(value, AXES, moves)  32.6 us
    pallas_call x10, Pallas kernels, call(): pl.pallas_call(kernel, out_shape=outs, in_specs=[IN_SMEM if i in in_smem...  15.7 us
  transfers between devices with their start and end apart: 31, of which 15 were waited for; matrix products, arithmetic and copies ran while one was open for 3% of the time, Pallas kernels for 13%

profile of v3, /device:TPU:0, one launch (start us, length us, event | category | flops | bytes accessed | tf_op | source)
XLA Modules:
  0.0 111.1 jit_solution(2202895645553491594)
XLA Ops:
  0.0 0.5 collective-permute-start.70
  0.5 1.2 %dynamic-slice_bitcast_fusion = f32[1536,128]{1,0:T(8,128)S(1)} fusion(f32[2,1536,128]{2,1,0:T(8,128)} %bitcast.9, s32[]{:T(128)S(6)} %select_n.24), kind=kLoop, calls=%fused_computation | loop fusion | bytes 1572868 | tf_op jit(solution)/shard_map/jit(dynamic_index_in_dim)/squeeze | solution.py:25
  1.7 0.0 copy-start.22
  1.7 0.0 copy-start.21
  1.7 2.7 %collective-permute-start.71 = (f32[1536,128]{1,0:T(8,128)S(1)}, f32[1536,128]{1,0:T(8,128)S(1)}, u32[]{:S(2)}, u32[]{:S(2)}) collective-permute-start(f32[1536,128]{1,0:T(8,128)S(1)} %dynamic-slice_bitcast_fusion), channel_id=1, source_target_pairs={{0,2},{1,3},{2,0},{3,1},{4,6},{5,7},{6,4},{7,5},{8,10},{9,11},{10,... | collective-permute-start | bytes 2359304 | tf_op jit(solution)/shard_map/ppermute | solution.py:21
  4.4 18.1 %collective-permute-done.71.face = f32[1536,128]{1,0:T(8,128)S(1)} collective-permute-done((f32[1536,128]{1,0:T(8,128)S(1)}, f32[1536,128]{1,0:T(8,128)S(1)}, u32[]{:S(2)}, u32[]{:S(2)}) %collective-permute-start.71) | collective-permute-done | bytes 786464 | tf_op jit(solution)/shard_map/ppermute | solution.py:21
  22.5 0.0 collective-permute-start.72
  22.5 1.7 %shard_map.50 = (f32[128,384]{1,0:T(8,128)S(1)}, f32[128,384]{1,0:T(8,128)S(1)}, f32[1536,128]{1,0:T(8,128)}, bf16[1024,384]{1,0:T(8,128)(2,1)}, bf16[1024,384]{1,0:T(8,128)(2,1)}) custom-call(f32[3072,128]{1,0:T(8,128)S(1)} %bitcast.10), custom_call_target="tpu_custom_call" | custom-call | flops 905969664 | bytes 4325376 | tf_op jit(solution)/shard_map/pallas_call | solution.py:211
  24.2 1.7 %collective-permute-start.69 = (f32[128,384]{1,0:T(8,128)S(1)}, f32[128,384]{1,0:T(8,128)S(1)}, u32[]{:S(2)}, u32[]{:S(2)}) collective-permute-start(f32[128,384]{1,0:T(8,128)S(1)} %get-tuple-element.293), channel_id=1, source_target_pairs={{0,4},{1,5},{2,6},{3,7},{4,0},{5,1},{6,2},{7,3},{8,12},{9,13},{10,... | collective-permute-start | bytes 589832 | tf_op jit(solution)/shard_map/ppermute | solution.py:21
  26.6 4.9 %collective-permute-done.69.refs_1_ = f32[128,384]{1,0:T(8,128)S(1)} collective-permute-done((f32[128,384]{1,0:T(8,128)S(1)}, f32[128,384]{1,0:T(8,128)S(1)}, u32[]{:S(2)}, u32[]{:S(2)}) %collective-permute-start.69) | collective-permute-done | bytes 196640 | tf_op jit(solution)/shard_map/ppermute | solution.py:21
  31.5 0.8 fusion
  34.4 3.2 %shard_map.51 = (f32[96,384]{1,0:T(8,128)S(1)}, f32[96,384]{1,0:T(8,128)S(1)}, bf16[1024,384]{1,0:T(8,128)(2,1)S(1)}, bf16[1024,384]{1,0:T(8,128)(2,1)S(1)}) custom-call(bf16[1024,384]{1,0:T(8,128)(2,1)} %get-tuple-element.334.own_top, bf16[1024,384]{1,0:T(8,128)(2,1)} %get-tuple-element.335.own_low, f32[3072,128]{1,0:T(8,128)} %collective-permute-done.70.twin), custom_call_target="tpu_custom_call" | custom-call | flops 905969664 | bytes 5013504 | tf_op jit(solution)/shard_map/pallas_call | solution.py:211
  37.6 1.8 %collective-permute-start.75 = (f32[96,384]{1,0:T(8,128)S(1)}, f32[96,384]{1,0:T(8,128)S(1)}, u32[]{:S(2)}, u32[]{:S(2)}) collective-permute-start(f32[96,384]{1,0:T(8,128)S(1)} %get-tuple-element.303), channel_id=1, source_target_pairs={{0,4},{1,5},{2,6},{3,7},{4,0},{5,1},{6,2},{7,3},{8,12},{9,13},{10,... | collective-permute-start | bytes 442376 | tf_op jit(solution)/shard_map/ppermute | solution.py:21
  39.4 0.0 collective-permute-start.73
  39.4 0.0 collective-permute-done.72.face_twin
  39.4 3.6 %shard_map.52 = (f32[48,384]{1,0:T(8,128)S(1)}, f32[48,384]{1,0:T(8,128)}, f32[48,384]{1,0:T(8,128)}, f32[48,384]{1,0:T(8,128)}, f32[96,384]{1,0:T(8,128)}, /*in...) custom-call(s32[4,4]{1,0:T(4,128)S(1)} %copy-done.21, ...), custom_call_target="tpu_custom_call" | custom-call | flops 905969664 | bytes 8355904 | tf_op jit(solution)/shard_map/pallas_call | solution.py:211
  43.0 0.7 pad_maximum_fusion
  43.7 0.1 rev.3
  43.8 0.1 shard_map.53
  44.0 1.6 %collective-permute-start.76 = (f32[56,384]{1,0:T(8,128)S(1)}, f32[56,384]{1,0:T(8,128)S(1)}, u32[]{:S(2)}, u32[]{:S(2)}) collective-permute-start(f32[56,384]{1,0:T(8,128)S(1)} %get-tuple-element.309), channel_id=1, source_target_pairs={{0,8},{1,9},{2,10},{3,11},{4,12},{5,13},{6,14},{7,15},{8,0},{9,1},... | collective-permute-start | bytes 258056 | tf_op jit(solution)/shard_map/ppermute | solution.py:21
  45.6 2.6 %collective-permute-start.77 = (f32[56,384]{1,0:T(8,128)S(1)}, f32[56,384]{1,0:T(8,128)S(1)}, u32[]{:S(2)}, u32[]{:S(2)}) collective-permute-start(f32[56,384]{1,0:T(8,128)S(1)} %get-tuple-element.310), channel_id=1, source_target_pairs={{0,16},{1,17},{2,18},{3,19},{4,20},{5,21},{6,22},{7,23},{8,24},{9,... | collective-permute-start | bytes 258056 | tf_op jit(solution)/shard_map/ppermute | solution.py:21
  48.2 0.2 collective-permute-start.78
  48.4 0.7 broadcast_select_fusion
  49.1 1.5 %collective-permute-start.74 = (f32[2]{0:T(128)S(1)}, f32[2]{0:T(128)S(1)}, u32[]{:S(2)}, u32[]{:S(2)}) collective-permute-start(f32[2]{0:T(128)S(1)} %broadcast_select_fusion), channel_id=1, source_target_pairs={{0,2},{1,3},{2,0},{3,1},{4,6},{5,7},{6,4},{7,5},{8,10},{9,11},{10,... | collective-permute-start | bytes 32 | tf_op jit(solution)/shard_map/ppermute | solution.py:21
  50.7 2.0 %collective-permute-done.74 = f32[2]{0:T(128)S(1)} collective-permute-done((f32[2]{0:T(128)S(1)}, f32[2]{0:T(128)S(1)}, u32[]{:S(2)}, u32[]{:S(2)}) %collective-permute-start.74) | collective-permute-done | bytes 40 | tf_op jit(solution)/shard_map/ppermute | solution.py:21
  52.7 2.8 %collective-permute-done.77 = f32[56,384]{1,0:T(8,128)S(1)} collective-permute-done((f32[56,384]{1,0:T(8,128)S(1)}, f32[56,384]{1,0:T(8,128)S(1)}, u32[]{:S(2)}, u32[]{:S(2)}) %collective-permute-start.77) | collective-permute-done | bytes 86048 | tf_op jit(solution)/shard_map/ppermute | solution.py:21
  55.5 54.5 %conditional.1 = (f32[1024,1,384]{2,1,0:T(1,128)S(1)}) conditional(s32[]{:T(128)} %clamp.3, (s32[4,4]{1,0:T(4,128)S(1)}, f32[2]{0:T(128)S(1)}, f32[2]{0:T(128)S(1)}, f32[1,768]{1,0:T(1,128)S(1)}, f32[384,128]{1,0:T(8,128)S(1)}, /*index=5*/f32[56,384]{1,0:T(8,128)S(1)}, f32[56,384]{1,0:T(8,128)S(1)}, ...), branch_computations={%region_1.2_spmd, %region_2.3_spmd, %region_3.4_spmd, %region_4.5_... | conditional | flops 3623878656 | bytes 64875736 | solution.py:721
  55.5 0.9 collective-permute-start.12
  56.4 1.5 %collective-permute-start.13 = (f32[48,384]{1,0:T(8,128)}, f32[48,384]{1,0:T(8,128)S(1)}, u32[]{:S(2)}, u32[]{:S(2)}) collective-permute-start(f32[48,384]{1,0:T(8,128)} %get-tuple-element.188), channel_id=1, source_target_pairs={{0,2},{1,3},{2,0},{3,1},{4,6},{5,7},{6,4},{7,5},{8,10},{9,11},{10,... | collective-permute-start | bytes 221192 | tf_op jit(solution)/shard_map/cond/branch_1_fun/ppermute | solution.py:21
  57.9 1.1 %collective-permute-start.14 = (f32[48,384]{1,0:T(8,128)}, f32[48,384]{1,0:T(8,128)S(1)}, u32[]{:S(2)}, u32[]{:S(2)}) collective-permute-start(f32[48,384]{1,0:T(8,128)} %get-tuple-element.189), channel_id=1, source_target_pairs={{0,6},{1,7},{2,4},{3,5},{4,2},{5,3},{6,0},{7,1},{8,14},{9,15},{10,... | collective-permute-start | bytes 221192 | tf_op jit(solution)/shard_map/cond/branch_1_fun/ppermute | solution.py:21
  59.0 1.1 collective-permute-done.12.refs_1_
  60.1 0.8 collective-permute-done.13.refs_2_
  61.0 2.5 %collective-permute-done.14.refs_3_ = f32[48,384]{1,0:T(8,128)S(1)} collective-permute-done((f32[48,384]{1,0:T(8,128)}, f32[48,384]{1,0:T(8,128)S(1)}, u32[]{:S(2)}, u32[]{:S(2)}) %collective-permute-start.14) | collective-permute-done | bytes 73760 | tf_op jit(solution)/shard_map/cond/branch_1_fun/ppermute | solution.py:21
  63.5 0.6 collective-permute-start.15
  64.0 0.7 branch_1_fun.6.refs_0_
  64.7 2.5 %collective-permute-start.8 = (f32[56,384]{1,0:T(8,128)S(1)}, f32[56,384]{1,0:T(8,128)S(1)}, u32[]{:S(2)}, u32[]{:S(2)}) collective-permute-start(f32[56,384]{1,0:T(8,128)S(1)} %branch_1_fun.6.refs_0_), channel_id=1, source_target_pairs={{0,24},{1,25},{2,26},{3,27},{4,28},{5,29},{6,30},{7,31},{8,16},{9,... | collective-permute-start | bytes 258056 | tf_op jit(solution)/shard_map/cond/branch_1_fun/ppermute | solution.py:21
  67.2 0.4 collective-permute-start.7
  67.7 1.5 %collective-permute-start.6 = (f32[56,384]{1,0:T(8,128)S(1)}, f32[56,384]{1,0:T(8,128)S(1)}, u32[]{:S(2)}, u32[]{:S(2)}) collective-permute-start(f32[56,384]{1,0:T(8,128)S(1)} %branch_1_fun.6.refs_0_), channel_id=1, source_target_pairs={{0,8},{1,9},{2,10},{3,11},{4,12},{5,13},{6,14},{7,15},{8,0},{9,1},... | collective-permute-start | bytes 258056 | tf_op jit(solution)/shard_map/cond/branch_1_fun/ppermute | solution.py:21
  69.2 1.9 %collective-permute-done.8.refs_3_ = f32[56,384]{1,0:T(8,128)S(1)} collective-permute-done((f32[56,384]{1,0:T(8,128)S(1)}, f32[56,384]{1,0:T(8,128)S(1)}, u32[]{:S(2)}, u32[]{:S(2)}) %collective-permute-start.8) | collective-permute-done | bytes 86048 | tf_op jit(solution)/shard_map/cond/branch_1_fun/ppermute | solution.py:21
  71.1 2.4 %collective-permute-done.7.refs_2_ = f32[56,384]{1,0:T(8,128)S(1)} collective-permute-done((f32[56,384]{1,0:T(8,128)S(1)}, f32[56,384]{1,0:T(8,128)S(1)}, u32[]{:S(2)}, u32[]{:S(2)}) %collective-permute-start.7) | collective-permute-done | bytes 86048 | tf_op jit(solution)/shard_map/cond/branch_1_fun/ppermute | solution.py:21
  73.5 0.0 collective-permute-done.6.refs_1_
  73.5 1.5 %collective-permute-start.9 = (f32[224,384]{1,0:T(8,128)S(1)}, f32[224,384]{1,0:T(8,128)S(1)}, u32[]{:S(2)}, u32[]{:S(2)}) collective-permute-start(f32[224,384]{1,0:T(8,128)S(1)} %branch_1_fun.7.keep), channel_id=1, source_target_pairs={{0,4},{1,5},{2,6},{3,7},{4,0},{5,1},{6,2},{7,3},{8,12},{9,13},{10,... | collective-permute-start | bytes 1032200 | tf_op jit(solution)/shard_map/cond/branch_1_fun/ppermute | solution.py:21
  75.0 5.2 %collective-permute-done.15.far = f32[1536,128]{1,0:T(8,128)S(1)} collective-permute-done((f32[1536,128]{1,0:T(8,128)}, f32[1536,128]{1,0:T(8,128)S(1)}, u32[]{:S(2)}, u32[]{:S(2)}) %collective-permute-start.15) | collective-permute-done | bytes 786464 | tf_op jit(solution)/shard_map/cond/branch_1_fun/ppermute | solution.py:21
  80.2 0.0 collective-permute-start.16
  80.2 0.5 collective-permute-start.10
  80.7 0.1 collective-permute-done.9.other
  80.8 0.0 collective-permute-start.11
  80.8 3.2 %collective-permute-start.18 = (f32[48,384]{1,0:T(8,128)S(1)}, f32[48,384]{1,0:T(8,128)S(1)}, u32[]{:S(2)}, u32[]{:S(2)}) collective-permute-start(f32[48,384]{1,0:T(8,128)S(1)} %branch_1_fun.9.refs_0_), channel_id=1, source_target_pairs={{0,16},{1,17},{2,18},{3,19},{4,20},{5,21},{6,22},{7,23},{8,24},{9,... | collective-permute-start | bytes 221192 | tf_op jit(solution)/shard_map/cond/branch_1_fun/ppermute | solution.py:21
  84.1 4.3 %collective-permute-done.18.refs_2_ = f32[48,384]{1,0:T(8,128)S(1)} collective-permute-done((f32[48,384]{1,0:T(8,128)S(1)}, f32[48,384]{1,0:T(8,128)S(1)}, u32[]{:S(2)}, u32[]{:S(2)}) %collective-permute-start.18) | collective-permute-done | bytes 73760 | tf_op jit(solution)/shard_map/cond/branch_1_fun/ppermute | solution.py:21
  88.3 1.1 collective-permute-start.19
  89.4 0.0 collective-permute-done.17.refs_1_
  89.4 3.3 %collective-permute-done.19.refs_3_ = f32[48,384]{1,0:T(8,128)S(1)} collective-permute-done((f32[48,384]{1,0:T(8,128)S(1)}, f32[48,384]{1,0:T(8,128)S(1)}, u32[]{:S(2)}, u32[]{:S(2)}) %collective-permute-start.19) | collective-permute-done | bytes 73760 | tf_op jit(solution)/shard_map/cond/branch_1_fun/ppermute | solution.py:21
  92.7 0.7 branch_1_fun.10.rest_0_
  93.4 2.2 %collective-permute-start.22 = (f32[48,384]{1,0:T(8,128)S(1)}, f32[48,384]{1,0:T(8,128)S(1)}, u32[]{:S(2)}, u32[]{:S(2)}) collective-permute-start(f32[48,384]{1,0:T(8,128)S(1)} %branch_1_fun.10.rest_0_), channel_id=1, source_target_pairs={{0,6},{1,7},{2,4},{3,5},{4,2},{5,3},{6,0},{7,1},{8,14},{9,15},{10,... | collective-permute-start | bytes 221192 | tf_op jit(solution)/shard_map/cond/branch_1_fun/ppermute | solution.py:21
  95.6 0.8 collective-permute-start.21
  96.4 2.3 %collective-permute-done.22.rest_3_ = f32[48,384]{1,0:T(8,128)S(1)} collective-permute-done((f32[48,384]{1,0:T(8,128)S(1)}, f32[48,384]{1,0:T(8,128)S(1)}, u32[]{:S(2)}, u32[]{:S(2)}) %collective-permute-start.22) | collective-permute-done | bytes 73760 | tf_op jit(solution)/shard_map/cond/branch_1_fun/ppermute | solution.py:21
  98.7 1.5 %collective-permute-start.20 = (f32[48,384]{1,0:T(8,128)S(1)}, f32[48,384]{1,0:T(8,128)S(1)}, u32[]{:S(2)}, u32[]{:S(2)}) collective-permute-start(f32[48,384]{1,0:T(8,128)S(1)} %branch_1_fun.10.rest_0_), channel_id=1, source_target_pairs={{0,4},{1,5},{2,6},{3,7},{4,0},{5,1},{6,2},{7,3},{8,12},{9,13},{10,... | collective-permute-start | bytes 221192 | tf_op jit(solution)/shard_map/cond/branch_1_fun/ppermute | solution.py:21
  100.2 2.8 %collective-permute-done.20.rest_1_ = f32[48,384]{1,0:T(8,128)S(1)} collective-permute-done((f32[48,384]{1,0:T(8,128)S(1)}, f32[48,384]{1,0:T(8,128)S(1)}, u32[]{:S(2)}, u32[]{:S(2)}) %collective-permute-start.20) | collective-permute-done | bytes 73760 | tf_op jit(solution)/shard_map/cond/branch_1_fun/ppermute | solution.py:21
  103.0 0.5 collective-permute-start.25
  103.5 0.1 collective-permute-start.24
  103.6 4.8 %branch_1_fun.8.base = f32[1024,384]{1,0:T(8,128)S(1)} custom-call(bf16[1024,384]{1,0:T(8,128)(2,1)S(1)} %copy-done.9, bf16[1024,384]{1,0:T(8,128)(2,1)S(1)} %copy-done.13, bf16[1024,384]{1,0:T(8,128)(2,1)} %get-tuple-element.173.twin_top, bf16[1024,384]{1,0:T(8,128)(2,1)} %get-tuple-element.174.twin_low, f32[224,384]{1,0:T(8,128)S(1)} %branch_1_fun.7.keep, ...), custom_call_target="tpu_custom_call" | custom-call | flops 1811939328 | bytes 6094848 | tf_op jit(solution)/shard_map/cond/branch_1_fun/pallas_call | solution.py:211
  108.5 0.9 branch_1_fun.11
  109.9 0.0 copy-start.7
  109.9 1.1 %copy-done.7 = f32[1024,1,384]{2,1,0:T(1,128)} copy-done((f32[1024,1,384]{2,1,0:T(1,128)}, f32[1024,1,384]{2,1,0:T(1,128)S(1)}, u32[]{:S(2)}) %copy-start.7) | copy-done | bytes 1572888
  (39 shorter events, 0.1 us)
Async XLA Ops:
  0.0 22.5 %copy-start = (f32[1024,1,384]{2,1,0:T(1,128)S(1)}, f32[1024,1,384]{2,1,0:T(1,128)}, u32[]{:S(2)}) copy-start(f32[1024,1,384]{2,1,0:T(1,128)} %param.8) | copy-start | bytes 4718596
  0.0 34.4 %collective-permute-start.70 = (f32[3072,128]{1,0:T(8,128)}, f32[3072,128]{1,0:T(8,128)}, u32[]{:S(2)}, u32[]{:S(2)}) collective-permute-start(f32[3072,128]{1,0:T(8,128)} %bitcast.8), channel_id=1, source_target_pairs={{0,1},{1,0},{2,3},{3,2},{4,5},{5,4},{6,7},{7,6},{8,9},{9,8},{10,11... | collective-permute-start | bytes 4718600 | tf_op jit(solution)/shard_map/ppermute | solution.py:21
  1.7 24.9 %copy-start.22 = (f32[384]{0:T(512)S(1)}, f32[384]{0:T(512)}, u32[]{:S(2)}) copy-start(f32[384]{0:T(512)} %param.10) | copy-start | bytes 4612
  1.7 29.8 %copy-start.21 = (s32[4,4]{1,0:T(4,128)S(1)}, s32[4,4]{1,0:T(4,128)}, u32[]{:S(2)}) copy-start(s32[4,4]{1,0:T(4,128)} %mask.1) | copy-start | bytes 196
  1.7 20.8 %collective-permute-start.71 = (f32[1536,128]{1,0:T(8,128)S(1)}, f32[1536,128]{1,0:T(8,128)S(1)}, u32[]{:S(2)}, u32[]{:S(2)}) collective-permute-start(f32[1536,128]{1,0:T(8,128)S(1)} %dynamic-slice_bitcast_fusion), channel_id=1, source_target_pairs={{0,2},{1,3},{2,0},{3,1},{4,6},{5,7},{6,4},{7,5},{8,10},{9,11},{10,... | collective-permute-start | bytes 2359304 | tf_op jit(solution)/shard_map/ppermute | solution.py:21
  22.5 16.9 %collective-permute-start.72 = (f32[1536,128]{1,0:T(8,128)S(1)}, f32[1536,128]{1,0:T(8,128)S(1)}, u32[]{:S(2)}, u32[]{:S(2)}) collective-permute-start(f32[1536,128]{1,0:T(8,128)S(1)} %collective-permute-done.71.face), channel_id=1, source_target_pairs={{0,1},{1,0},{2,3},{3,2},{4,5},{5,4},{6,7},{7,6},{8,9},{9,8},{10,11... | collective-permute-start | bytes 2359304 | tf_op jit(solution)/shard_map/ppermute | solution.py:21
  24.2 7.3 %collective-permute-start.69 = (f32[128,384]{1,0:T(8,128)S(1)}, f32[128,384]{1,0:T(8,128)S(1)}, u32[]{:S(2)}, u32[]{:S(2)}) collective-permute-start(f32[128,384]{1,0:T(8,128)S(1)} %get-tuple-element.293), channel_id=1, source_target_pairs={{0,4},{1,5},{2,6},{3,7},{4,0},{5,1},{6,2},{7,3},{8,12},{9,13},{10,... | collective-permute-start | bytes 589832 | tf_op jit(solution)/shard_map/ppermute | solution.py:21
  34.4 5.0 %copy-start.8 = (bf16[1024,384]{1,0:T(8,128)(2,1)S(1)}, bf16[1024,384]{1,0:T(8,128)(2,1)}, u32[]{:S(2)}) copy-start(bf16[1024,384]{1,0:T(8,128)(2,1)} %get-tuple-element.334.own_top) | copy-start | bytes 2359300
  34.4 5.0 %copy-start.12 = (bf16[1024,384]{1,0:T(8,128)(2,1)S(1)}, bf16[1024,384]{1,0:T(8,128)(2,1)}, u32[]{:S(2)}) copy-start(bf16[1024,384]{1,0:T(8,128)(2,1)} %get-tuple-element.335.own_low) | copy-start | bytes 2359300
  37.6 5.4 %copy-start.16 = (bf16[1024,384]{1,0:T(8,128)(2,1)}, bf16[1024,384]{1,0:T(8,128)(2,1)S(1)}, u32[]{:S(2)}) copy-start(bf16[1024,384]{1,0:T(8,128)(2,1)S(1)} %get-tuple-element.336.twin_top) | copy-start | bytes 2359300
  37.6 5.4 %copy-start.19 = (bf16[1024,384]{1,0:T(8,128)(2,1)}, bf16[1024,384]{1,0:T(8,128)(2,1)S(1)}, u32[]{:S(2)}) copy-start(bf16[1024,384]{1,0:T(8,128)(2,1)S(1)} %get-tuple-element.337.twin_low) | copy-start | bytes 2359300
  37.6 6.2 %collective-permute-start.75 = (f32[96,384]{1,0:T(8,128)S(1)}, f32[96,384]{1,0:T(8,128)S(1)}, u32[]{:S(2)}, u32[]{:S(2)}) collective-permute-start(f32[96,384]{1,0:T(8,128)S(1)} %get-tuple-element.303), channel_id=1, source_target_pairs={{0,4},{1,5},{2,6},{3,7},{4,0},{5,1},{6,2},{7,3},{8,12},{9,13},{10,... | collective-permute-start | bytes 442376 | tf_op jit(solution)/shard_map/ppermute | solution.py:21
  39.4 3.6 %collective-permute-start.73 = (f32[1]{0:T(128)}, f32[1]{0:T(128)}, u32[]{:S(2)}, u32[]{:S(2)}) collective-permute-start(f32[1]{0:T(128)} %param.9), channel_id=1, source_target_pairs={{0,1},{1,0},{2,3},{3,2},{4,5},{5,4},{6,7},{7,6},{8,9},{9,8},{10,11... | collective-permute-start | bytes 20 | tf_op jit(solution)/shard_map/ppermute | solution.py:21
  44.0 8.7 %collective-permute-start.76 = (f32[56,384]{1,0:T(8,128)S(1)}, f32[56,384]{1,0:T(8,128)S(1)}, u32[]{:S(2)}, u32[]{:S(2)}) collective-permute-start(f32[56,384]{1,0:T(8,128)S(1)} %get-tuple-element.309), channel_id=1, source_target_pairs={{0,8},{1,9},{2,10},{3,11},{4,12},{5,13},{6,14},{7,15},{8,0},{9,1},... | collective-permute-start | bytes 258056 | tf_op jit(solution)/shard_map/ppermute | solution.py:21
  45.6 9.8 %collective-permute-start.77 = (f32[56,384]{1,0:T(8,128)S(1)}, f32[56,384]{1,0:T(8,128)S(1)}, u32[]{:S(2)}, u32[]{:S(2)}) collective-permute-start(f32[56,384]{1,0:T(8,128)S(1)} %get-tuple-element.310), channel_id=1, source_target_pairs={{0,16},{1,17},{2,18},{3,19},{4,20},{5,21},{6,22},{7,23},{8,24},{9,... | collective-permute-start | bytes 258056 | tf_op jit(solution)/shard_map/ppermute | solution.py:21
  48.2 7.3 %collective-permute-start.78 = (f32[56,384]{1,0:T(8,128)S(1)}, f32[56,384]{1,0:T(8,128)S(1)}, u32[]{:S(2)}, u32[]{:S(2)}) collective-permute-start(f32[56,384]{1,0:T(8,128)S(1)} %get-tuple-element.311), channel_id=1, source_target_pairs={{0,24},{1,25},{2,26},{3,27},{4,28},{5,29},{6,30},{7,31},{8,16},{9,... | collective-permute-start | bytes 258056 | tf_op jit(solution)/shard_map/ppermute | solution.py:21
  49.1 3.6 %collective-permute-start.74 = (f32[2]{0:T(128)S(1)}, f32[2]{0:T(128)S(1)}, u32[]{:S(2)}, u32[]{:S(2)}) collective-permute-start(f32[2]{0:T(128)S(1)} %broadcast_select_fusion), channel_id=1, source_target_pairs={{0,2},{1,3},{2,0},{3,1},{4,6},{5,7},{6,4},{7,5},{8,10},{9,11},{10,... | collective-permute-start | bytes 32 | tf_op jit(solution)/shard_map/ppermute | solution.py:21
  55.5 48.1 %copy-start.9 = (bf16[1024,384]{1,0:T(8,128)(2,1)S(1)}, bf16[1024,384]{1,0:T(8,128)(2,1)}, u32[]{:S(2)}) copy-start(bf16[1024,384]{1,0:T(8,128)(2,1)} %get-tuple-element.171.own_top) | copy-start | bytes 2359300 | tf_op jit(solution)/shard_map/cond
  55.5 48.1 %copy-start.13 = (bf16[1024,384]{1,0:T(8,128)(2,1)S(1)}, bf16[1024,384]{1,0:T(8,128)(2,1)}, u32[]{:S(2)}) copy-start(bf16[1024,384]{1,0:T(8,128)(2,1)} %get-tuple-element.172.own_low) | copy-start | bytes 2359300 | tf_op jit(solution)/shard_map/cond
  55.5 4.6 %collective-permute-start.12 = (f32[48,384]{1,0:T(8,128)}, f32[48,384]{1,0:T(8,128)S(1)}, u32[]{:S(2)}, u32[]{:S(2)}) collective-permute-start(f32[48,384]{1,0:T(8,128)} %get-tuple-element.187), channel_id=1, source_target_pairs={{0,4},{1,5},{2,6},{3,7},{4,0},{5,1},{6,2},{7,3},{8,12},{9,13},{10,... | collective-permute-start | bytes 221192 | tf_op jit(solution)/shard_map/cond/branch_1_fun/ppermute | solution.py:21
  56.4 4.6 %collective-permute-start.13 = (f32[48,384]{1,0:T(8,128)}, f32[48,384]{1,0:T(8,128)S(1)}, u32[]{:S(2)}, u32[]{:S(2)}) collective-permute-start(f32[48,384]{1,0:T(8,128)} %get-tuple-element.188), channel_id=1, source_target_pairs={{0,2},{1,3},{2,0},{3,1},{4,6},{5,7},{6,4},{7,5},{8,10},{9,11},{10,... | collective-permute-start | bytes 221192 | tf_op jit(solution)/shard_map/cond/branch_1_fun/ppermute | solution.py:21
  57.9 5.5 %collective-permute-start.14 = (f32[48,384]{1,0:T(8,128)}, f32[48,384]{1,0:T(8,128)S(1)}, u32[]{:S(2)}, u32[]{:S(2)}) collective-permute-start(f32[48,384]{1,0:T(8,128)} %get-tuple-element.189), channel_id=1, source_target_pairs={{0,6},{1,7},{2,4},{3,5},{4,2},{5,3},{6,0},{7,1},{8,14},{9,15},{10,... | collective-permute-start | bytes 221192 | tf_op jit(solution)/shard_map/cond/branch_1_fun/ppermute | solution.py:21
  63.5 16.8 %collective-permute-start.15 = (f32[1536,128]{1,0:T(8,128)}, f32[1536,128]{1,0:T(8,128)S(1)}, u32[]{:S(2)}, u32[]{:S(2)}) collective-permute-start(f32[1536,128]{1,0:T(8,128)} %get-tuple-element.190), channel_id=1, source_target_pairs={{0,2},{1,3},{2,0},{3,1},{4,6},{5,7},{6,4},{7,5},{8,10},{9,11},{10,... | collective-permute-start | bytes 2359304 | tf_op jit(solution)/shard_map/cond/branch_1_fun/ppermute | solution.py:21
  64.7 6.4 %collective-permute-start.8 = (f32[56,384]{1,0:T(8,128)S(1)}, f32[56,384]{1,0:T(8,128)S(1)}, u32[]{:S(2)}, u32[]{:S(2)}) collective-permute-start(f32[56,384]{1,0:T(8,128)S(1)} %branch_1_fun.6.refs_0_), channel_id=1, source_target_pairs={{0,24},{1,25},{2,26},{3,27},{4,28},{5,29},{6,30},{7,31},{8,16},{9,... | collective-permute-start | bytes 258056 | tf_op jit(solution)/shard_map/cond/branch_1_fun/ppermute | solution.py:21
  67.2 6.2 %collective-permute-start.7 = (f32[56,384]{1,0:T(8,128)S(1)}, f32[56,384]{1,0:T(8,128)S(1)}, u32[]{:S(2)}, u32[]{:S(2)}) collective-permute-start(f32[56,384]{1,0:T(8,128)S(1)} %branch_1_fun.6.refs_0_), channel_id=1, source_target_pairs={{0,16},{1,17},{2,18},{3,19},{4,20},{5,21},{6,22},{7,23},{8,24},{9,... | collective-permute-start | bytes 258056 | tf_op jit(solution)/shard_map/cond/branch_1_fun/ppermute | solution.py:21
  67.7 5.8 %collective-permute-start.6 = (f32[56,384]{1,0:T(8,128)S(1)}, f32[56,384]{1,0:T(8,128)S(1)}, u32[]{:S(2)}, u32[]{:S(2)}) collective-permute-start(f32[56,384]{1,0:T(8,128)S(1)} %branch_1_fun.6.refs_0_), channel_id=1, source_target_pairs={{0,8},{1,9},{2,10},{3,11},{4,12},{5,13},{6,14},{7,15},{8,0},{9,1},... | collective-permute-start | bytes 258056 | tf_op jit(solution)/shard_map/cond/branch_1_fun/ppermute | solution.py:21
  73.5 7.3 %collective-permute-start.9 = (f32[224,384]{1,0:T(8,128)S(1)}, f32[224,384]{1,0:T(8,128)S(1)}, u32[]{:S(2)}, u32[]{:S(2)}) collective-permute-start(f32[224,384]{1,0:T(8,128)S(1)} %branch_1_fun.7.keep), channel_id=1, source_target_pairs={{0,4},{1,5},{2,6},{3,7},{4,0},{5,1},{6,2},{7,3},{8,12},{9,13},{10,... | collective-permute-start | bytes 1032200 | tf_op jit(solution)/shard_map/cond/branch_1_fun/ppermute | solution.py:21
  80.2 28.3 %collective-permute-start.16 = (f32[1536,128]{1,0:T(8,128)S(1)}, f32[1536,128]{1,0:T(8,128)S(1)}, u32[]{:S(2)}, u32[]{:S(2)}) collective-permute-start(f32[1536,128]{1,0:T(8,128)S(1)} %collective-permute-done.15.far), channel_id=1, source_target_pairs={{0,1},{1,0},{2,3},{3,2},{4,5},{5,4},{6,7},{7,6},{8,9},{9,8},{10,11... | collective-permute-start | bytes 2359304 | tf_op jit(solution)/shard_map/cond/branch_1_fun/ppermute | solution.py:21
  80.2 22.8 %collective-permute-start.10 = (f32[224,384]{1,0:T(8,128)S(1)}, f32[224,384]{1,0:T(8,128)S(1)}, u32[]{:S(2)}, u32[]{:S(2)}) collective-permute-start(f32[224,384]{1,0:T(8,128)S(1)} %branch_1_fun.7.keep), channel_id=1, source_target_pairs={{0,1},{1,0},{2,3},{3,2},{4,5},{5,4},{6,7},{7,6},{8,9},{9,8},{10,11... | collective-permute-start | bytes 1032200 | tf_op jit(solution)/shard_map/cond/branch_1_fun/ppermute | solution.py:21
  80.8 22.7 %collective-permute-start.11 = (f32[224,384]{1,0:T(8,128)S(1)}, f32[224,384]{1,0:T(8,128)S(1)}, u32[]{:S(2)}, u32[]{:S(2)}) collective-permute-start(f32[224,384]{1,0:T(8,128)S(1)} %collective-permute-done.9.other), channel_id=1, source_target_pairs={{0,1},{1,0},{2,3},{3,2},{4,5},{5,4},{6,7},{7,6},{8,9},{9,8},{10,11... | collective-permute-start | bytes 1032200 | tf_op jit(solution)/shard_map/cond/branch_1_fun/ppermute | solution.py:21
  80.8 7.5 %collective-permute-start.18 = (f32[48,384]{1,0:T(8,128)S(1)}, f32[48,384]{1,0:T(8,128)S(1)}, u32[]{:S(2)}, u32[]{:S(2)}) collective-permute-start(f32[48,384]{1,0:T(8,128)S(1)} %branch_1_fun.9.refs_0_), channel_id=1, source_target_pairs={{0,16},{1,17},{2,18},{3,19},{4,20},{5,21},{6,22},{7,23},{8,24},{9,... | collective-permute-start | bytes 221192 | tf_op jit(solution)/shard_map/cond/branch_1_fun/ppermute | solution.py:21
  84.1 5.3 %collective-permute-start.17 = (f32[48,384]{1,0:T(8,128)S(1)}, f32[48,384]{1,0:T(8,128)S(1)}, u32[]{:S(2)}, u32[]{:S(2)}) collective-permute-start(f32[48,384]{1,0:T(8,128)S(1)} %branch_1_fun.9.refs_0_), channel_id=1, source_target_pairs={{0,8},{1,9},{2,10},{3,11},{4,12},{5,13},{6,14},{7,15},{8,0},{9,1},... | collective-permute-start | bytes 221192 | tf_op jit(solution)/shard_map/cond/branch_1_fun/ppermute | solution.py:21
  88.3 4.4 %collective-permute-start.19 = (f32[48,384]{1,0:T(8,128)S(1)}, f32[48,384]{1,0:T(8,128)S(1)}, u32[]{:S(2)}, u32[]{:S(2)}) collective-permute-start(f32[48,384]{1,0:T(8,128)S(1)} %collective-permute-done.18.refs_2_), channel_id=1, source_target_pairs={{0,8},{1,9},{2,10},{3,11},{4,12},{5,13},{6,14},{7,15},{8,0},{9,1},... | collective-permute-start | bytes 221192 | tf_op jit(solution)/shard_map/cond/branch_1_fun/ppermute | solution.py:21
  93.4 5.3 %collective-permute-start.22 = (f32[48,384]{1,0:T(8,128)S(1)}, f32[48,384]{1,0:T(8,128)S(1)}, u32[]{:S(2)}, u32[]{:S(2)}) collective-permute-start(f32[48,384]{1,0:T(8,128)S(1)} %branch_1_fun.10.rest_0_), channel_id=1, source_target_pairs={{0,6},{1,7},{2,4},{3,5},{4,2},{5,3},{6,0},{7,1},{8,14},{9,15},{10,... | collective-permute-start | bytes 221192 | tf_op jit(solution)/shard_map/cond/branch_1_fun/ppermute | solution.py:21
  95.6 4.7 %collective-permute-start.21 = (f32[48,384]{1,0:T(8,128)S(1)}, f32[48,384]{1,0:T(8,128)S(1)}, u32[]{:S(2)}, u32[]{:S(2)}) collective-permute-start(f32[48,384]{1,0:T(8,128)S(1)} %branch_1_fun.10.rest_0_), channel_id=1, source_target_pairs={{0,2},{1,3},{2,0},{3,1},{4,6},{5,7},{6,4},{7,5},{8,10},{9,11},{10,... | collective-permute-start | bytes 221192 | tf_op jit(solution)/shard_map/cond/branch_1_fun/ppermute | solution.py:21
  98.7 4.4 %collective-permute-start.20 = (f32[48,384]{1,0:T(8,128)S(1)}, f32[48,384]{1,0:T(8,128)S(1)}, u32[]{:S(2)}, u32[]{:S(2)}) collective-permute-start(f32[48,384]{1,0:T(8,128)S(1)} %branch_1_fun.10.rest_0_), channel_id=1, source_target_pairs={{0,4},{1,5},{2,6},{3,7},{4,0},{5,1},{6,2},{7,3},{8,12},{9,13},{10,... | collective-permute-start | bytes 221192 | tf_op jit(solution)/shard_map/cond/branch_1_fun/ppermute | solution.py:21
  100.2 8.2 %collective-permute-start.23 = (f32[48,384]{1,0:T(8,128)S(1)}, f32[48,384]{1,0:T(8,128)S(1)}, u32[]{:S(2)}, u32[]{:S(2)}) collective-permute-start(f32[48,384]{1,0:T(8,128)S(1)} %branch_1_fun.10.rest_0_), channel_id=1, source_target_pairs={{0,1},{1,0},{2,3},{3,2},{4,5},{5,4},{6,7},{7,6},{8,9},{9,8},{10,11... | collective-permute-start | bytes 221192 | tf_op jit(solution)/shard_map/cond/branch_1_fun/ppermute | solution.py:21
  103.0 5.4 %collective-permute-start.26 = (f32[48,384]{1,0:T(8,128)S(1)}, f32[48,384]{1,0:T(8,128)S(1)}, u32[]{:S(2)}, u32[]{:S(2)}) collective-permute-start(f32[48,384]{1,0:T(8,128)S(1)} %collective-permute-done.22.rest_3_), channel_id=1, source_target_pairs={{0,1},{1,0},{2,3},{3,2},{4,5},{5,4},{6,7},{7,6},{8,9},{9,8},{10,11... | collective-permute-start | bytes 221192 | tf_op jit(solution)/shard_map/cond/branch_1_fun/ppermute | solution.py:21
  103.0 5.4 %collective-permute-start.25 = (f32[48,384]{1,0:T(8,128)S(1)}, f32[48,384]{1,0:T(8,128)S(1)}, u32[]{:S(2)}, u32[]{:S(2)}) collective-permute-start(f32[48,384]{1,0:T(8,128)S(1)} %collective-permute-done.21.rest_2_), channel_id=1, source_target_pairs={{0,1},{1,0},{2,3},{3,2},{4,5},{5,4},{6,7},{7,6},{8,9},{9,8},{10,11... | collective-permute-start | bytes 221192 | tf_op jit(solution)/shard_map/cond/branch_1_fun/ppermute | solution.py:21
  103.5 4.9 %collective-permute-start.24 = (f32[48,384]{1,0:T(8,128)S(1)}, f32[48,384]{1,0:T(8,128)S(1)}, u32[]{:S(2)}, u32[]{:S(2)}) collective-permute-start(f32[48,384]{1,0:T(8,128)S(1)} %collective-permute-done.20.rest_1_), channel_id=1, source_target_pairs={{0,1},{1,0},{2,3},{3,2},{4,5},{5,4},{6,7},{7,6},{8,9},{9,8},{10,11... | collective-permute-start | bytes 221192 | tf_op jit(solution)/shard_map/cond/branch_1_fun/ppermute | solution.py:21
  103.6 4.9 %copy-start.1 = (bf16[1024,384]{1,0:T(8,128)(2,1)S(1)}, bf16[1024,384]{1,0:T(8,128)(2,1)}, u32[]{:S(2)}) copy-start(bf16[1024,384]{1,0:T(8,128)(2,1)} %get-tuple-element.183.face_tops) | copy-start | bytes 2359300 | tf_op jit(solution)/shard_map/cond
  103.6 4.9 %copy-start.4 = (bf16[1024,384]{1,0:T(8,128)(2,1)S(1)}, bf16[1024,384]{1,0:T(8,128)(2,1)}, u32[]{:S(2)}) copy-start(bf16[1024,384]{1,0:T(8,128)(2,1)} %get-tuple-element.184.face_lows) | copy-start | bytes 2359300 | tf_op jit(solution)/shard_map/cond
  109.9 1.1 %copy-start.7 = (f32[1024,1,384]{2,1,0:T(1,128)}, f32[1024,1,384]{2,1,0:T(1,128)S(1)}, u32[]{:S(2)}) copy-start(f32[1024,1,384]{2,1,0:T(1,128)S(1)} %get-tuple-element.496) | copy-start | bytes 4718596
